TPU v7x, 128 devices: a whole 4x4x4 slice. The times are simulated.
128 devices in a mesh: grp: 4 (over z), tile: 32 (over y, x, core).
Axes of the slice: x: 4, y: 4, z: 4, core: 2. Of those that a mesh axis runs over, the one named last changes fastest.
Arguments:
- right_side: float32 [16, 32768], P(None, ('grp', 'tile')), may hold values from -6 to 6
- ridge: float32 [32768], P(('grp', 'tile')), may hold values from 1 to 4
- tiles: float32 [512, 1024, 1024], P(('grp', 'tile')), may hold values from -0.013671875 to 0.013671875
- tile_list: int32 [512, 2], P(('grp', 'tile')), may hold values from 0 to 31, as said below
Outputs:
- solution: float32 [16, 32768], P(None, ('grp', 'tile'))
- residual: float32 [16, 32768], P(None, ('grp', 'tile'))
Inputs may be any that keep to these rules, and one draw needn't show every extreme that they name: `tile_list`: each row is a pair (row block, column block) with row block >= column block; no pair appears twice; rows stand in packed row-major order (row block rising, then column block rising).
All inputs are finite; a program needn't handle non-finite values.
Results may differ from a plain program's by a relative error of at most 0.0003.
Values sent between devices are 32-bit elements; how exact they have to be, the bound alone decides.
No kernel may reach another device: no remote copies, remote signals or barrier semaphores. Data moves between devices by JAX's collectives and lax.ppermute only.
A program may use at most 64 MiB of HBM per device.

v0:
```python
import jax
import jax.numpy as jnp
from jax import lax
from jax.sharding import PartitionSpec as P

ITERS = 2


def gauss_solve(matrix, rhs):
    order = matrix.shape[0]
    for pivot in range(order):
        scale = 1.0 / matrix[pivot, pivot]
        row_new = matrix[pivot] * scale
        rhs_new = rhs[pivot] * scale
        factor = matrix[:, pivot] * (1.0 - (jnp.arange(order) == pivot).astype(matrix.dtype))
        matrix = matrix - factor[:, None] * row_new[None, :]
        rhs = rhs - factor[:, None] * rhs_new[None, :]
        matrix = matrix.at[pivot].set(row_new)
        rhs = rhs.at[pivot].set(rhs_new)
    return rhs


def gram(left, right):
    return lax.dot_general(
        left,
        right,
        (((1,), (1,)), ((), ())),
        precision=lax.Precision.HIGHEST,
        preferred_element_type=jnp.float32,
    )


def mixed(coeffs, rows):
    return jnp.dot(coeffs.T, rows, precision=lax.Precision.HIGHEST)


def tile_masks(order):
    rowid = lax.broadcasted_iota(jnp.int32, (order, order), 0)
    colid = lax.broadcasted_iota(jnp.int32, (order, order), 1)
    return (rowid >= colid, rowid > colid)


def apply_kernel(tiles, tile_list, field):
    order = tiles.shape[1]
    lower, strict = tile_masks(order)

    def step(total, item):
        tile, pair = item
        block_row = pair[0]
        block_col = pair[1]
        differ = block_row != block_col
        direct_tile = jnp.where(jnp.logical_or(lower, differ), tile, jnp.zeros_like(tile))
        mirror_tile = jnp.where(jnp.logical_or(strict, differ), tile, jnp.zeros_like(tile))
        row_start = block_row * order
        col_start = block_col * order
        from_col = lax.dynamic_slice_in_dim(field, col_start, order, 1)
        from_row = lax.dynamic_slice_in_dim(field, row_start, order, 1)
        into_row = lax.dot_general(
            from_col,
            direct_tile,
            (((1,), (1,)), ((), ())),
            precision=lax.Precision.HIGHEST,
            preferred_element_type=jnp.float32,
        )
        into_col = jnp.dot(
            from_row,
            mirror_tile,
            precision=lax.Precision.HIGHEST,
            preferred_element_type=jnp.float32,
        )
        total = lax.dynamic_update_slice_in_dim(
            total, lax.dynamic_slice_in_dim(total, row_start, order, 1) + into_row, row_start, 1
        )
        total = lax.dynamic_update_slice_in_dim(
            total, lax.dynamic_slice_in_dim(total, col_start, order, 1) + into_col, col_start, 1
        )
        return (total, None)

    start = jnp.zeros(field.shape, jnp.float32)
    total, _ = lax.scan(step, start, (tiles, tile_list))
    return total


def local(right_side, ridge, tiles, tile_list):
    solution = jnp.zeros_like(right_side)
    residual = right_side
    direction = right_side
    norm_now = lax.psum(gram(residual, residual), ("grp", "tile"))
    for step in range(ITERS):
        whole_direction = lax.all_gather(direction, ("grp", "tile"), axis=1, tiled=True)
        partial_image = apply_kernel(tiles, tile_list, whole_direction)
        image = (
            lax.psum_scatter(partial_image, ("grp", "tile"), scatter_dimension=1, tiled=True)
            + ridge[None, :] * direction
        )
        curvature = lax.psum(gram(direction, image), ("grp", "tile"))
        alpha = gauss_solve(curvature, norm_now)
        solution = solution + mixed(alpha, direction)
        residual = residual - mixed(alpha, image)
        if step + 1 < ITERS:
            norm_next = lax.psum(gram(residual, residual), ("grp", "tile"))
            beta = gauss_solve(norm_now, norm_next)
            direction = residual + mixed(beta, direction)
            norm_now = norm_next
    return (solution, residual)


def solution(mesh):
    return jax.shard_map(
        local,
        mesh=mesh,
        in_specs=(
            P(None, ("grp", "tile")),
            P(("grp", "tile")),
            P(("grp", "tile"), None, None),
            P(("grp", "tile"), None),
        ),
        out_specs=(P(None, ("grp", "tile")), P(None, ("grp", "tile"))),
        check_vma=False,
    )
```

profile of v0, /device:TPU:1, one launch (start us, length us, event | category | flops | bytes accessed | tf_op | source)
XLA Modules:
  0.0 1806.4 jit_solution(17161838119397110656)
XLA Ops:
  7.9 71.4 %all-gather.3.cloned.1.call-done = f32[16,32768]{1,0:T(8,128)} async-done(((f32[16,256]{1,0:T(8,128)}), f32[16,32768]{1,0:T(8,128)}) %all-gather.3.cloned.1.call-update) | async-done | bytes 2097168 | tf_op jit(solution)/shard_map/all_gather | solution.py:90
  79.5 55.9 %while.115 = (s32[]{:T(128)}, f32[16,32768]{1,0:T(8,128)S(1)}, s32[4,2]{0,1:T(2,128)}, f32[16,32768]{1,0:T(8,128)}, f32[4,1024,1024]{2,1,0:T(8,128)}, /*index=5*/s32[]{:T(128)}, s32[1,1]{0,1:T(1,128)}, s32[]{:T(128)}, s32[]{:T(128)}) while((s32[]{:T(128)}, f32[16,32768]{1,0:T(8,128)S(1)}, s32[4,2]{0,1:T(2,128)}, ...), condition=%wide.region_2.3_spmd.clone, body=%wide.region_1.2_spmd.clone.sunk | while | flops 408977408 | bytes 8784118 | solution.py:80
  83.4 5.6 fusion.227
  89.0 4.5 fusion.228
  97.3 5.6 fusion.227
  103.0 4.5 fusion.228
  111.3 5.6 fusion.227
  116.9 4.5 fusion.228
  125.3 5.6 fusion.227
  130.9 4.5 fusion.228
  135.4 1.3 copy-done.1
  137.0 630.1 %reduce-scatter.3.cloned.1.call-done = f32[16,256]{1,0:T(8,128)} async-done(((f32[16,32768]{1,0:T(8,128)}), f32[16,256]{1,0:T(8,128)}) %reduce-scatter.3.cloned.1.call-update) | async-done | bytes 16400 | tf_op jit(solution)/shard_map/reduce_scatter | solution.py:93
  767.0 0.9 convolution_bitcast_fusion
  767.9 69.3 %all-reduce = (f32[16,16]{1,0:T(8,128)S(1)}, f32[16,16]{1,0:T(8,128)S(1)}) all-reduce(f32[16,16]{1,0:T(8,128)S(1)} %fusion.107, f32[16,16]{1,0:T(8,128)S(1)} %convolution_bitcast_fusion), channel_id=1, replica_groups=mesh['grp'=4,'tile'=32] {'grp','tile'}, use_global_device_ids=true, to_apply=%region_0.0 | all-reduce | flops 512 | bytes 4096 | tf_op jit(solution)/shard_map/psum | solution.py:88
  864.5 0.9 convolution_subtract_fusion.1
  865.5 62.7 %psum.30 = f32[16,16]{1,0:T(8,128)S(1)} all-reduce(f32[16,16]{1,0:T(8,128)S(1)} %fusion.109), channel_id=1, replica_groups=mesh['grp'=4,'tile'=32] {'grp','tile'}, use_global_device_ids=true, to_apply=%region_5.6 | all-reduce | flops 256 | bytes 2048 | tf_op jit(solution)/shard_map/psum | solution.py:101
  953.1 0.8 convolution_add_fusion.1
  954.0 62.6 %all-gather.5.cloned.1.call-done = f32[16,32768]{1,0:T(8,128)} async-done(((f32[16,256]{1,0:T(8,128)}), f32[16,32768]{1,0:T(8,128)}) %all-gather.5.cloned.1.call-update) | async-done | bytes 2097168 | tf_op jit(solution)/shard_map/all_gather | solution.py:90
  1016.8 52.9 %while.116 = (s32[]{:T(128)}, f32[16,32768]{1,0:T(8,128)S(1)}, s32[4,2]{0,1:T(2,128)S(1)}, f32[16,32768]{1,0:T(8,128)}, f32[4,1024,1024]{2,1,0:T(8,128)}, /*inde...) while((s32[]{:T(128)}, f32[16,32768]{1,0:T(8,128)S(1)}, s32[4,2]{0,1:T(2,128)S(1)}, ...), condition=%wide.region_7.8_spmd.clone, body=%wide.region_6.7_spmd.clone.sunk | while | flops 408977408 | bytes 8784118 | solution.py:80
  1019.9 5.6 fusion.232
  1025.5 4.5 fusion.233
  1033.1 5.6 fusion.232
  1038.7 4.5 fusion.233
  1046.3 5.6 fusion.232
  1052.0 4.5 fusion.233
  1059.6 5.6 fusion.232
  1065.2 4.5 fusion.233
  1069.7 1.3 copy-done
  1071.3 630.1 %reduce-scatter.5.cloned.1.call-done = f32[16,256]{1,0:T(8,128)} async-done(((f32[16,32768]{1,0:T(8,128)}), f32[16,256]{1,0:T(8,128)}) %reduce-scatter.5.cloned.1.call-update) | async-done | bytes 16400 | tf_op jit(solution)/shard_map/reduce_scatter | solution.py:93
  1701.4 0.8 fusion.52
  1702.2 69.2 %psum.31 = f32[16,16]{1,0:T(8,128)S(1)} all-reduce(f32[16,16]{1,0:T(8,128)S(1)} %fusion.52), channel_id=1, replica_groups=mesh['grp'=4,'tile'=32] {'grp','tile'}, use_global_device_ids=true, to_apply=%region_9.10 | all-reduce | flops 256 | bytes 2048 | tf_op jit(solution)/shard_map/psum | solution.py:96
  1798.4 1.5 convolution_subtract_fusion
  (457 shorter events, 54.0 us)
Async XLA Ops:
  7.2 72.2 %all-gather.3.cloned.1.call-start = ((), (), s32[]{:S(2)}) async-start(), calls=%async_computation.2 | async-start | bytes 2113536 | tf_op jit(solution)/shard_map/all_gather | solution.py:90
  7.9 759.1 %reduce-scatter.3.cloned.1.call-start = ((), (), s32[]{:S(2)}) async-start(), calls=%async_computation.3 | async-start | bytes 2113536 | tf_op jit(solution)/shard_map/reduce_scatter | solution.py:93
  79.5 57.3 %copy-start.2 = (f32[16,256]{1,0:T(8,128)S(1)}, f32[16,256]{1,0:T(8,128)}, u32[]{:S(2)}) copy-start(f32[16,256]{1,0:T(8,128)} %param.194) | copy-start | bytes 49156
  79.5 687.5 %copy-start.5 = (f32[256]{0:T(256)S(1)}, f32[256]{0:T(256)}, u32[]{:S(2)}) copy-start(f32[256]{0:T(256)} %param.195) | copy-start | bytes 3076
  135.4 1.4 copy-start.1
  135.4 881.3 %copy-start.4 = (s32[4,2]{0,1:T(2,128)S(1)}, s32[4,2]{0,1:T(2,128)}, u32[]{:S(2)}) copy-start(s32[4,2]{0,1:T(2,128)} %get-tuple-element.1476) | copy-start | bytes 100
  136.8 879.8 %all-gather.5.cloned.1.call-start = ((), (), s32[]{:S(2)}) async-start(), calls=%async_computation.4 | async-start | bytes 2113536 | tf_op jit(solution)/shard_map/all_gather | solution.py:90
  953.9 747.5 %reduce-scatter.5.cloned.1.call-start = ((), (), s32[]{:S(2)}) async-start(), calls=%async_computation.5 | async-start | bytes 2113536 | tf_op jit(solution)/shard_map/reduce_scatter | solution.py:93
  1016.8 684.6 %copy-start.3 = (f32[16,256]{1,0:T(8,128)S(1)}, f32[16,256]{1,0:T(8,128)}, u32[]{:S(2)}) copy-start(f32[16,256]{1,0:T(8,128)} %convolution_add_fusion.1) | copy-start | bytes 49156
  1069.7 1.4 copy-start
Sparse Core Ops, SparseCore 0:
  10.8 68.4 all-gather.2
  136.9 630.0 reduce-scatter.2
  954.1 62.5 all-gather.4
  1071.2 630.1 reduce-scatter.4
where the time goes:
time: 1810 us
  waiting for transfers between devices  1390 us (77%)
  blocking collectives  201 us (11%)
  matrix products  87.4 us (5%)
  between operations  48.2 us (3%)
  local copies, waits for them, and re-layouts  41.3 us (2%)
  loops' own time  20 us (1%)
    reduce_scatter x2, waiting for transfers between devices, local(): lax.psum_scatter(partial_image, ('grp', 'tile'), scatter_dimension=1, til...  1260 us
    all_gather x2, waiting for transfers between devices, local(): lax.all_gather(direction, ('grp', 'tile'), axis=1, tiled=True)  134 us
    psum x1, blocking collectives, local(): norm_now = lax.psum(gram(residual, residual), ('grp', 'tile'))  69.3 us
    psum x1, blocking collectives, local(): curvature = lax.psum(gram(direction, image), ('grp', 'tile'))  69.2 us
    psum x1, blocking collectives, local(): norm_next = lax.psum(gram(residual, residual), ('grp', 'tile'))  62.7 us
    dot_general x8, matrix products, step(): lax.dot_general(from_col, direct_tile, (((1,), (1,)), ((), ())), precisio...  45.1 us
  transfers between devices with their start and end apart: 4, of which 4 were waited for; matrix products, arithmetic and copies ran while one was open for 0% of the time, Pallas kernels for 0%

commit v1 on v0

v1 whole, which is shorter than its diff:
```python
import functools

import jax
import jax.numpy as jnp
from jax import lax
from jax.experimental import pallas as pl
from jax.experimental.pallas import tpu as pltpu
from jax.sharding import PartitionSpec as P

AXES = ("grp", "tile")
S = 16
B = 1024
NB = 32
D = 128
J = 8
ENDS = 8
R1_ROWS = 12
R2_ROWS = 14
F32 = jnp.float32
BF16 = jnp.bfloat16


def iota(shape, dim):
    return lax.broadcasted_iota(jnp.int32, shape, dim)


def exact(left, right):
    return jnp.dot(left, right, precision=lax.Precision.HIGHEST, preferred_element_type=F32)


def same_column():
    return (iota((D, D), 0) % S == iota((D, D), 1) % S).astype(F32)


def spread_sum(x):
    return exact(x, same_column())


def own_lanes():
    return iota((S, D), 1) // S == iota((S, D), 0) % 8


def flat_rows(g):
    kept = jnp.where(own_lanes(), g, 0.0)
    return jnp.concatenate(
        [jnp.sum(kept[:8], axis=0, keepdims=True), jnp.sum(kept[8:], axis=0, keepdims=True)], axis=0
    )


def from_rows(rows):
    top = jnp.broadcast_to(rows[0:1], (8, D))
    low = jnp.broadcast_to(rows[1:2], (8, D))
    return spread_sum(jnp.where(own_lanes(), jnp.concatenate([top, low], axis=0), 0.0))


def stack8(g):
    return jnp.concatenate([g] * 8, axis=0)


def block_diag(g):
    keep = iota((D, D), 0) // S == iota((D, D), 1) // S
    return jnp.where(keep, stack8(g), 0.0)


def small_mul(left, right):
    return exact(jnp.where(iota((S, D), 1) < S, left, 0.0), stack8(right))


def small_t(g):
    return stack8(g).T[:S]


def owner_gram(left, right):
    both = exact(left.T, right)
    keep = iota((D, D), 0) // S == iota((D, D), 1) // S
    kept = jnp.where(keep, both, 0.0)
    total = kept[0:S]
    for j in range(1, J):
        total = total + kept[j * S : (j + 1) * S]
    return spread_sum(total)


def gauss_solve(matrix, rhs):
    lane = iota((S, D), 1)
    row = iota((S, D), 0)
    work = jnp.where(lane < S, matrix, rhs)
    for pivot in range(S):
        row_new = work[pivot : pivot + 1] * (1.0 / work[pivot : pivot + 1, pivot : pivot + 1])
        factor = jnp.where(row == pivot, 0.0, work[:, pivot : pivot + 1])
        work = jnp.where(row == pivot, row_new, work - factor * row_new)
    return spread_sum(jnp.where((lane >= S) & (lane < 2 * S), work, 0.0))


def pack_kernel(right_ref, ridge_ref, list_ref, out_ref, gram_ref):
    right = right_ref[...]
    ridge = ridge_ref[...]
    rows = [right[:, :D], right[:, D:]]
    rows += [jnp.broadcast_to(ridge[j : j + 1], (S, D)) for j in range(2)]
    rows += [jnp.broadcast_to(list_ref[...], (ENDS, D)), jnp.zeros((D - 4 * S - ENDS, D), F32)]
    out_ref[...] = jnp.concatenate(rows, axis=0).T
    scaled = jnp.concatenate([right[:, :D] * ridge[0:1], right[:, D:] * ridge[1:2]], axis=1)
    nt = (((1,), (1,)), ((), ()))
    tall = jnp.concatenate([right] * 8, axis=0)
    gram_ref[0] = lax.dot_general(
        right, tall, nt, precision=lax.Precision.HIGHEST, preferred_element_type=F32
    )
    gram_ref[1] = lax.dot_general(
        scaled, tall, nt, precision=lax.Precision.HIGHEST, preferred_element_type=F32
    )


def end_matches(ends, k):
    return (ends[:, k : k + 1] == iota((D, NB), 1).astype(F32)).astype(F32)


def send_ends(ends, field, out_ref):
    for k in range(ENDS):
        out_ref[:, k, :] = exact(end_matches(ends, k), field)


def take_ends(ends, got_ref, rows):
    total = jnp.zeros((NB, D), F32)
    for k in range(ENDS):
        part = got_ref[pl.ds(k, D, stride=rows), :]
        total = total + exact(end_matches(ends, k).T, part)
    return total


def take_gram(got_ref, rows, which):
    first = ENDS + 2 * which
    return from_rows(
        jnp.concatenate(
            [
                jnp.sum(got_ref[pl.ds(first + i, D, stride=rows), :], axis=0, keepdims=True)
                for i in range(2)
            ],
            axis=0,
        )
    )


def owner_first_kernel(got_ref, right_ref, ridge_ref, ends_ref, send_ref):
    for target, lanes in ((right_ref, 0), (ridge_ref, 2 * S)):
        target[...] = jnp.concatenate(
            [got_ref[pl.ds(q, NB, stride=4), :][:, lanes : lanes + 2 * S] for q in range(4)], axis=1
        )
    ends = got_ref[...][:, 4 * S : 4 * S + ENDS]
    ends_ref[...] = ends
    send_ends(ends, right_ref[...], send_ref)


def split(x):
    high = x.astype(BF16)
    return high, (x - high.astype(F32)).astype(BF16)


def matvec_kernel(rows, n_grams, list_ref, got_ref, tiles_ref, grams_ref, out_ref, gram_ref):
    t = pl.program_id(0)
    nt = (((1,), (1,)), ((), ()))
    nn = (((1,), (0,)), ((), ()))

    def field(k):
        turned = got_ref[:, k, :].T
        return jnp.concatenate([turned[j * S : (j + 1) * S] for j in range(J)], axis=1)

    def product(vec, high, low, dims):
        vec_high, vec_low = split(vec)
        both = jnp.concatenate([vec_high, vec_low], axis=0)
        main = lax.dot_general(both, high, dims, preferred_element_type=F32)
        rest = lax.dot_general(vec_high, low, dims, preferred_element_type=F32)
        return main[:S] + (main[S:] + rest)

    def put(k, value):
        tall = jnp.concatenate([value[:, j * D : (j + 1) * D] for j in range(J)], axis=0)
        out_ref[pl.ds(k, D, stride=rows), :] = tall.T

    def finish(k, value, vec):
        put(k, value)
        tall = jnp.concatenate([value] * 8, axis=0)
        gram_ref[...] += lax.dot_general(
            vec, tall, nt, precision=lax.Precision.HIGHEST, preferred_element_type=F32
        )

    @pl.when(t == 0)
    def _():
        gram_ref[...] = grams_ref[n_grams - 1]

    def run(step):
        k = 2 * step
        from_row = field(k)
        from_col = field(k + 1)
        diagonal = list_ref[step, 0] == list_ref[step, 1]

        def emit(tile, extra):
            high, low = split(tile)
            finish(k, product(from_col, high, low, nt), from_row)
            into_col = product(from_row, high, low, nn)
            if extra is not None:
                into_col = into_col - from_row * extra
            finish(k + 1, into_col, from_col)

        @pl.when(diagonal)
        def _():
            tile = tiles_ref[0]
            row, col = iota((B, B), 0), iota((B, B), 1)
            middle = jnp.sum(jnp.where(row == col, tile, 0.0), axis=0, keepdims=True)
            emit(jnp.where(row >= col, tile, 0.0), middle)

        @pl.when(jnp.logical_not(diagonal))
        def _():
            emit(tiles_ref[0], None)

    for step in range(4):
        pl.when(t == step)(functools.partial(run, step))

    @pl.when(t == 3)
    def _():
        for which in range(n_grams):
            gram = gram_ref[...] if which == n_grams - 1 else grams_ref[which]
            flat = flat_rows(gram)
            for i in range(2):
                out_ref[pl.ds(ENDS + 2 * which + i, D, stride=rows), :] = jnp.broadcast_to(
                    flat[i : i + 1], (D, D)
                )


def matvec(got, tiles, tile_list, grams, rows):
    n_grams = (rows - ENDS) // 2
    return pl.pallas_call(
        functools.partial(matvec_kernel, rows, n_grams),
        out_shape=jax.ShapeDtypeStruct((D * rows, D), F32),
        grid_spec=pltpu.PrefetchScalarGridSpec(
            num_scalar_prefetch=1,
            grid=(4,),
            in_specs=[
                pl.BlockSpec((D, ENDS, D), lambda t, ref: (0, 0, 0)),
                pl.BlockSpec((1, B, B), lambda t, ref: (t, 0, 0)),
                pl.BlockSpec((n_grams, S, D), lambda t, ref: (0, 0, 0)),
            ],
            out_specs=pl.BlockSpec((D * rows, D), lambda t, ref: (0, 0)),
            scratch_shapes=[pltpu.VMEM((S, D), F32)],
        ),
        compiler_params=pltpu.CompilerParams(
            dimension_semantics=("arbitrary",), vmem_limit_bytes=56 << 20
        ),
        name="matvec",
    )(tile_list, got, tiles, grams)


def owner_middle_kernel(
    got_ref, ends_ref, right_ref, ridge_ref, send_ref, grams_ref, keep_ref, small_ref
):
    ends = ends_ref[...]
    right = right_ref[...]
    ridge = ridge_ref[...]
    image = take_ends(ends, got_ref, R1_ROWS) + ridge * right
    norm = take_gram(got_ref, R1_ROWS, 0)
    curvature = take_gram(got_ref, R1_ROWS, 1)
    alpha = gauss_solve(curvature, norm)
    residual = right - exact(image, block_diag(alpha))
    send_ends(ends, residual, send_ref)
    grams_ref[0] = owner_gram(residual, residual)
    grams_ref[1] = owner_gram(residual, image)
    grams_ref[2] = owner_gram(residual, ridge * residual)
    keep_ref[0] = residual
    keep_ref[1] = image
    small_ref[0] = norm
    small_ref[1] = curvature
    small_ref[2] = alpha


def owner_last_kernel(
    got_ref, ends_ref, right_ref, ridge_ref, keep_ref, small_ref, out_ref, bend_ref
):
    right = right_ref[...]
    residual = keep_ref[0]
    image = keep_ref[1]
    norm, curvature, alpha = small_ref[0], small_ref[1], small_ref[2]
    second = take_ends(ends_ref[...], got_ref, R2_ROWS) + ridge_ref[...] * residual
    norm_next = take_gram(got_ref, R2_ROWS, 0)
    cross = take_gram(got_ref, R2_ROWS, 1)
    bend_ref[...] = take_gram(got_ref, R2_ROWS, 2)
    beta = gauss_solve(norm, norm_next)
    mixed = small_mul(cross, beta)
    bent = bend_ref[...] + mixed + small_t(mixed) + small_mul(small_t(beta), small_mul(curvature, beta))
    last = gauss_solve(bent, norm_next)
    beta_wide = block_diag(beta)
    last_wide = block_diag(last)
    direction = residual + exact(right, beta_wide)
    image_next = second + exact(image, beta_wide)
    solution = exact(right, block_diag(alpha)) + exact(direction, last_wide)
    residual = residual - exact(image_next, last_wide)
    for q in range(4):
        lanes = slice(q * 2 * S, (q + 1) * 2 * S)
        row = jnp.concatenate(
            [solution[:, lanes], residual[:, lanes], jnp.zeros((NB, D - 4 * S), F32)], axis=1
        )
        out_ref[pl.ds(q, NB, stride=4), :] = row


def unpack_kernel(got_ref, solution_ref, residual_ref):
    turned = got_ref[...].T
    for j in range(2):
        solution_ref[:, j * D : (j + 1) * D] = turned[j * S : (j + 1) * S]
        residual_ref[:, j * D : (j + 1) * D] = turned[(2 + j) * S : (3 + j) * S]


def call(kernel, name, shapes, *args, scratch=()):
    return pl.pallas_call(
        kernel,
        out_shape=[jax.ShapeDtypeStruct(shape, F32) for shape in shapes],
        scratch_shapes=[pltpu.VMEM(shape, F32) for shape in scratch],
        compiler_params=pltpu.CompilerParams(vmem_limit_bytes=32 << 20),
        name=name,
    )(*args)


def exchange(x):
    return lax.all_to_all(x, AXES, 0, 0)


def exchange_rows(x, rows):
    return exchange(x.reshape(D, 1, rows * D)).reshape(D * rows, D)


def local(right_side, ridge, tiles, tile_list):
    ends_own = tile_list.reshape(ENDS, 1).astype(F32)
    packed, own_grams = call(
        pack_kernel, "pack", [(D, D), (2, S, D)], right_side, ridge.reshape(2, D), ends_own
    )
    got = exchange_rows(packed, 1)
    right, ridge_wide, ends, send = call(
        owner_first_kernel,
        "owner_first",
        [(NB, D), (NB, D), (D, ENDS), (D, ENDS, D)],
        got,
    )
    got = exchange(send)
    sent = matvec(got, tiles, tile_list, own_grams, R1_ROWS)
    got = exchange_rows(sent, R1_ROWS)
    send, grams, keep, small = call(
        owner_middle_kernel,
        "owner_middle",
        [(D, ENDS, D), (3, S, D), (2, NB, D), (3, S, D)],
        got,
        ends,
        right,
        ridge_wide,
    )
    got = exchange(send)
    sent = matvec(got, tiles, tile_list, grams, R2_ROWS)
    got = exchange_rows(sent, R2_ROWS)
    (packed,) = call(
        owner_last_kernel,
        "owner_last",
        [(D, D)],
        got,
        ends,
        right,
        ridge_wide,
        keep,
        small,
        scratch=[(S, D)],
    )
    got = exchange_rows(packed, 1)
    return tuple(call(unpack_kernel, "unpack", [(S, 2 * D), (S, 2 * D)], got))


def solution(mesh):
    return jax.shard_map(
        local,
        mesh=mesh,
        in_specs=(P(None, AXES), P(AXES), P(AXES, None, None), P(AXES, None)),
        out_specs=(P(None, AXES), P(None, AXES)),
        check_vma=False,
    )
```

time: 1810 us -> 167 us (0.09)
  waiting for transfers between devices: 1390 us -> 12.4 us
  blocking collectives: 201 us -> 96.9 us
  matrix products: 87.4 us -> 0 us
  between operations: 48.2 us -> 0.9 us
  Pallas kernels: 0 us -> 45 us
  local copies, waits for them, and re-layouts: 41.3 us -> 4.33 us
  loops' own time: 20 us -> 0 us
    reduce_scatter x2 -> x0, waiting for transfers between devices: 1260 us -> none  [local(): lax.psum_scatter(partial_image, ('grp', 'tile'), scatter_dimension=1, til...]
    psum x3 -> x0, blocking collectives: 201 us -> none  [the longest x1 69.3 us: local(): norm_now = lax.psum(gram(residual, residual), ('grp', 'tile'))]
    all_gather x2 -> x0, waiting for transfers between devices: 134 us -> none  [local(): lax.all_gather(direction, ('grp', 'tile'), axis=1, tiled=True)]
    all_to_all x0 -> x5, blocking collectives: none -> 96.9 us  [exchange(): return lax.all_to_all(x, AXES, 0, 0)]
    dot_general x25 -> x0, matrix products: 87.4 us -> none  [the longest x8 45.1 us: step(): lax.dot_general(from_col, direct_tile, (((1,), (1,)), ((), ())), precisio...]
    pallas_call x0 -> x7, Pallas kernels: none -> 45 us  [the longest x2 34.4 us: matvec(): pl.pallas_call(functools.partial(matvec_kernel, rows, n_grams), out_shape...]
    slice x56 -> x0, local copies, waits for them, and re-layouts: 32.1 us -> none  [the longest x48 27.8 us: gauss_solve(): scale = 1.0 / matrix[pivot, pivot]]
    another operation x2 -> x0, loops' own time: 20 us -> none  [apply_kernel(): total, _ = lax.scan(step, start, (tiles, tile_list))]
  transfers between devices with their start and end apart: 4 -> 1, of which waited for: 4 -> 1; matrix products, arithmetic and copies ran while one was open for 0% -> 1% of each run, Pallas kernels for 0% -> 0%
where the time goes in v1:
time: 167 us; the launch traced here: 165 us
  blocking collectives  96.9 us (58%)
  Pallas kernels  45 us (27%)
  waiting for transfers between devices  12.4 us (7%)
  starting transfers between devices  4.5 us (3%)
  local copies, waits for them, and re-layouts  4.33 us (3%)
    all_to_all x5, blocking collectives, exchange(): return lax.all_to_all(x, AXES, 0, 0)  96.9 us
    pallas_call x2, Pallas kernels, matvec(): pl.pallas_call(functools.partial(matvec_kernel, rows, n_grams), out_shape...  34.4 us
    all_to_all x1, waiting for transfers between devices, exchange(): return lax.all_to_all(x, AXES, 0, 0)  12.4 us
    pallas_call x5, Pallas kernels, call(): pl.pallas_call(kernel, out_shape=[jax.ShapeDtypeStruct(shape, F32) for sh...  10.7 us
    all_to_all x1, starting transfers between devices, exchange(): return lax.all_to_all(x, AXES, 0, 0)  4.5 us
    unnamed x11, local copies, waits for them, and re-layouts  4.16 us
  transfers between devices with their start and end apart: 1, of which 1 were waited for; matrix products, arithmetic and copies ran while one was open for 1% of the time, Pallas kernels for 0%

profile of v1, /device:TPU:1, one launch (start us, length us, event | category | flops | bytes accessed | tf_op | source)
XLA Modules:
  0.0 164.7 jit_solution(12847964818231639712)
XLA Ops:
  0.6 0.7 convert_element_type.5
  1.3 0.1 copy.14
  1.4 0.1 convert_element_type.7.list_ref
  1.5 0.0 copy-start.1
  1.5 0.7 copy-done.1
  2.2 0.0 copy-start.3
  2.2 0.7 copy-done.3
  2.9 0.3 pack.1
  3.2 0.0 copy-start.2
  3.2 0.6 copy-done.2
  3.8 20.9 %all_to_all.30 = f32[128,1,128]{2,1,0:T(1,128)S(1)} all-to-all(f32[128,1,128]{2,1,0:T(1,128)S(1)} %bitcast.18), channel_id=1, replica_groups=mesh['grp'=4,'tile'=32] {'grp','tile'}, dimensions={0} | all-to-all | bytes 131072 | tf_op jit(solution)/shard_map/all_to_all | solution.py:319
  24.7 1.6 owner_first.1
  26.3 4.5 %all-to-all-start.1 = ((f32[128,8,128]{2,1,0:T(8,128)}), f32[128,8,128]{2,1,0:T(8,128)S(1)}, u32[]{:S(2)}, u32[]{:S(2)}) async-start(f32[128,8,128]{2,1,0:T(8,128)} %get-tuple-element.13), calls=%async_computation.1 | async-start | bytes 1048576 | tf_op jit(solution)/shard_map/all_to_all | solution.py:319
  30.8 1.3 copy.19.list_ref
  32.1 12.4 %all-to-all-done.1.got_ref = f32[128,8,128]{2,1,0:T(8,128)S(1)} async-done(((f32[128,8,128]{2,1,0:T(8,128)}), f32[128,8,128]{2,1,0:T(8,128)S(1)}, u32[]{:S(2)}, u32[]{:S(2)}) %all-to-all-start.1) | async-done | bytes 524320 | tf_op jit(solution)/shard_map/all_to_all | solution.py:319
  44.5 0.0 copy-start.4
  44.5 0.8 copy-done.4
  45.3 17.3 %matvec.2 = f32[1536,128]{1,0:T(8,128)} custom-call(s32[4,2]{1,0:T(4,128)} %copy.19.list_ref, f32[128,8,128]{2,1,0:T(8,128)} %copy-done.4, f32[4,1024,1024]{2,1,0:T(8,128)} %tiles_ref.3, f32[2,16,128]{2,1,0:T(8,128)} %copy-done.2), custom_call_target="tpu_custom_call" | custom-call | tf_op jit(solution)/shard_map/matvec/pallas_call | solution.py:229
  62.6 21.3 %all_to_all.31 = f32[128,1,1536]{2,1,0:T(1,128)S(1)} all-to-all(f32[128,1,1536]{2,1,0:T(1,128)} %bitcast.21), channel_id=1, replica_groups=mesh['grp'=4,'tile'=32] {'grp','tile'}, dimensions={0} | all-to-all | bytes 1572864 | tf_op jit(solution)/shard_map/all_to_all | solution.py:319
  83.9 3.7 %owner_middle.1 = (f32[128,8,128]{2,1,0:T(8,128)S(1)}, f32[3,16,128]{2,1,0:T(8,128)S(1)}, f32[2,32,128]{2,1,0:T(8,128)S(1)}, f32[3,16,128]{2,1,0:T(8,128)S(1)}) custom-call(f32[1536,128]{1,0:T(8,128)S(1)} %bitcast.14, f32[128,8]{1,0:T(8,128)S(1)} %get-tuple-element.15.ends_ref, f32[32,128]{1,0:T(8,128)S(1)} %get-tuple-element.16.right_ref, ...), custom_call_target="tpu_custom_call" | custom-call | tf_op jit(solution)/shard_map/owner_middle/pallas_call | solution.py:309
  87.5 0.0 copy-start
  87.5 18.2 %all_to_all.32.got_ref = f32[128,8,128]{2,1,0:T(8,128)} all-to-all(f32[128,8,128]{2,1,0:T(8,128)S(1)} %get-tuple-element.18), channel_id=1, replica_groups=mesh['grp'=4,'tile'=32] {'grp','tile'}, dimensions={0} | all-to-all | bytes 1048576 | tf_op jit(solution)/shard_map/all_to_all | solution.py:319
  105.7 0.0 copy-done
  105.7 17.1 %matvec.3 = f32[1792,128]{1,0:T(8,128)} custom-call(s32[4,2]{1,0:T(4,128)} %copy.19.list_ref, f32[128,8,128]{2,1,0:T(8,128)} %all_to_all.32.got_ref, f32[4,1024,1024]{2,1,0:T(8,128)} %tiles_ref.3, f32[3,16,128]{2,1,0:T(8,128)} %copy-done), custom_call_target="tpu_custom_call" | custom-call | tf_op jit(solution)/shard_map/matvec/pallas_call | solution.py:229
  122.9 22.7 %all_to_all.33 = f32[128,1,1792]{2,1,0:T(1,128)S(1)} all-to-all(f32[128,1,1792]{2,1,0:T(1,128)} %bitcast.20), channel_id=1, replica_groups=mesh['grp'=4,'tile'=32] {'grp','tile'}, dimensions={0} | all-to-all | bytes 1835008 | tf_op jit(solution)/shard_map/all_to_all | solution.py:319
  145.5 4.4 %owner_last.1 = f32[128,128]{1,0:T(8,128)S(1)} custom-call(f32[1792,128]{1,0:T(8,128)S(1)} %bitcast.13, f32[128,8]{1,0:T(8,128)S(1)} %get-tuple-element.15.ends_ref, f32[32,128]{1,0:T(8,128)S(1)} %get-tuple-element.16.right_ref, f32[32,128]{1,0:T(8,128)S(1)} %get-tuple-element.17.ridge_ref, f32[2,32,128]{2,1,0:T(8,128)S(1)} %get-tuple-element.20.keep_ref, ...), custom_call_target="tpu_custom_call" | custom-call | tf_op jit(solution)/shard_map/owner_last/pallas_call | solution.py:309
  150.0 13.8 %all_to_all.34 = f32[128,1,128]{2,1,0:T(1,128)S(1)} all-to-all(f32[128,1,128]{2,1,0:T(1,128)S(1)} %bitcast.15), channel_id=1, replica_groups=mesh['grp'=4,'tile'=32] {'grp','tile'}, dimensions={0} | all-to-all | bytes 131072 | tf_op jit(solution)/shard_map/all_to_all | solution.py:319
  163.8 0.7 unpack.1
Async XLA Ops:
  1.5 0.7 copy-start.1
  2.2 0.7 copy-start.3
  3.2 0.6 copy-start.2
  26.3 18.2 %all-to-all-start.1 = ((f32[128,8,128]{2,1,0:T(8,128)}), f32[128,8,128]{2,1,0:T(8,128)S(1)}, u32[]{:S(2)}, u32[]{:S(2)}) async-start(f32[128,8,128]{2,1,0:T(8,128)} %get-tuple-element.13), calls=%async_computation.1 | async-start | bytes 1048576 | tf_op jit(solution)/shard_map/all_to_all | solution.py:319
  44.5 0.8 copy-start.4
  87.5 18.2 %copy-start = (f32[3,16,128]{2,1,0:T(8,128)}, f32[3,16,128]{2,1,0:T(8,128)S(1)}, u32[]{:S(2)}) copy-start(f32[3,16,128]{2,1,0:T(8,128)S(1)} %get-tuple-element.19.grams_ref) | copy-start | bytes 73732

commit v2 on v0

v2 whole, which is shorter than its diff:
```python
import functools

import jax
import jax.numpy as jnp
from jax import lax
from jax.experimental import pallas as pl
from jax.experimental.pallas import tpu as pltpu
from jax.sharding import PartitionSpec as P

CHIPS = ("grp", "ring")
ALL = ("grp", "ring", "core")
S = 16
B = 1024
NB = 32
D = 128
N = 64
J = 8
ENDS = 8
SLOT = 40
RIDGE, NORM, LIST = 32, 34, 36
GRAMS = 32
R1_ROWS = 10
G2_ROWS = 9
F32 = jnp.float32
BF16 = jnp.bfloat16
PIECE = 256
PIECES = B // PIECE
PART = 512
PARTS = B // PART
NT = (((1,), (1,)), ((), ()))
NN = (((1,), (0,)), ((), ()))


def iota(shape, dim):
    return lax.broadcasted_iota(jnp.int32, shape, dim)


def exact(left, right):
    return jnp.dot(left, right, precision=lax.Precision.HIGHEST, preferred_element_type=F32)


def same_column():
    return (iota((D, D), 0) % S == iota((D, D), 1) % S).astype(F32)


def spread_sum(x):
    return exact(x, same_column())


def own_lanes():
    return iota((S, D), 1) // S == iota((S, D), 0) % 8


def flat_rows(g):
    kept = jnp.where(own_lanes(), g, 0.0)
    return jnp.concatenate(
        [jnp.sum(kept[:8], axis=0, keepdims=True), jnp.sum(kept[8:], axis=0, keepdims=True)], axis=0
    )


def from_rows(rows):
    top = jnp.broadcast_to(rows[0:1], (8, D))
    low = jnp.broadcast_to(rows[1:2], (8, D))
    return spread_sum(jnp.where(own_lanes(), jnp.concatenate([top, low], axis=0), 0.0))


def stack8(g):
    return jnp.concatenate([g] * 8, axis=0)


def small_mul(left, right):
    return exact(jnp.where(iota((S, D), 1) < S, left, 0.0), stack8(right))


def small_t(g):
    return stack8(g).T[:S]


def gram(left, right):
    return lax.dot_general(
        left, right, NT, precision=lax.Precision.HIGHEST, preferred_element_type=F32
    )


def widen(g):
    return jnp.concatenate([g] * 8, axis=1)


def mixed(coeffs, rows):
    return exact(small_t(coeffs)[:, :S], rows)


def gauss_solve(matrix, rhs):
    lane = iota((S, D), 1)
    row = iota((S, D), 0)
    work = jnp.where(lane < S, matrix, rhs)
    for pivot in range(S):
        row_new = work[pivot : pivot + 1] * (1.0 / work[pivot : pivot + 1, pivot : pivot + 1])
        factor = jnp.where(row == pivot, 0.0, work[:, pivot : pivot + 1])
        work = jnp.where(row == pivot, row_new, work - factor * row_new)
    return spread_sum(jnp.where((lane >= S) & (lane < 2 * S), work, 0.0))


def gather_pack_kernel(right_ref, ridge_ref, list_ref, out_ref):
    right = right_ref[...]
    rows = [right[:, :D], right[:, D:], ridge_ref[...], flat_rows(widen(gram(right, right)))]
    slot = iota((1, D), 1)
    ends = jnp.zeros((1, D), F32)
    for k in range(ENDS):
        ends = jnp.where(slot == k, list_ref[k // 2, k % 2].astype(F32), ends)
    rows += [ends, jnp.zeros((SLOT - LIST - 1, D), F32)]
    packed = jnp.concatenate(rows, axis=0)
    for chip in range(N):
        out_ref[chip] = packed


def split(x):
    high = x.astype(BF16)
    return high, (x - high.astype(F32)).astype(BF16)


def stage_kernel(list_ref, tiles_ref, high_ref, low_ref, held, high, low, in_sems, out_sems):
    def fetch(i):
        rows = pl.ds(i % PIECES * PIECE, PIECE)
        return pltpu.make_async_copy(tiles_ref.at[i // PIECES, rows], held.at[i], in_sems.at[i])

    def flush(i):
        rows = pl.ds(i % PIECES * PIECE, PIECE)
        return [
            pltpu.make_async_copy(here.at[i], there.at[i // PIECES, rows], out_sems.at[which, i])
            for which, (here, there) in enumerate(((high, high_ref), (low, low_ref)))
        ]

    for i in range(4 * PIECES):
        fetch(i).start()
    for i in range(4 * PIECES):
        fetch(i).wait()
        tile, first = i // PIECES, i % PIECES * PIECE
        high[i], low[i] = split(held[i])

        @pl.when(list_ref[tile, 0] == list_ref[tile, 1])
        def _():
            row, col = iota((PIECE, B), 0) + first, iota((PIECE, B), 1)
            kept = jnp.where(row > col, held[i], jnp.where(row == col, 0.5 * held[i], 0.0))
            high[i], low[i] = split(kept)

        for copy in flush(i):
            copy.start()
    for i in range(4 * PIECES):
        for copy in flush(i):
            copy.wait()


def stage(tiles, tile_list):
    anywhere = pl.BlockSpec(memory_space=pltpu.HBM)
    return pl.pallas_call(
        stage_kernel,
        out_shape=[pltpu.HBM((4, B, B), BF16)] * 2,
        in_specs=[pl.BlockSpec(memory_space=pltpu.SMEM), anywhere],
        out_specs=[anywhere] * 2,
        scratch_shapes=[
            pltpu.VMEM((4 * PIECES, PIECE, B), F32),
            pltpu.VMEM((4 * PIECES, PIECE, B), BF16),
            pltpu.VMEM((4 * PIECES, PIECE, B), BF16),
            pltpu.SemaphoreType.DMA((4 * PIECES,)),
            pltpu.SemaphoreType.DMA((2, 4 * PIECES)),
        ],
        compiler_params=pltpu.CompilerParams(vmem_limit_bytes=40 << 20),
        name="stage",
    )(tile_list, tiles)


def by_core(mine, other):
    first = lax.axis_index("core") == 0
    return jnp.where(first, mine, other), jnp.where(first, other, mine)


def block_of(mine_ref, other_ref, block):
    field, ridge = [], []
    for half in range(2):
        chip = 2 * block + half
        for piece in by_core(mine_ref[chip], other_ref[chip]):
            field += [piece[:S], piece[S : 2 * S]]
            ridge += [piece[RIDGE : RIDGE + 1], piece[RIDGE + 1 : RIDGE + 2]]
    return jnp.concatenate(field, axis=1), jnp.concatenate(ridge, axis=1)


def fetch_parts(high_hbm, low_hbm, high_ref, low_ref, sems):
    def fetch(i):
        part = (i // PARTS, pl.ds(i % PARTS * PART, PART))
        return [
            pltpu.make_async_copy(there.at[part], here.at[part], sems.at[which, i])
            for which, (there, here) in enumerate(((high_hbm, high_ref), (low_hbm, low_ref)))
        ]

    for i in range(4 * PARTS):
        for copy in fetch(i):
            copy.start()
    return fetch


def multiply(fetch, high_ref, low_ref, field, put):
    def product(vec, tile, part, dims):
        vec_high, vec_low = split(vec)
        both = jnp.concatenate([vec_high, vec_low], axis=0)
        main = lax.dot_general(both, high_ref[tile, part], dims, preferred_element_type=F32)
        rest = lax.dot_general(vec_high, low_ref[tile, part], dims, preferred_element_type=F32)
        return main[:S] + (main[S:] + rest)

    half = jnp.zeros((S, S), F32)
    for tile in range(4):
        from_row, from_col = field(2 * tile), field(2 * tile + 1)
        into_row, into_col = [], []
        for part in range(PARTS):
            for copy in fetch(tile * PARTS + part):
                copy.wait()
            at = slice(part * PART, (part + 1) * PART)
            into_row.append(product(from_col, tile, at, NT))
            into_col.append(product(from_row[:, at], tile, at, NN))
        into_row = jnp.concatenate(into_row, axis=1)
        put(2 * tile, into_row)
        put(2 * tile + 1, sum(into_col[1:], into_col[0]))
        half = half + gram(from_row, into_row)
    return half + half.T


def first_kernel(
    list_ref, mine_ref, other_ref, right_ref, ridge_ref, high_hbm, low_hbm, out_ref,
    high_ref, low_ref, gram_ref, sems,
):
    fetch = fetch_parts(high_hbm, low_hbm, high_ref, low_ref, sems)

    def field(k):
        return block_of(mine_ref, other_ref, list_ref[k // 2, k % 2])[0]

    def put(k, value):
        tall = jnp.concatenate([value[:, j * D : (j + 1) * D] for j in range(J)], axis=0)
        out_ref[pl.ds(k, D, stride=R1_ROWS), :] = tall.T

    right = right_ref[...]
    ridge = jnp.concatenate([ridge_ref[0:1], ridge_ref[1:2]], axis=1)
    gram_ref[...] = gram(right, ridge * right)
    curvature = multiply(fetch, high_ref, low_ref, field, put)
    flat = flat_rows(widen(gram_ref[...] + curvature))
    for i in range(2):
        out_ref[pl.ds(ENDS + i, D, stride=R1_ROWS), :] = jnp.broadcast_to(flat[i : i + 1], (D, D))


def end_matches(ends, k):
    return (ends[:, k : k + 1] == iota((D, NB), 1).astype(F32)).astype(F32)


def owner_kernel(got_ref, mine_ref, other_ref, out_ref, ends_ref):
    even, odd = by_core(mine_ref[:, LIST, :], other_ref[:, LIST, :])
    ends_ref[pl.ds(0, N, stride=2), :] = even
    ends_ref[pl.ds(1, N, stride=2), :] = odd
    ends = ends_ref[...]
    total = jnp.zeros((NB, D), F32)
    for k in range(ENDS):
        part = got_ref[pl.ds(k, D, stride=R1_ROWS), :]
        total = total + exact(end_matches(ends, k).T, part)
    for k in range(ENDS):
        out_ref[pl.ds(k, D, stride=G2_ROWS), :] = exact(end_matches(ends, k), total)
    for q in range(4):
        own = [total[:, 2 * S * q : 2 * S * (q + 1)], jnp.zeros((NB, D - 2 * S), F32)]
        out_ref[pl.ds(G2_ROWS * q + ENDS, NB, stride=4 * G2_ROWS), :] = jnp.concatenate(own, axis=1)


def alpha_kernel(got_ref, mine_ref, other_ref, out_ref):
    curvature, norm = [], []
    for i in range(2):
        part = got_ref[pl.ds(ENDS + i, D, stride=R1_ROWS), :]
        curvature.append(jnp.sum(part, axis=0, keepdims=True))
        part = mine_ref[:, NORM + i, :] + other_ref[:, NORM + i, :]
        norm.append(jnp.sum(part, axis=0, keepdims=True))
    out_ref[0] = from_rows(jnp.concatenate(norm, axis=0))
    out_ref[1] = from_rows(jnp.concatenate(curvature, axis=0))
    out_ref[2] = gauss_solve(out_ref[1], out_ref[0])


def second_kernel(
    list_ref, mine_ref, other_ref, right_ref, ridge_ref, got_ref, small_ref, high_hbm, low_hbm,
    out_ref, keep_ref, high_ref, low_ref, gram_ref, sems,
):
    fetch = fetch_parts(high_hbm, low_hbm, high_ref, low_ref, sems)
    alpha_t = small_t(small_ref[2])[:, :S]

    def field(k):
        right, ridge = block_of(mine_ref, other_ref, list_ref[k // 2, k % 2])
        turned = got_ref[pl.ds(k, D, stride=G2_ROWS), :].T
        image = jnp.concatenate([turned[j * S : (j + 1) * S] for j in range(J)], axis=1)
        return right - exact(alpha_t, image + ridge * right)

    core = lax.axis_index("core")
    out_ref[...] = jnp.zeros(out_ref.shape, F32)

    def put(k, value):
        block = list_ref[k // 2, k % 2]
        for q in range(4):
            chip, side = 2 * block + q // 2, (q % 2 + core) % 2
            for j in range(2):
                rows = slice(j * S, (j + 1) * S)
                lanes = slice((2 * q + j) * D, (2 * q + j + 1) * D)
                out_ref[side, chip, rows] = out_ref[side, chip, rows] + value[:, lanes]

    right = right_ref[...]
    ridge = jnp.concatenate([ridge_ref[0:1], ridge_ref[1:2]], axis=1)
    turned = got_ref[pl.ds(ENDS, D, stride=G2_ROWS), :].T
    image = jnp.concatenate([turned[:S], turned[S : 2 * S]], axis=1) + ridge * right
    residual = right - exact(alpha_t, image)
    keep_ref[0] = residual
    keep_ref[1] = image
    gram_ref[0] = gram(residual, residual)
    gram_ref[1] = gram(residual, image)
    gram_ref[2] = gram(residual, ridge * residual)
    gram_ref[2] += multiply(fetch, high_ref, low_ref, field, put)
    flat = jnp.concatenate(
        [flat_rows(widen(gram_ref[i])) for i in range(3)] + [jnp.zeros((2, D), F32)], axis=0
    )
    for side in range(2):
        for chip in range(N):
            out_ref[side, chip, GRAMS:] = flat


def last_kernel(
    got_ref, right_ref, ridge_ref, keep_ref, small_ref, solution_ref, residual_ref, gram_ref
):
    total = got_ref[0]
    for chip in range(1, N):
        total = total + got_ref[chip]
    right = right_ref[...]
    residual, image = keep_ref[0], keep_ref[1]
    ridge = jnp.concatenate([ridge_ref[0:1], ridge_ref[1:2]], axis=1)
    second = jnp.concatenate([total[:S], total[S : 2 * S]], axis=1) + ridge * residual
    for i in range(3):
        gram_ref[i] = from_rows(total[GRAMS + 2 * i : GRAMS + 2 * i + 2])
    beta = gauss_solve(small_ref[0], gram_ref[0])
    gram_ref[3] = small_mul(gram_ref[1], beta)
    gram_ref[4] = small_mul(small_t(beta), small_mul(small_ref[1], beta))
    bent = gram_ref[2] + gram_ref[3] + small_t(gram_ref[3]) + gram_ref[4]
    last = gauss_solve(bent, gram_ref[0])
    direction = residual + mixed(beta, right)
    image_next = second + mixed(beta, image)
    solution_ref[...] = mixed(small_ref[2], right) + mixed(last, direction)
    residual_ref[...] = residual - mixed(last, image_next)


HERE = pl.BlockSpec(memory_space=pltpu.VMEM)
SCALARS = pl.BlockSpec(memory_space=pltpu.SMEM)
THERE = pl.BlockSpec(memory_space=pltpu.HBM)
STAGED = [
    pltpu.VMEM((4, B, B), BF16),
    pltpu.VMEM((4, B, B), BF16),
]


def call(kernel, name, shapes, specs, args, scratch=(), limit=32):
    return pl.pallas_call(
        kernel,
        out_shape=[jax.ShapeDtypeStruct(shape, F32) for shape in shapes],
        in_specs=specs,
        out_specs=[HERE] * len(shapes),
        scratch_shapes=scratch,
        compiler_params=pltpu.CompilerParams(vmem_limit_bytes=limit << 20),
        name=name,
    )(*args)


def exchange_rows(x, rows):
    return lax.all_to_all(x.reshape(D, 1, rows * D), ALL, 0, 0).reshape(D * rows, D)


def swap(x):
    return lax.ppermute(x, "core", [(0, 1), (1, 0)])


def local(right, ridge, tiles, tile_list):
    ridge = ridge.reshape(2, D)
    (packed,) = call(
        gather_pack_kernel, "pack", [(N, SLOT, D)], [HERE, HERE, SCALARS], (right, ridge, tile_list)
    )
    later_list, packed = lax.optimization_barrier((tile_list, packed))
    staged = stage(tiles, later_list)
    mine = lax.all_to_all(packed, CHIPS, 0, 0)
    mine, *staged = lax.optimization_barrier((mine, *staged))
    other = swap(mine)
    sems = pltpu.SemaphoreType.DMA((2, 4 * PARTS))
    (sent,) = call(
        first_kernel,
        "first",
        [(D * R1_ROWS, D)],
        [SCALARS] + [HERE] * 4 + [THERE] * 2,
        (tile_list, mine, other, right, ridge, *staged),
        [*STAGED, pltpu.VMEM((S, S), F32), sems],
        48,
    )
    got = exchange_rows(sent, R1_ROWS)
    (sent,) = call(
        owner_kernel,
        "owner",
        [(D * G2_ROWS, D)],
        [HERE] * 3,
        (got, mine, other),
        [pltpu.VMEM((D, D), F32)],
    )
    (small,) = call(alpha_kernel, "alpha", [(3, S, D)], [HERE] * 3, (got, mine, other))
    got = exchange_rows(sent, G2_ROWS)
    sent, keep = call(
        second_kernel,
        "second",
        [(2, N, SLOT, D), (2, S, 2 * D)],
        [SCALARS] + [HERE] * 6 + [THERE] * 2,
        (tile_list, mine, other, right, ridge, got, small, *staged),
        [*STAGED, pltpu.VMEM((3, S, S), F32), sems],
        48,
    )
    got = lax.all_to_all(sent[0] + swap(sent[1]), CHIPS, 0, 0)
    return tuple(
        call(
            last_kernel,
            "last",
            [(S, 2 * D)] * 2,
            [HERE] * 5,
            (got, right, ridge, keep, small),
            [pltpu.VMEM((5, S, D), F32)],
        )
    )


def solution(mesh):
    mesh = jax.sharding.Mesh(mesh.devices.reshape(4, 16, 2), ALL)
    return jax.shard_map(
        local,
        mesh=mesh,
        in_specs=(P(None, ALL), P(ALL), P(ALL, None, None), P(ALL, None)),
        out_specs=(P(None, ALL), P(None, ALL)),
        check_vma=False,
    )
```

time: 1810 us -> 141 us (0.08)
  waiting for transfers between devices: 1390 us -> 25.1 us
  blocking collectives: 201 us -> 44.2 us
  matrix products: 87.4 us -> 0 us
  between operations: 48.2 us -> 0.71 us
  Pallas kernels: 0 us -> 46.3 us
  local copies, waits for them, and re-layouts: 41.3 us -> 3.15 us
  starting transfers between devices: 0.16 us -> 20.5 us
  loops' own time: 20 us -> 0 us
    reduce_scatter x2 -> x0, waiting for transfers between devices: 1260 us -> none  [local(): lax.psum_scatter(partial_image, ('grp', 'tile'), scatter_dimension=1, til...]
    psum x3 -> x0, blocking collectives: 201 us -> none  [the longest x1 69.3 us: local(): norm_now = lax.psum(gram(residual, residual), ('grp', 'tile'))]
    all_gather x2 -> x0, waiting for transfers between devices: 134 us -> none  [local(): lax.all_gather(direction, ('grp', 'tile'), axis=1, tiled=True)]
    dot_general x25 -> x0, matrix products: 87.4 us -> none  [the longest x8 45.1 us: step(): lax.dot_general(from_col, direct_tile, (((1,), (1,)), ((), ())), precisio...]
    pallas_call x0 -> x7, Pallas kernels: none -> 46.3 us  [the longest x6 33.3 us: call(): pl.pallas_call(kernel, out_shape=[jax.ShapeDtypeStruct(shape, F32) for sh...]
    all_to_all x0 -> x2, blocking collectives: none -> 44.2 us  [the longest x1 25.3 us: local(): got = lax.all_to_all(sent[0] + swap(sent[1]), CHIPS, 0, 0)]
    slice x56 -> x0, local copies, waits for them, and re-layouts: 32.1 us -> none  [the longest x48 27.8 us: gauss_solve(): scale = 1.0 / matrix[pivot, pivot]]
    another operation x2 -> x0, loops' own time: 20 us -> none  [apply_kernel(): total, _ = lax.scan(step, start, (tiles, tile_list))]
  transfers between devices with their start and end apart: 4 -> 4, of which waited for: 4 -> 4; matrix products, arithmetic and copies ran while one was open for 0% -> 0% of each run, Pallas kernels for 0% -> 11%
where the time goes in v2:
time: 141 us; the launch traced here: 140 us
  Pallas kernels  46.3 us (33%)
  blocking collectives  44.2 us (31%)
  waiting for transfers between devices  25.1 us (18%)
  starting transfers between devices  20.5 us (15%)
  local copies, waits for them, and re-layouts  3.15 us (2%)
    pallas_call x6, Pallas kernels, call(): pl.pallas_call(kernel, out_shape=[jax.ShapeDtypeStruct(shape, F32) for sh...  33.3 us
    all_to_all x1, blocking collectives, local(): got = lax.all_to_all(sent[0] + swap(sent[1]), CHIPS, 0, 0)  25.3 us
    all_to_all x1, blocking collectives, exchange_rows(): lax.all_to_all(x.reshape(D, 1, rows * D), ALL, 0, 0).reshape(D * rows, D)  18.8 us
    pallas_call x1, Pallas kernels, stage(): pl.pallas_call(stage_kernel, out_shape=[pltpu.HBM((4, B, B), BF16)] * 2,...  12.9 us
    all_to_all x1, waiting for transfers between devices, exchange_rows(): lax.all_to_all(x.reshape(D, 1, rows * D), ALL, 0, 0).reshape(D * rows, D)  12.4 us
    all_to_all x1, starting transfers between devices, local(): mine = lax.all_to_all(packed, CHIPS, 0, 0)  12.1 us
    all_to_all x1, waiting for transfers between devices, local(): mine = lax.all_to_all(packed, CHIPS, 0, 0)  7.4 us
    ppermute x2, waiting for transfers between devices, swap(): return lax.ppermute(x, 'core', [(0, 1), (1, 0)])  5.32 us
  transfers between devices with their start and end apart: 4, of which 4 were waited for; matrix products, arithmetic and copies ran while one was open for 0% of the time, Pallas kernels for 11%

profile of v2, /device:TPU:1, one launch (start us, length us, event | category | flops | bytes accessed | tf_op | source)
XLA Modules:
  0.0 140.1 jit_solution(9032493375157566079)
XLA Ops:
  0.6 0.8 copy.15.list_ref
  1.4 0.0 copy-start.1
  1.4 0.7 copy-done.1
  2.1 0.0 copy-start.3
  2.1 0.7 copy-done.3
  2.8 1.9 %pack.1 = f32[64,40,128]{2,1,0:T(8,128)} custom-call(f32[16,256]{1,0:T(8,128)S(1)} %copy-done.1, f32[2,128]{1,0:T(2,128)S(1)} %bitcast.13, s32[4,2]{1,0:T(4,128)S(1)} %copy.15.list_ref), custom_call_target="tpu_custom_call" | custom-call | tf_op jit(solution)/shard_map/pack/pallas_call | solution.py:358
  4.7 0.0 copy-start.5
  4.7 12.1 %all-to-all-start = ((f32[64,40,128]{2,1,0:T(8,128)}), f32[64,40,128]{2,1,0:T(8,128)S(1)}, u32[]{:S(2)}, u32[]{:S(2)}) async-start(f32[64,40,128]{2,1,0:T(8,128)} %pack.1), calls=%async_computation | async-start | bytes 2621440 | tf_op jit(solution)/shard_map/all_to_all | solution.py:384
  16.8 0.0 copy-done.5
  16.8 0.1 copy.11.list_ref
  16.9 0.0 copy-start.2
  16.9 12.9 %stage.1 = (bf16[4,1024,1024]{2,1,0:T(8,128)(2,1)}, bf16[4,1024,1024]{2,1,0:T(8,128)(2,1)}) custom-call(s32[4,2]{1,0:T(4,128)S(1)} %copy.11.list_ref, f32[4,1024,1024]{2,1,0:T(8,128)} %tiles_ref.1), custom_call_target="tpu_custom_call" | custom-call | tf_op jit(solution)/shard_map/stage/pallas_call | solution.py:156
  29.8 7.4 %all-to-all-done.mine_ref = f32[64,40,128]{2,1,0:T(8,128)S(1)} async-done(((f32[64,40,128]{2,1,0:T(8,128)}), f32[64,40,128]{2,1,0:T(8,128)S(1)}, u32[]{:S(2)}, u32[]{:S(2)}) %all-to-all-start) | async-done | bytes 1310752 | tf_op jit(solution)/shard_map/all_to_all | solution.py:384
  37.2 2.2 %collective-permute-start = (f32[64,40,128]{2,1,0:T(8,128)S(1)}, f32[64,40,128]{2,1,0:T(8,128)S(1)}, u32[]{:S(2)}, u32[]{:S(2)}) collective-permute-start(f32[64,40,128]{2,1,0:T(8,128)S(1)} %all-to-all-done.mine_ref), channel_id=1, source_target_pairs={{0,1},{1,0},{2,3},{3,2},{4,5},{5,4},{6,7},{7,6},{8,9},{9,8},{10,11... | collective-permute-start | bytes 3932168 | tf_op jit(solution)/shard_map/ppermute | solution.py:374
  39.4 2.7 %collective-permute-done.other_ref = f32[64,40,128]{2,1,0:T(8,128)S(1)} collective-permute-done((f32[64,40,128]{2,1,0:T(8,128)S(1)}, f32[64,40,128]{2,1,0:T(8,128)S(1)}, u32[]{:S(2)}, u32[]{:S(2)}) %collective-permute-start) | collective-permute-done | bytes 1310752 | tf_op jit(solution)/shard_map/ppermute | solution.py:374
  42.1 0.0 copy-done.2
  42.1 0.0 copy-done.4
  42.1 11.3 %first.1 = f32[1280,128]{1,0:T(8,128)S(1)} custom-call(s32[4,2]{1,0:T(4,128)S(1)} %copy.15.list_ref, f32[64,40,128]{2,1,0:T(8,128)S(1)} %all-to-all-done.mine_ref, f32[64,40,128]{2,1,0:T(8,128)S(1)} %collective-permute-done.other_ref, f32[16,256]{1,0:T(8,128)S(1)} %copy-done.2, f32[2,128]{1,0:T(2,128)S(1)} %bitcast.14, ...), custom_call_target="tpu_custom_call" | custom-call | tf_op jit(solution)/shard_map/first/pallas_call | solution.py:358
  53.4 18.8 %all_to_all.20 = f32[128,1,1280]{2,1,0:T(1,128)S(1)} all-to-all(f32[128,1,1280]{2,1,0:T(1,128)S(1)} %bitcast.11), channel_id=1, replica_groups=mesh['grp'=4,'ring'=16,'core'=2] {'grp','ring','core'}, dimensions={0} | all-to-all | bytes 1310720 | tf_op jit(solution)/shard_map/all_to_all | solution.py:370
  72.2 2.0 %owner.1 = f32[1152,128]{1,0:T(8,128)S(1)} custom-call(f32[1280,128]{1,0:T(8,128)S(1)} %bitcast.9, f32[64,40,128]{2,1,0:T(8,128)S(1)} %all-to-all-done.mine_ref, f32[64,40,128]{2,1,0:T(8,128)S(1)} %collective-permute-done.other_ref), custom_call_target="tpu_custom_call" | custom-call | tf_op jit(solution)/shard_map/owner/pallas_call | solution.py:358
  74.2 0.0 copy-start
  74.2 0.8 copy-done
  75.0 5.3 %all-to-all-start.2 = ((f32[128,1,1152]{2,1,0:T(1,128)}), f32[128,1,1152]{2,1,0:T(1,128)}, u32[]{:S(2)}, u32[]{:S(2)}) async-start(f32[128,1,1152]{2,1,0:T(1,128)} %bitcast.12), calls=%async_computation.2 | async-start | bytes 1179648 | tf_op jit(solution)/shard_map/all_to_all | solution.py:370
  80.3 1.8 %alpha.1.small_ref = f32[3,16,128]{2,1,0:T(8,128)S(1)} custom-call(f32[1280,128]{1,0:T(8,128)S(1)} %bitcast.10, f32[64,40,128]{2,1,0:T(8,128)S(1)} %all-to-all-done.mine_ref, f32[64,40,128]{2,1,0:T(8,128)S(1)} %collective-permute-done.other_ref), custom_call_target="tpu_custom_call" | custom-call | tf_op jit(solution)/shard_map/alpha/pallas_call | solution.py:358
  82.2 12.4 %all-to-all-done.2 = f32[128,1,1152]{2,1,0:T(1,128)} async-done(((f32[128,1,1152]{2,1,0:T(1,128)}), f32[128,1,1152]{2,1,0:T(1,128)}, u32[]{:S(2)}, u32[]{:S(2)}) %all-to-all-start.2) | async-done | bytes 589856 | tf_op jit(solution)/shard_map/all_to_all | solution.py:370
  94.6 11.7 %second.1 = (f32[2,64,40,128]{3,2,1,0:T(8,128)S(1)}, f32[2,16,256]{2,1,0:T(8,128)S(1)}) custom-call(s32[4,2]{1,0:T(4,128)S(1)} %copy.15.list_ref, f32[64,40,128]{2,1,0:T(8,128)S(1)} %all-to-all-done.mine_ref, f32[64,40,128]{2,1,0:T(8,128)S(1)} %collective-permute-done.other_ref, f32[16,256]{1,0:T(8,128)S(1)} %copy-done.2, f32[2,128]{1,0:T(2,128)S(1)} %bitcast.15, ...), custom_call_target="tpu_custom_call" | custom-call | tf_op jit(solution)/shard_map/second/pallas_call | solution.py:358
  106.3 0.1 slice_bitcast_fusion
  106.4 1.0 collective-permute-start.1
  107.3 2.7 %collective-permute-done.1 = f32[64,40,128]{2,1,0:T(8,128)S(1)} collective-permute-done((f32[64,40,128]{2,1,0:T(8,128)S(1)}, f32[64,40,128]{2,1,0:T(8,128)S(1)}, u32[]{:S(2)}, u32[]{:S(2)}) %collective-permute-start.1) | collective-permute-done | bytes 1310752 | tf_op jit(solution)/shard_map/ppermute | solution.py:374
  110.0 0.1 bitcast_add_fusion
  110.1 25.3 %all_to_all.21.got_ref = f32[64,40,128]{2,1,0:T(8,128)S(1)} all-to-all(f32[64,40,128]{2,1,0:T(8,128)S(1)} %bitcast_add_fusion), channel_id=1, replica_groups=mesh['grp'=4,'ring'=16,'core'=2] {'grp','ring'}, dimensions={0} | all-to-all | bytes 2621440 | tf_op jit(solution)/shard_map/all_to_all | solution.py:417
  135.4 4.6 %last.1 = (f32[16,256]{1,0:T(8,128)}, f32[16,256]{1,0:T(8,128)}) custom-call(f32[64,40,128]{2,1,0:T(8,128)S(1)} %all_to_all.21.got_ref, f32[16,256]{1,0:T(8,128)S(1)} %copy-done.2, f32[2,128]{1,0:T(2,128)S(1)} %bitcast.16, f32[2,16,256]{2,1,0:T(8,128)S(1)} %get-tuple-element.19.keep_ref, f32[3,16,128]{2,1,0:T(8,128)S(1)} %alpha.1.small_ref), custom_call_target="tpu_custom_call" | custom-call | tf_op jit(solution)/shard_map/last/pallas_call | solution.py:358
  (1 shorter events, 0.0 us)
Async XLA Ops:
  1.4 0.7 copy-start.1
  2.1 0.7 copy-start.3
  4.7 12.1 %copy-start.5 = (s32[4,2]{0,1:T(2,128)S(1)}, s32[4,2]{0,1:T(2,128)}, u32[]{:S(2)}) copy-start(s32[4,2]{0,1:T(2,128)} %param.7) | copy-start | bytes 100
  4.7 32.5 %all-to-all-start = ((f32[64,40,128]{2,1,0:T(8,128)}), f32[64,40,128]{2,1,0:T(8,128)S(1)}, u32[]{:S(2)}, u32[]{:S(2)}) async-start(f32[64,40,128]{2,1,0:T(8,128)} %pack.1), calls=%async_computation | async-start | bytes 2621440 | tf_op jit(solution)/shard_map/all_to_all | solution.py:384
  16.9 25.2 %copy-start.2 = (f32[16,256]{1,0:T(8,128)S(1)}, f32[16,256]{1,0:T(8,128)}, u32[]{:S(2)}) copy-start(f32[16,256]{1,0:T(8,128)} %right_ref.7) | copy-start | bytes 49156
  16.9 25.2 %copy-start.4 = (f32[256]{0:T(256)S(1)}, f32[256]{0:T(256)}, u32[]{:S(2)}) copy-start(f32[256]{0:T(256)} %param.5) | copy-start | bytes 3076
  37.2 4.8 %collective-permute-start = (f32[64,40,128]{2,1,0:T(8,128)S(1)}, f32[64,40,128]{2,1,0:T(8,128)S(1)}, u32[]{:S(2)}, u32[]{:S(2)}) collective-permute-start(f32[64,40,128]{2,1,0:T(8,128)S(1)} %all-to-all-done.mine_ref), channel_id=1, source_target_pairs={{0,1},{1,0},{2,3},{3,2},{4,5},{5,4},{6,7},{7,6},{8,9},{9,8},{10,11... | collective-permute-start | bytes 3932168 | tf_op jit(solution)/shard_map/ppermute | solution.py:374
  74.2 0.8 copy-start
  75.0 19.6 %all-to-all-start.2 = ((f32[128,1,1152]{2,1,0:T(1,128)}), f32[128,1,1152]{2,1,0:T(1,128)}, u32[]{:S(2)}, u32[]{:S(2)}) async-start(f32[128,1,1152]{2,1,0:T(1,128)} %bitcast.12), calls=%async_computation.2 | async-start | bytes 1179648 | tf_op jit(solution)/shard_map/all_to_all | solution.py:370
  106.4 3.6 %collective-permute-start.1 = (f32[64,40,128]{2,1,0:T(8,128)S(1)}, f32[64,40,128]{2,1,0:T(8,128)S(1)}, u32[]{:S(2)}, u32[]{:S(2)}) collective-permute-start(f32[64,40,128]{2,1,0:T(8,128)S(1)} %slice_bitcast_fusion), channel_id=1, source_target_pairs={{0,1},{1,0},{2,3},{3,2},{4,5},{5,4},{6,7},{7,6},{8,9},{9,8},{10,11... | collective-permute-start | bytes 3932168 | tf_op jit(solution)/shard_map/ppermute | solution.py:374

commit v3 on v2

--- a/solution.py
+++ b/solution.py
@@ -16,17 +16,18 @@
 N = 64
 J = 8
 ENDS = 8
+GATHER = 32
+OWN = 10
 SLOT = 40
-RIDGE, NORM, LIST = 32, 34, 36
 GRAMS = 32
-R1_ROWS = 10
+R1_ROWS = 11
 G2_ROWS = 9
 F32 = jnp.float32
 BF16 = jnp.bfloat16
 PIECE = 256
 PIECES = B // PIECE
-PART = 512
-PARTS = B // PART
+PARTS = [(0, 0, 256), (0, 256, 256), (0, 512, 512)]
+PARTS += [(tile, first, 512) for tile in range(1, 4) for first in (0, 512)]
 NT = (((1,), (1,)), ((), ()))
 NN = (((1,), (0,)), ((), ()))
 
@@ -101,15 +102,9 @@
     return spread_sum(jnp.where((lane >= S) & (lane < 2 * S), work, 0.0))
 
 
-def gather_pack_kernel(right_ref, ridge_ref, list_ref, out_ref):
+def gather_pack_kernel(right_ref, out_ref):
     right = right_ref[...]
-    rows = [right[:, :D], right[:, D:], ridge_ref[...], flat_rows(widen(gram(right, right)))]
-    slot = iota((1, D), 1)
-    ends = jnp.zeros((1, D), F32)
-    for k in range(ENDS):
-        ends = jnp.where(slot == k, list_ref[k // 2, k % 2].astype(F32), ends)
-    rows += [ends, jnp.zeros((SLOT - LIST - 1, D), F32)]
-    packed = jnp.concatenate(rows, axis=0)
+    packed = jnp.concatenate([right[:, :D], right[:, D:]], axis=0)
     for chip in range(N):
         out_ref[chip] = packed
 
@@ -138,7 +133,7 @@
         tile, first = i // PIECES, i % PIECES * PIECE
         high[i], low[i] = split(held[i])
 
-        @pl.when(list_ref[tile, 0] == list_ref[tile, 1])
+        @pl.when(list_ref[0, tile] == list_ref[1, tile])
         def _():
             row, col = iota((PIECE, B), 0) + first, iota((PIECE, B), 1)
             kept = jnp.where(row > col, held[i], jnp.where(row == col, 0.5 * held[i], 0.0))
@@ -176,24 +171,24 @@
 
 
 def block_of(mine_ref, other_ref, block):
-    field, ridge = [], []
+    field = []
     for half in range(2):
         chip = 2 * block + half
         for piece in by_core(mine_ref[chip], other_ref[chip]):
-            field += [piece[:S], piece[S : 2 * S]]
-            ridge += [piece[RIDGE : RIDGE + 1], piece[RIDGE + 1 : RIDGE + 2]]
-    return jnp.concatenate(field, axis=1), jnp.concatenate(ridge, axis=1)
+            field += [piece[:S], piece[S:]]
+    return jnp.concatenate(field, axis=1)
 
 
 def fetch_parts(high_hbm, low_hbm, high_ref, low_ref, sems):
     def fetch(i):
-        part = (i // PARTS, pl.ds(i % PARTS * PART, PART))
+        tile, first, rows = PARTS[i]
+        part = (tile, pl.ds(first, rows))
         return [
             pltpu.make_async_copy(there.at[part], here.at[part], sems.at[which, i])
             for which, (there, here) in enumerate(((high_hbm, high_ref), (low_hbm, low_ref)))
         ]
 
-    for i in range(4 * PARTS):
+    for i in range(len(PARTS)):
         for copy in fetch(i):
             copy.start()
     return fetch
@@ -211,10 +206,12 @@
     for tile in range(4):
         from_row, from_col = field(2 * tile), field(2 * tile + 1)
         into_row, into_col = [], []
-        for part in range(PARTS):
-            for copy in fetch(tile * PARTS + part):
+        for i, (owner, first, rows) in enumerate(PARTS):
+            if owner != tile:
+                continue
+            for copy in fetch(i):
                 copy.wait()
-            at = slice(part * PART, (part + 1) * PART)
+            at = slice(first, first + rows)
             into_row.append(product(from_col, tile, at, NT))
             into_col.append(product(from_row[:, at], tile, at, NN))
         into_row = jnp.concatenate(into_row, axis=1)
@@ -231,15 +228,21 @@
     fetch = fetch_parts(high_hbm, low_hbm, high_ref, low_ref, sems)
 
     def field(k):
-        return block_of(mine_ref, other_ref, list_ref[k // 2, k % 2])[0]
+        return block_of(mine_ref, other_ref, list_ref[k % 2, k // 2])
 
     def put(k, value):
         tall = jnp.concatenate([value[:, j * D : (j + 1) * D] for j in range(J)], axis=0)
         out_ref[pl.ds(k, D, stride=R1_ROWS), :] = tall.T
 
     right = right_ref[...]
-    ridge = jnp.concatenate([ridge_ref[0:1], ridge_ref[1:2]], axis=1)
-    gram_ref[...] = gram(right, ridge * right)
+    scaled = jnp.concatenate([ridge_ref[0:1], ridge_ref[1:2]], axis=1) * right
+    gram_ref[...] = gram(right, scaled)
+    slot = iota((ENDS, D), 0)
+    ends = jnp.zeros((ENDS, D), F32)
+    for k in range(ENDS):
+        ends = jnp.where(slot == k, list_ref[k % 2, k // 2].astype(F32), ends)
+    own = [scaled[:, :D], scaled[:, D:], ends, jnp.zeros((D - 2 * S - ENDS, D), F32)]
+    out_ref[pl.ds(OWN, D, stride=R1_ROWS), :] = jnp.concatenate(own, axis=0).T
     curvature = multiply(fetch, high_ref, low_ref, field, put)
     flat = flat_rows(widen(gram_ref[...] + curvature))
     for i in range(2):
@@ -247,33 +250,49 @@
 
 
 def end_matches(ends, k):
-    return (ends[:, k : k + 1] == iota((D, NB), 1).astype(F32)).astype(F32)
-
-
-def owner_kernel(got_ref, mine_ref, other_ref, out_ref, ends_ref):
-    even, odd = by_core(mine_ref[:, LIST, :], other_ref[:, LIST, :])
-    ends_ref[pl.ds(0, N, stride=2), :] = even
-    ends_ref[pl.ds(1, N, stride=2), :] = odd
-    ends = ends_ref[...]
-    total = jnp.zeros((NB, D), F32)
+    return ends[:, k : k + 1] == iota((D, NB), 1).astype(F32)
+
+
+def select(matches, values):
+    high, rest = split(values)
+    low = (values - high.astype(F32) - rest.astype(F32)).astype(BF16)
+    parts = jnp.dot(
+        matches.astype(F32).astype(BF16),
+        jnp.concatenate([high, rest, low], axis=1),
+        preferred_element_type=F32,
+    )
+    return parts[:, :D] + parts[:, D : 2 * D] + parts[:, 2 * D :]
+
+
+def owner_kernel(got_ref, out_ref):
+    own = [got_ref[pl.ds(R1_ROWS * q + OWN, NB, stride=4 * R1_ROWS), :] for q in range(4)]
+    total = jnp.concatenate([part[:, : 2 * S] for part in own], axis=1)
+    ends = got_ref[pl.ds(OWN, D, stride=R1_ROWS), :][:, 2 * S : 2 * S + ENDS]
     for k in range(ENDS):
         part = got_ref[pl.ds(k, D, stride=R1_ROWS), :]
-        total = total + exact(end_matches(ends, k).T, part)
+        total = total + select(end_matches(ends, k).astype(F32).T, part)
     for k in range(ENDS):
-        out_ref[pl.ds(k, D, stride=G2_ROWS), :] = exact(end_matches(ends, k), total)
+        out_ref[pl.ds(k, D, stride=G2_ROWS), :] = select(end_matches(ends, k), total)
     for q in range(4):
         own = [total[:, 2 * S * q : 2 * S * (q + 1)], jnp.zeros((NB, D - 2 * S), F32)]
         out_ref[pl.ds(G2_ROWS * q + ENDS, NB, stride=4 * G2_ROWS), :] = jnp.concatenate(own, axis=1)
 
 
-def alpha_kernel(got_ref, mine_ref, other_ref, out_ref):
-    curvature, norm = [], []
+def alpha_kernel(got_ref, mine_ref, other_ref, out_ref, norm_ref):
+    norm_ref[...] = jnp.zeros((S, S), F32)
+    for ref in (mine_ref, other_ref):
+
+        @pl.loop(0, N, step=4)
+        def _(chip):
+            pieces = [ref[chip + i] for i in range(4)]
+            wide = jnp.concatenate([half for p in pieces for half in (p[:S], p[S:])], axis=1)
+            norm_ref[...] += gram(wide, wide)
+
+    curvature = []
     for i in range(2):
         part = got_ref[pl.ds(ENDS + i, D, stride=R1_ROWS), :]
         curvature.append(jnp.sum(part, axis=0, keepdims=True))
-        part = mine_ref[:, NORM + i, :] + other_ref[:, NORM + i, :]
-        norm.append(jnp.sum(part, axis=0, keepdims=True))
-    out_ref[0] = from_rows(jnp.concatenate(norm, axis=0))
+    out_ref[0] = widen(norm_ref[...])
     out_ref[1] = from_rows(jnp.concatenate(curvature, axis=0))
     out_ref[2] = gauss_solve(out_ref[1], out_ref[0])
 
@@ -286,16 +305,15 @@
     alpha_t = small_t(small_ref[2])[:, :S]
 
     def field(k):
-        right, ridge = block_of(mine_ref, other_ref, list_ref[k // 2, k % 2])
         turned = got_ref[pl.ds(k, D, stride=G2_ROWS), :].T
         image = jnp.concatenate([turned[j * S : (j + 1) * S] for j in range(J)], axis=1)
-        return right - exact(alpha_t, image + ridge * right)
+        return block_of(mine_ref, other_ref, list_ref[k % 2, k // 2]) - exact(alpha_t, image)
 
     core = lax.axis_index("core")
     out_ref[...] = jnp.zeros(out_ref.shape, F32)
 
     def put(k, value):
-        block = list_ref[k // 2, k % 2]
+        block = list_ref[k % 2, k // 2]
         for q in range(4):
             chip, side = 2 * block + q // 2, (q % 2 + core) % 2
             for j in range(2):
@@ -306,7 +324,7 @@
     right = right_ref[...]
     ridge = jnp.concatenate([ridge_ref[0:1], ridge_ref[1:2]], axis=1)
     turned = got_ref[pl.ds(ENDS, D, stride=G2_ROWS), :].T
-    image = jnp.concatenate([turned[:S], turned[S : 2 * S]], axis=1) + ridge * right
+    image = jnp.concatenate([turned[:S], turned[S : 2 * S]], axis=1)
     residual = right - exact(alpha_t, image)
     keep_ref[0] = residual
     keep_ref[1] = image
@@ -376,15 +394,14 @@
 
 def local(right, ridge, tiles, tile_list):
     ridge = ridge.reshape(2, D)
-    (packed,) = call(
-        gather_pack_kernel, "pack", [(N, SLOT, D)], [HERE, HERE, SCALARS], (right, ridge, tile_list)
-    )
+    tile_list = tile_list.T
+    (packed,) = call(gather_pack_kernel, "pack", [(N, GATHER, D)], [HERE], (right,))
     later_list, packed = lax.optimization_barrier((tile_list, packed))
     staged = stage(tiles, later_list)
     mine = lax.all_to_all(packed, CHIPS, 0, 0)
     mine, *staged = lax.optimization_barrier((mine, *staged))
     other = swap(mine)
-    sems = pltpu.SemaphoreType.DMA((2, 4 * PARTS))
+    sems = pltpu.SemaphoreType.DMA((2, len(PARTS)))
     (sent,) = call(
         first_kernel,
         "first",
@@ -399,11 +416,17 @@
         owner_kernel,
         "owner",
         [(D * G2_ROWS, D)],
+        [HERE],
+        (got,),
+    )
+    (small,) = call(
+        alpha_kernel,
+        "alpha",
+        [(3, S, D)],
         [HERE] * 3,
         (got, mine, other),
-        [pltpu.VMEM((D, D), F32)],
-    )
-    (small,) = call(alpha_kernel, "alpha", [(3, S, D)], [HERE] * 3, (got, mine, other))
+        [pltpu.VMEM((S, S), F32)],
+    )
     got = exchange_rows(sent, G2_ROWS)
     sent, keep = call(
         second_kernel,

time: 141 us -> 134 us (0.950)
  waiting for transfers between devices: 25.1 us -> 16.2 us
  Pallas kernels: 46.3 us -> 50.6 us
  local copies, waits for them, and re-layouts: 3.15 us -> 1.64 us
    all_to_all x1, waiting for transfers between devices: 12.4 us -> 6.53 us  [exchange_rows(): lax.all_to_all(x.reshape(D, 1, rows * D), ALL, 0, 0).reshape(D * rows, D)]
    pallas_call x6, Pallas kernels: 33.3 us -> 37.6 us  [call(): pl.pallas_call(kernel, out_shape=[jax.ShapeDtypeStruct(shape, F32) for sh...]
    all_to_all x1, waiting for transfers between devices: 7.4 us -> 4.68 us  [local(): mine = lax.all_to_all(packed, CHIPS, 0, 0)]
    unnamed x13 -> x10, local copies, waits for them, and re-layouts: 2.97 us -> 1.55 us
  transfers between devices with their start and end apart: 4 -> 4, of which waited for: 4 -> 4; matrix products, arithmetic and copies ran while one was open for 0% -> 0% of each run, Pallas kernels for 11% -> 16%
where the time goes in v3:
time: 134 us
  Pallas kernels  50.6 us (38%)
  blocking collectives  44.6 us (33%)
  starting transfers between devices  19.7 us (15%)
  waiting for transfers between devices  16.2 us (12%)
  local copies, waits for them, and re-layouts  1.64 us (1%)
    pallas_call x6, Pallas kernels, call(): pl.pallas_call(kernel, out_shape=[jax.ShapeDtypeStruct(shape, F32) for sh...  37.6 us
    all_to_all x1, blocking collectives, local(): got = lax.all_to_all(sent[0] + swap(sent[1]), CHIPS, 0, 0)  25.3 us
    all_to_all x1, blocking collectives, exchange_rows(): lax.all_to_all(x.reshape(D, 1, rows * D), ALL, 0, 0).reshape(D * rows, D)  19.3 us
    pallas_call x1, Pallas kernels, stage(): pl.pallas_call(stage_kernel, out_shape=[pltpu.HBM((4, B, B), BF16)] * 2,...  12.9 us
    all_to_all x1, starting transfers between devices, local(): mine = lax.all_to_all(packed, CHIPS, 0, 0)  12.1 us
    all_to_all x1, waiting for transfers between devices, exchange_rows(): lax.all_to_all(x.reshape(D, 1, rows * D), ALL, 0, 0).reshape(D * rows, D)  6.53 us
    ppermute x2, waiting for transfers between devices, swap(): return lax.ppermute(x, 'core', [(0, 1), (1, 0)])  4.95 us
    all_to_all x1, waiting for transfers between devices, local(): mine = lax.all_to_all(packed, CHIPS, 0, 0)  4.68 us
  transfers between devices with their start and end apart: 4, of which 4 were waited for; matrix products, arithmetic and copies ran while one was open for 0% of the time, Pallas kernels for 16%

profile of v3, /device:TPU:1, one launch (start us, length us, event | category | flops | bytes accessed | tf_op | source)
XLA Modules:
  0.0 133.6 jit_solution(10222417750661733452)
XLA Ops:
  0.6 0.0 copy-start.1
  0.6 0.7 copy-done.1
  1.3 1.1 pack.1
  2.5 0.0 copy-start.3
  2.5 12.1 %all-to-all-start = ((f32[64,32,128]{2,1,0:T(8,128)}), f32[64,32,128]{2,1,0:T(8,128)S(1)}, u32[]{:S(2)}, u32[]{:S(2)}) async-start(f32[64,32,128]{2,1,0:T(8,128)} %pack.1), calls=%async_computation | async-start | bytes 2097152 | tf_op jit(solution)/shard_map/all_to_all | solution.py:401
  14.6 0.0 copy-done.3
  14.6 0.0 copy-start.2
  14.6 0.0 copy-start.4
  14.6 12.9 %stage.1 = (bf16[4,1024,1024]{2,1,0:T(8,128)(2,1)}, bf16[4,1024,1024]{2,1,0:T(8,128)(2,1)}) custom-call(s32[2,4]{1,0:T(2,128)S(1)} %bitcast.15, f32[4,1024,1024]{2,1,0:T(8,128)} %tiles_ref.1), custom_call_target="tpu_custom_call" | custom-call | tf_op jit(solution)/shard_map/stage/pallas_call | solution.py:151
  27.5 4.7 %all-to-all-done.mine_ref = f32[64,32,128]{2,1,0:T(8,128)S(1)} async-done(((f32[64,32,128]{2,1,0:T(8,128)}), f32[64,32,128]{2,1,0:T(8,128)S(1)}, u32[]{:S(2)}, u32[]{:S(2)}) %all-to-all-start) | async-done | bytes 1048608 | tf_op jit(solution)/shard_map/all_to_all | solution.py:401
  32.2 2.2 %collective-permute-start = (f32[64,32,128]{2,1,0:T(8,128)S(1)}, f32[64,32,128]{2,1,0:T(8,128)S(1)}, u32[]{:S(2)}, u32[]{:S(2)}) collective-permute-start(f32[64,32,128]{2,1,0:T(8,128)S(1)} %all-to-all-done.mine_ref), channel_id=1, source_target_pairs={{0,1},{1,0},{2,3},{3,2},{4,5},{5,4},{6,7},{7,6},{8,9},{9,8},{10,11... | collective-permute-start | bytes 3145736 | tf_op jit(solution)/shard_map/ppermute | solution.py:392
  34.4 2.3 %collective-permute-done.other_ref = f32[64,32,128]{2,1,0:T(8,128)S(1)} collective-permute-done((f32[64,32,128]{2,1,0:T(8,128)S(1)}, f32[64,32,128]{2,1,0:T(8,128)S(1)}, u32[]{:S(2)}, u32[]{:S(2)}) %collective-permute-start) | collective-permute-done | bytes 1048608 | tf_op jit(solution)/shard_map/ppermute | solution.py:392
  36.7 0.0 copy-done.2
  36.7 0.0 copy-done.4
  36.7 11.7 %first.1 = f32[1408,128]{1,0:T(8,128)S(1)} custom-call(s32[2,4]{1,0:T(2,128)S(1)} %bitcast.16, f32[64,32,128]{2,1,0:T(8,128)S(1)} %all-to-all-done.mine_ref, f32[64,32,128]{2,1,0:T(8,128)S(1)} %collective-permute-done.other_ref, f32[16,256]{1,0:T(8,128)S(1)} %copy-done.2, f32[2,128]{1,0:T(2,128)S(1)} %bitcast.18, ...), custom_call_target="tpu_custom_call" | custom-call | tf_op jit(solution)/shard_map/first/pallas_call | solution.py:376
  48.4 19.3 %all_to_all.20 = f32[128,1,1408]{2,1,0:T(1,128)S(1)} all-to-all(f32[128,1,1408]{2,1,0:T(1,128)S(1)} %bitcast.12), channel_id=1, replica_groups=mesh['grp'=4,'ring'=16,'core'=2] {'grp','ring','core'}, dimensions={0} | all-to-all | bytes 1441792 | tf_op jit(solution)/shard_map/all_to_all | solution.py:388
  67.7 0.9 owner.1
  68.6 0.0 copy-start
  68.6 0.8 copy-done
  69.4 4.5 %all-to-all-start.2 = ((f32[128,1,1152]{2,1,0:T(1,128)}), f32[128,1,1152]{2,1,0:T(1,128)S(1)}, u32[]{:S(2)}, u32[]{:S(2)}) async-start(f32[128,1,1152]{2,1,0:T(1,128)} %bitcast.14), calls=%async_computation.2 | async-start | bytes 1179648 | tf_op jit(solution)/shard_map/all_to_all | solution.py:388
  73.9 7.9 %alpha.1.small_ref = f32[3,16,128]{2,1,0:T(8,128)S(1)} custom-call(f32[1408,128]{1,0:T(8,128)S(1)} %bitcast.11, f32[64,32,128]{2,1,0:T(8,128)S(1)} %all-to-all-done.mine_ref, f32[64,32,128]{2,1,0:T(8,128)S(1)} %collective-permute-done.other_ref), custom_call_target="tpu_custom_call" | custom-call | tf_op jit(solution)/shard_map/alpha/pallas_call | solution.py:376
  81.8 6.5 %all-to-all-done.2 = f32[128,1,1152]{2,1,0:T(1,128)S(1)} async-done(((f32[128,1,1152]{2,1,0:T(1,128)}), f32[128,1,1152]{2,1,0:T(1,128)S(1)}, u32[]{:S(2)}, u32[]{:S(2)}) %all-to-all-start.2) | async-done | bytes 589856 | tf_op jit(solution)/shard_map/all_to_all | solution.py:388
  88.3 11.5 %second.1 = (f32[2,64,40,128]{3,2,1,0:T(8,128)S(1)}, f32[2,16,256]{2,1,0:T(8,128)S(1)}) custom-call(s32[2,4]{1,0:T(2,128)S(1)} %bitcast.17, f32[64,32,128]{2,1,0:T(8,128)S(1)} %all-to-all-done.mine_ref, f32[64,32,128]{2,1,0:T(8,128)S(1)} %collective-permute-done.other_ref, f32[16,256]{1,0:T(8,128)S(1)} %copy-done.2, f32[2,128]{1,0:T(2,128)S(1)} %bitcast.19, ...), custom_call_target="tpu_custom_call" | custom-call | tf_op jit(solution)/shard_map/second/pallas_call | solution.py:376
  99.8 0.1 slice_bitcast_fusion
  99.9 1.0 collective-permute-start.1
  100.8 2.7 %collective-permute-done.1 = f32[64,40,128]{2,1,0:T(8,128)S(1)} collective-permute-done((f32[64,40,128]{2,1,0:T(8,128)S(1)}, f32[64,40,128]{2,1,0:T(8,128)S(1)}, u32[]{:S(2)}, u32[]{:S(2)}) %collective-permute-start.1) | collective-permute-done | bytes 1310752 | tf_op jit(solution)/shard_map/ppermute | solution.py:392
  103.5 0.1 bitcast_add_fusion
  103.6 25.3 %all_to_all.21.got_ref = f32[64,40,128]{2,1,0:T(8,128)S(1)} all-to-all(f32[64,40,128]{2,1,0:T(8,128)S(1)} %bitcast_add_fusion), channel_id=1, replica_groups=mesh['grp'=4,'ring'=16,'core'=2] {'grp','ring'}, dimensions={0} | all-to-all | bytes 2621440 | tf_op jit(solution)/shard_map/all_to_all | solution.py:440
  129.0 4.6 %last.1 = (f32[16,256]{1,0:T(8,128)}, f32[16,256]{1,0:T(8,128)}) custom-call(f32[64,40,128]{2,1,0:T(8,128)S(1)} %all_to_all.21.got_ref, f32[16,256]{1,0:T(8,128)S(1)} %copy-done.2, f32[2,128]{1,0:T(2,128)S(1)} %bitcast.20, f32[2,16,256]{2,1,0:T(8,128)S(1)} %get-tuple-element.19.keep_ref, f32[3,16,128]{2,1,0:T(8,128)S(1)} %alpha.1.small_ref), custom_call_target="tpu_custom_call" | custom-call | tf_op jit(solution)/shard_map/last/pallas_call | solution.py:376
Async XLA Ops:
  0.6 0.7 copy-start.1
  2.5 12.1 %copy-start.3 = (s32[4,2]{0,1:T(2,128)S(1)}, s32[4,2]{0,1:T(2,128)}, u32[]{:S(2)}) copy-start(s32[4,2]{0,1:T(2,128)} %param.7) | copy-start | bytes 100
  2.5 29.8 %all-to-all-start = ((f32[64,32,128]{2,1,0:T(8,128)}), f32[64,32,128]{2,1,0:T(8,128)S(1)}, u32[]{:S(2)}, u32[]{:S(2)}) async-start(f32[64,32,128]{2,1,0:T(8,128)} %pack.1), calls=%async_computation | async-start | bytes 2097152 | tf_op jit(solution)/shard_map/all_to_all | solution.py:401
  14.6 22.1 %copy-start.2 = (f32[16,256]{1,0:T(8,128)S(1)}, f32[16,256]{1,0:T(8,128)}, u32[]{:S(2)}) copy-start(f32[16,256]{1,0:T(8,128)} %right_ref.7) | copy-start | bytes 49156
  14.6 22.1 %copy-start.4 = (f32[256]{0:T(256)S(1)}, f32[256]{0:T(256)}, u32[]{:S(2)}) copy-start(f32[256]{0:T(256)} %param.5) | copy-start | bytes 3076
  32.2 4.5 %collective-permute-start = (f32[64,32,128]{2,1,0:T(8,128)S(1)}, f32[64,32,128]{2,1,0:T(8,128)S(1)}, u32[]{:S(2)}, u32[]{:S(2)}) collective-permute-start(f32[64,32,128]{2,1,0:T(8,128)S(1)} %all-to-all-done.mine_ref), channel_id=1, source_target_pairs={{0,1},{1,0},{2,3},{3,2},{4,5},{5,4},{6,7},{7,6},{8,9},{9,8},{10,11... | collective-permute-start | bytes 3145736 | tf_op jit(solution)/shard_map/ppermute | solution.py:392
  68.6 0.8 copy-start
  69.4 18.9 %all-to-all-start.2 = ((f32[128,1,1152]{2,1,0:T(1,128)}), f32[128,1,1152]{2,1,0:T(1,128)S(1)}, u32[]{:S(2)}, u32[]{:S(2)}) async-start(f32[128,1,1152]{2,1,0:T(1,128)} %bitcast.14), calls=%async_computation.2 | async-start | bytes 1179648 | tf_op jit(solution)/shard_map/all_to_all | solution.py:388
  99.9 3.6 %collective-permute-start.1 = (f32[64,40,128]{2,1,0:T(8,128)S(1)}, f32[64,40,128]{2,1,0:T(8,128)S(1)}, u32[]{:S(2)}, u32[]{:S(2)}) collective-permute-start(f32[64,40,128]{2,1,0:T(8,128)S(1)} %slice_bitcast_fusion), channel_id=1, source_target_pairs={{0,1},{1,0},{2,3},{3,2},{4,5},{5,4},{6,7},{7,6},{8,9},{9,8},{10,11... | collective-permute-start | bytes 3932168 | tf_op jit(solution)/shard_map/ppermute | solution.py:392

commit v4 on v3

--- a/solution.py
+++ b/solution.py
@@ -16,11 +16,11 @@
 N = 64
 J = 8
 ENDS = 8
-GATHER = 32
-OWN = 10
+REST = 64
+OWN = 9
 SLOT = 40
 GRAMS = 32
-R1_ROWS = 11
+R1_ROWS = 10
 G2_ROWS = 9
 F32 = jnp.float32
 BF16 = jnp.bfloat16
@@ -65,6 +65,28 @@
     return spread_sum(jnp.where(own_lanes(), jnp.concatenate([top, low], axis=0), 0.0))
 
 
+def diagonals():
+    lane = iota((S, D), 1)
+    return iota((S, D), 0) == (lane % S + lane // S) % S
+
+
+def opposite():
+    return (iota((S, D), 0) == iota((S, D), 1) + S // 2) & (iota((S, D), 1) < S // 2)
+
+
+def pack_symmetric(g):
+    return [
+        jnp.sum(jnp.where(keep, g, 0.0), axis=0, keepdims=True) for keep in (diagonals(), opposite())
+    ]
+
+
+def from_symmetric(row, rest, ref):
+    lower = jnp.where(diagonals(), jnp.broadcast_to(row, (S, D)), 0.0)
+    ref[...] = spread_sum(lower + jnp.where(opposite(), jnp.broadcast_to(rest, (S, D)), 0.0))
+    middle = iota((S, D), 0) == iota((S, D), 1) % S
+    ref[...] = ref[...] + jnp.where(middle, 0.0, small_t(ref[...]))
+
+
 def stack8(g):
     return jnp.concatenate([g] * 8, axis=0)
 
@@ -100,13 +122,6 @@
         factor = jnp.where(row == pivot, 0.0, work[:, pivot : pivot + 1])
         work = jnp.where(row == pivot, row_new, work - factor * row_new)
     return spread_sum(jnp.where((lane >= S) & (lane < 2 * S), work, 0.0))
-
-
-def gather_pack_kernel(right_ref, out_ref):
-    right = right_ref[...]
-    packed = jnp.concatenate([right[:, :D], right[:, D:]], axis=0)
-    for chip in range(N):
-        out_ref[chip] = packed
 
 
 def split(x):
@@ -175,7 +190,7 @@
     for half in range(2):
         chip = 2 * block + half
         for piece in by_core(mine_ref[chip], other_ref[chip]):
-            field += [piece[:S], piece[S:]]
+            field += [piece[:, :D], piece[:, D:]]
     return jnp.concatenate(field, axis=1)
 
 
@@ -223,7 +238,7 @@
 
 def first_kernel(
     list_ref, mine_ref, other_ref, right_ref, ridge_ref, high_hbm, low_hbm, out_ref,
-    high_ref, low_ref, gram_ref, sems,
+    high_ref, low_ref, gram_ref, own_ref, sems,
 ):
     fetch = fetch_parts(high_hbm, low_hbm, high_ref, low_ref, sems)
 
@@ -242,11 +257,12 @@
     for k in range(ENDS):
         ends = jnp.where(slot == k, list_ref[k % 2, k // 2].astype(F32), ends)
     own = [scaled[:, :D], scaled[:, D:], ends, jnp.zeros((D - 2 * S - ENDS, D), F32)]
-    out_ref[pl.ds(OWN, D, stride=R1_ROWS), :] = jnp.concatenate(own, axis=0).T
+    own_ref[...] = jnp.concatenate(own, axis=0).T
     curvature = multiply(fetch, high_ref, low_ref, field, put)
-    flat = flat_rows(widen(gram_ref[...] + curvature))
-    for i in range(2):
-        out_ref[pl.ds(ENDS + i, D, stride=R1_ROWS), :] = jnp.broadcast_to(flat[i : i + 1], (D, D))
+    row, rest = pack_symmetric(widen(gram_ref[...] + curvature))
+    out_ref[pl.ds(ENDS, D, stride=R1_ROWS), :] = jnp.broadcast_to(row, (D, D))
+    rest = jnp.concatenate([jnp.zeros((1, REST), F32), rest[:, : D - REST]], axis=1)
+    out_ref[pl.ds(OWN, D, stride=R1_ROWS), :] = own_ref[...] + rest
 
 
 def end_matches(ends, k):
@@ -285,15 +301,16 @@
         @pl.loop(0, N, step=4)
         def _(chip):
             pieces = [ref[chip + i] for i in range(4)]
-            wide = jnp.concatenate([half for p in pieces for half in (p[:S], p[S:])], axis=1)
+            wide = jnp.concatenate(pieces, axis=1)
             norm_ref[...] += gram(wide, wide)
 
-    curvature = []
-    for i in range(2):
-        part = got_ref[pl.ds(ENDS + i, D, stride=R1_ROWS), :]
-        curvature.append(jnp.sum(part, axis=0, keepdims=True))
+    row, rest = [
+        jnp.sum(got_ref[pl.ds(at, D, stride=R1_ROWS), :], axis=0, keepdims=True)
+        for at in (ENDS, OWN)
+    ]
+    rest = jnp.concatenate([rest[:, REST:], jnp.zeros((1, REST), F32)], axis=1)
     out_ref[0] = widen(norm_ref[...])
-    out_ref[1] = from_rows(jnp.concatenate(curvature, axis=0))
+    from_symmetric(row, rest, out_ref.at[1])
     out_ref[2] = gauss_solve(out_ref[1], out_ref[0])
 
 
@@ -340,8 +357,15 @@
             out_ref[side, chip, GRAMS:] = flat
 
 
+def inverse_kernel(small_ref, right_ref, inverse_ref, begun_ref):
+    unit = (iota((S, D), 0) == iota((S, D), 1) % S).astype(F32)
+    inverse_ref[...] = gauss_solve(small_ref[0], unit)
+    begun_ref[...] = mixed(small_ref[2], right_ref[...])
+
+
 def last_kernel(
-    got_ref, right_ref, ridge_ref, keep_ref, small_ref, solution_ref, residual_ref, gram_ref
+    got_ref, right_ref, ridge_ref, keep_ref, small_ref, inverse_ref, begun_ref,
+    solution_ref, residual_ref, gram_ref,
 ):
     total = got_ref[0]
     for chip in range(1, N):
@@ -352,14 +376,15 @@
     second = jnp.concatenate([total[:S], total[S : 2 * S]], axis=1) + ridge * residual
     for i in range(3):
         gram_ref[i] = from_rows(total[GRAMS + 2 * i : GRAMS + 2 * i + 2])
-    beta = gauss_solve(small_ref[0], gram_ref[0])
+    gram_ref[5] = small_mul(inverse_ref[...], gram_ref[0])
+    beta = gram_ref[5]
     gram_ref[3] = small_mul(gram_ref[1], beta)
     gram_ref[4] = small_mul(small_t(beta), small_mul(small_ref[1], beta))
     bent = gram_ref[2] + gram_ref[3] + small_t(gram_ref[3]) + gram_ref[4]
     last = gauss_solve(bent, gram_ref[0])
     direction = residual + mixed(beta, right)
     image_next = second + mixed(beta, image)
-    solution_ref[...] = mixed(small_ref[2], right) + mixed(last, direction)
+    solution_ref[...] = begun_ref[...] + mixed(last, direction)
     residual_ref[...] = residual - mixed(last, image_next)
 
 
@@ -395,7 +420,7 @@
 def local(right, ridge, tiles, tile_list):
     ridge = ridge.reshape(2, D)
     tile_list = tile_list.T
-    (packed,) = call(gather_pack_kernel, "pack", [(N, GATHER, D)], [HERE], (right,))
+    packed = jnp.broadcast_to(right, (N, S, 2 * D))
     later_list, packed = lax.optimization_barrier((tile_list, packed))
     staged = stage(tiles, later_list)
     mine = lax.all_to_all(packed, CHIPS, 0, 0)
@@ -408,7 +433,7 @@
         [(D * R1_ROWS, D)],
         [SCALARS] + [HERE] * 4 + [THERE] * 2,
         (tile_list, mine, other, right, ridge, *staged),
-        [*STAGED, pltpu.VMEM((S, S), F32), sems],
+        [*STAGED, pltpu.VMEM((S, S), F32), pltpu.VMEM((D, D), F32), sems],
         48,
     )
     got = exchange_rows(sent, R1_ROWS)
@@ -437,15 +462,21 @@
         [*STAGED, pltpu.VMEM((3, S, S), F32), sems],
         48,
     )
-    got = lax.all_to_all(sent[0] + swap(sent[1]), CHIPS, 0, 0)
+    sent = sent[0] + swap(sent[1])
+    later, sent = lax.optimization_barrier((small, sent))
+    inverse, begun = call(
+        inverse_kernel, "inverse", [(S, D), (S, 2 * D)], [HERE] * 2, (later, right)
+    )
+    got = lax.all_to_all(sent, CHIPS, 0, 0)
+    got, inverse, begun = lax.optimization_barrier((got, inverse, begun))
     return tuple(
         call(
             last_kernel,
             "last",
             [(S, 2 * D)] * 2,
-            [HERE] * 5,
-            (got, right, ridge, keep, small),
-            [pltpu.VMEM((5, S, D), F32)],
+            [HERE] * 7,
+            (got, right, ridge, keep, small, inverse, begun),
+            [pltpu.VMEM((6, S, D), F32)],
         )
     )
 

time: 134 us -> 134 us (level)
  blocking collectives: 44.6 us -> 18.6 us
  waiting for transfers between devices: 16.2 us -> 35.5 us
  starting transfers between devices: 19.7 us -> 24.5 us
    all_to_all x1 -> x0, blocking collectives: 25.3 us -> none  [local(): got = lax.all_to_all(sent[0] + swap(sent[1]), CHIPS, 0, 0)]
    all_to_all x0 -> x1, waiting for transfers between devices: none -> 19.3 us  [local(): got = lax.all_to_all(sent, CHIPS, 0, 0)]
    all_to_all x0 -> x1, starting transfers between devices: none -> 4.76 us  [local(): got = lax.all_to_all(sent, CHIPS, 0, 0)]
    broadcast_in_dim x0 -> x1, local copies, waits for them, and re-layouts: none -> 1.83 us  [local(): packed = jnp.broadcast_to(right, (N, S, 2 * D))]
  transfers between devices with their start and end apart: 4 -> 5, of which waited for: 4 -> 5; matrix products, arithmetic and copies ran while one was open for 0% -> 0% of each run, Pallas kernels for 16% -> 17%
where the time goes in v4:
time: 134 us; the launch traced here: 133 us
  Pallas kernels  49.7 us (37%)
  waiting for transfers between devices  35.5 us (26%)
  starting transfers between devices  24.5 us (18%)
  blocking collectives  18.6 us (14%)
  local copies, waits for them, and re-layouts  2.75 us (2%)
    pallas_call x6, Pallas kernels, call(): pl.pallas_call(kernel, out_shape=[jax.ShapeDtypeStruct(shape, F32) for sh...  36.9 us
    all_to_all x1, waiting for transfers between devices, local(): got = lax.all_to_all(sent, CHIPS, 0, 0)  19.3 us
    all_to_all x1, blocking collectives, exchange_rows(): lax.all_to_all(x.reshape(D, 1, rows * D), ALL, 0, 0).reshape(D * rows, D)  18.6 us
    pallas_call x1, Pallas kernels, stage(): pl.pallas_call(stage_kernel, out_shape=[pltpu.HBM((4, B, B), BF16)] * 2,...  12.8 us
    all_to_all x1, starting transfers between devices, local(): mine = lax.all_to_all(packed, CHIPS, 0, 0)  12.1 us
    all_to_all x1, waiting for transfers between devices, exchange_rows(): lax.all_to_all(x.reshape(D, 1, rows * D), ALL, 0, 0).reshape(D * rows, D)  6.39 us
    ppermute x2, waiting for transfers between devices, swap(): return lax.ppermute(x, 'core', [(0, 1), (1, 0)])  4.95 us
    all_to_all x1, waiting for transfers between devices, local(): mine = lax.all_to_all(packed, CHIPS, 0, 0)  4.82 us
  transfers between devices with their start and end apart: 5, of which 5 were waited for; matrix products, arithmetic and copies ran while one was open for 0% of the time, Pallas kernels for 17%

profile of v4, /device:TPU:1, one launch (start us, length us, event | category | flops | bytes accessed | tf_op | source)
XLA Modules:
  0.0 132.9 jit_solution(6291359749819247583)
XLA Ops:
  0.6 1.8 %broadcast_in_dim.3 = f32[64,16,256]{2,1,0:T(8,128)} broadcast(f32[16,256]{1,0:T(8,128)} %right_ref.7), dimensions={1,2} | broadcast | bytes 1064960 | tf_op jit(solution)/shard_map/broadcast_in_dim | solution.py:423
  2.5 0.0 copy-start.2
  2.5 12.1 %all-to-all-start = ((f32[64,16,256]{2,1,0:T(8,128)}), f32[64,16,256]{2,1,0:T(8,128)S(1)}, u32[]{:S(2)}, u32[]{:S(2)}) async-start(f32[64,16,256]{2,1,0:T(8,128)} %broadcast_in_dim.3), calls=%async_computation | async-start | bytes 2097152 | tf_op jit(solution)/shard_map/all_to_all | solution.py:426
  14.6 0.0 copy-done.2
  14.6 0.0 copy-start.1
  14.6 0.0 copy-start.3
  14.6 12.8 %stage.1 = (bf16[4,1024,1024]{2,1,0:T(8,128)(2,1)}, bf16[4,1024,1024]{2,1,0:T(8,128)(2,1)}) custom-call(s32[2,4]{1,0:T(2,128)S(1)} %bitcast.15, f32[4,1024,1024]{2,1,0:T(8,128)} %tiles_ref.1), custom_call_target="tpu_custom_call" | custom-call | tf_op jit(solution)/shard_map/stage/pallas_call | solution.py:166
  27.4 4.8 %all-to-all-done.mine_ref = f32[64,16,256]{2,1,0:T(8,128)S(1)} async-done(((f32[64,16,256]{2,1,0:T(8,128)}), f32[64,16,256]{2,1,0:T(8,128)S(1)}, u32[]{:S(2)}, u32[]{:S(2)}) %all-to-all-start) | async-done | bytes 1048608 | tf_op jit(solution)/shard_map/all_to_all | solution.py:426
  32.2 2.2 %collective-permute-start = (f32[64,16,256]{2,1,0:T(8,128)S(1)}, f32[64,16,256]{2,1,0:T(8,128)S(1)}, u32[]{:S(2)}, u32[]{:S(2)}) collective-permute-start(f32[64,16,256]{2,1,0:T(8,128)S(1)} %all-to-all-done.mine_ref), channel_id=1, source_target_pairs={{0,1},{1,0},{2,3},{3,2},{4,5},{5,4},{6,7},{7,6},{8,9},{9,8},{10,11... | collective-permute-start | bytes 3145736 | tf_op jit(solution)/shard_map/ppermute | solution.py:417
  34.4 2.3 %collective-permute-done.other_ref = f32[64,16,256]{2,1,0:T(8,128)S(1)} collective-permute-done((f32[64,16,256]{2,1,0:T(8,128)S(1)}, f32[64,16,256]{2,1,0:T(8,128)S(1)}, u32[]{:S(2)}, u32[]{:S(2)}) %collective-permute-start) | collective-permute-done | bytes 1048608 | tf_op jit(solution)/shard_map/ppermute | solution.py:417
  36.7 0.0 copy-done.1
  36.7 0.0 copy-done.3
  36.7 11.8 %first.1 = f32[1280,128]{1,0:T(8,128)S(1)} custom-call(s32[2,4]{1,0:T(2,128)S(1)} %bitcast.16, f32[64,16,256]{2,1,0:T(8,128)S(1)} %all-to-all-done.mine_ref, f32[64,16,256]{2,1,0:T(8,128)S(1)} %collective-permute-done.other_ref, f32[16,256]{1,0:T(8,128)S(1)} %copy-done.1, f32[2,128]{1,0:T(2,128)S(1)} %bitcast.18, ...), custom_call_target="tpu_custom_call" | custom-call | tf_op jit(solution)/shard_map/first/pallas_call | solution.py:401
  48.5 18.6 %all_to_all.20 = f32[128,1,1280]{2,1,0:T(1,128)S(1)} all-to-all(f32[128,1,1280]{2,1,0:T(1,128)S(1)} %bitcast.12), channel_id=1, replica_groups=mesh['grp'=4,'ring'=16,'core'=2] {'grp','ring','core'}, dimensions={0} | all-to-all | bytes 1310720 | tf_op jit(solution)/shard_map/all_to_all | solution.py:413
  67.1 0.9 owner.1
  68.0 0.0 copy-start
  68.0 0.8 copy-done
  68.8 4.5 %all-to-all-start.2 = ((f32[128,1,1152]{2,1,0:T(1,128)}), f32[128,1,1152]{2,1,0:T(1,128)S(1)}, u32[]{:S(2)}, u32[]{:S(2)}) async-start(f32[128,1,1152]{2,1,0:T(1,128)} %bitcast.14), calls=%async_computation.2 | async-start | bytes 1179648 | tf_op jit(solution)/shard_map/all_to_all | solution.py:413
  73.3 8.0 %alpha.1.small_ref = f32[3,16,128]{2,1,0:T(8,128)S(1)} custom-call(f32[1280,128]{1,0:T(8,128)S(1)} %bitcast.11, f32[64,16,256]{2,1,0:T(8,128)S(1)} %all-to-all-done.mine_ref, f32[64,16,256]{2,1,0:T(8,128)S(1)} %collective-permute-done.other_ref), custom_call_target="tpu_custom_call" | custom-call | tf_op jit(solution)/shard_map/alpha/pallas_call | solution.py:401
  81.3 6.4 %all-to-all-done.2 = f32[128,1,1152]{2,1,0:T(1,128)S(1)} async-done(((f32[128,1,1152]{2,1,0:T(1,128)}), f32[128,1,1152]{2,1,0:T(1,128)S(1)}, u32[]{:S(2)}, u32[]{:S(2)}) %all-to-all-start.2) | async-done | bytes 589856 | tf_op jit(solution)/shard_map/all_to_all | solution.py:413
  87.7 11.5 %second.1 = (f32[2,64,40,128]{3,2,1,0:T(8,128)S(1)}, f32[2,16,256]{2,1,0:T(8,128)S(1)}) custom-call(s32[2,4]{1,0:T(2,128)S(1)} %bitcast.17, f32[64,16,256]{2,1,0:T(8,128)S(1)} %all-to-all-done.mine_ref, f32[64,16,256]{2,1,0:T(8,128)S(1)} %collective-permute-done.other_ref, f32[16,256]{1,0:T(8,128)S(1)} %copy-done.1, f32[2,128]{1,0:T(2,128)S(1)} %bitcast.19, ...), custom_call_target="tpu_custom_call" | custom-call | tf_op jit(solution)/shard_map/second/pallas_call | solution.py:401
  99.2 0.1 slice_bitcast_fusion
  99.3 0.9 collective-permute-start.1
  100.3 2.7 %collective-permute-done.1 = f32[64,40,128]{2,1,0:T(8,128)S(1)} collective-permute-done((f32[64,40,128]{2,1,0:T(8,128)S(1)}, f32[64,40,128]{2,1,0:T(8,128)S(1)}, u32[]{:S(2)}, u32[]{:S(2)}) %collective-permute-start.1) | collective-permute-done | bytes 1310752 | tf_op jit(solution)/shard_map/ppermute | solution.py:417
  102.9 1.2 bitcast_add_fusion
  104.1 4.8 %all-to-all-start.3 = ((f32[64,40,128]{2,1,0:T(8,128)}), f32[64,40,128]{2,1,0:T(8,128)S(1)}, u32[]{:S(2)}, u32[]{:S(2)}) async-start(f32[64,40,128]{2,1,0:T(8,128)} %bitcast_add_fusion), calls=%async_computation.3 | async-start | bytes 2621440 | tf_op jit(solution)/shard_map/all_to_all | solution.py:470
  108.9 1.4 %inverse.1 = (f32[16,128]{1,0:T(8,128)S(1)}, f32[16,256]{1,0:T(8,128)S(1)}) custom-call(f32[3,16,128]{2,1,0:T(8,128)S(1)} %alpha.1.small_ref, f32[16,256]{1,0:T(8,128)S(1)} %copy-done.1), custom_call_target="tpu_custom_call" | custom-call | tf_op jit(solution)/shard_map/inverse/pallas_call | solution.py:401
  110.3 19.3 %all-to-all-done.3.got_ref = f32[64,40,128]{2,1,0:T(8,128)S(1)} async-done(((f32[64,40,128]{2,1,0:T(8,128)}), f32[64,40,128]{2,1,0:T(8,128)S(1)}, u32[]{:S(2)}, u32[]{:S(2)}) %all-to-all-start.3) | async-done | bytes 1310752 | tf_op jit(solution)/shard_map/all_to_all | solution.py:470
  129.7 3.3 %last.1 = (f32[16,256]{1,0:T(8,128)}, f32[16,256]{1,0:T(8,128)}) custom-call(f32[64,40,128]{2,1,0:T(8,128)S(1)} %all-to-all-done.3.got_ref, f32[16,256]{1,0:T(8,128)S(1)} %copy-done.1, f32[2,128]{1,0:T(2,128)S(1)} %bitcast.20, f32[2,16,256]{2,1,0:T(8,128)S(1)} %get-tuple-element.31.keep_ref, f32[3,16,128]{2,1,0:T(8,128)S(1)} %alpha.1.small_ref, ...), custom_call_target="tpu_custom_call" | custom-call | tf_op jit(solution)/shard_map/last/pallas_call | solution.py:401
Async XLA Ops:
  2.5 12.1 %copy-start.2 = (s32[4,2]{0,1:T(2,128)S(1)}, s32[4,2]{0,1:T(2,128)}, u32[]{:S(2)}) copy-start(s32[4,2]{0,1:T(2,128)} %param.7) | copy-start | bytes 100
  2.5 29.8 %all-to-all-start = ((f32[64,16,256]{2,1,0:T(8,128)}), f32[64,16,256]{2,1,0:T(8,128)S(1)}, u32[]{:S(2)}, u32[]{:S(2)}) async-start(f32[64,16,256]{2,1,0:T(8,128)} %broadcast_in_dim.3), calls=%async_computation | async-start | bytes 2097152 | tf_op jit(solution)/shard_map/all_to_all | solution.py:426
  14.6 22.1 %copy-start.1 = (f32[16,256]{1,0:T(8,128)S(1)}, f32[16,256]{1,0:T(8,128)}, u32[]{:S(2)}) copy-start(f32[16,256]{1,0:T(8,128)} %right_ref.7) | copy-start | bytes 49156
  14.6 22.1 %copy-start.3 = (f32[256]{0:T(256)S(1)}, f32[256]{0:T(256)}, u32[]{:S(2)}) copy-start(f32[256]{0:T(256)} %param.5) | copy-start | bytes 3076
  32.2 4.5 %collective-permute-start = (f32[64,16,256]{2,1,0:T(8,128)S(1)}, f32[64,16,256]{2,1,0:T(8,128)S(1)}, u32[]{:S(2)}, u32[]{:S(2)}) collective-permute-start(f32[64,16,256]{2,1,0:T(8,128)S(1)} %all-to-all-done.mine_ref), channel_id=1, source_target_pairs={{0,1},{1,0},{2,3},{3,2},{4,5},{5,4},{6,7},{7,6},{8,9},{9,8},{10,11... | collective-permute-start | bytes 3145736 | tf_op jit(solution)/shard_map/ppermute | solution.py:417
  68.0 0.8 copy-start
  68.8 18.9 %all-to-all-start.2 = ((f32[128,1,1152]{2,1,0:T(1,128)}), f32[128,1,1152]{2,1,0:T(1,128)S(1)}, u32[]{:S(2)}, u32[]{:S(2)}) async-start(f32[128,1,1152]{2,1,0:T(1,128)} %bitcast.14), calls=%async_computation.2 | async-start | bytes 1179648 | tf_op jit(solution)/shard_map/all_to_all | solution.py:413
  99.3 3.6 %collective-permute-start.1 = (f32[64,40,128]{2,1,0:T(8,128)S(1)}, f32[64,40,128]{2,1,0:T(8,128)S(1)}, u32[]{:S(2)}, u32[]{:S(2)}) collective-permute-start(f32[64,40,128]{2,1,0:T(8,128)S(1)} %slice_bitcast_fusion), channel_id=1, source_target_pairs={{0,1},{1,0},{2,3},{3,2},{4,5},{5,4},{6,7},{7,6},{8,9},{9,8},{10,11... | collective-permute-start | bytes 3932168 | tf_op jit(solution)/shard_map/ppermute | solution.py:417
  104.1 25.5 %all-to-all-start.3 = ((f32[64,40,128]{2,1,0:T(8,128)}), f32[64,40,128]{2,1,0:T(8,128)S(1)}, u32[]{:S(2)}, u32[]{:S(2)}) async-start(f32[64,40,128]{2,1,0:T(8,128)} %bitcast_add_fusion), calls=%async_computation.3 | async-start | bytes 2621440 | tf_op jit(solution)/shard_map/all_to_all | solution.py:470

commit v5 on v4

--- a/solution.py
+++ b/solution.py
@@ -9,6 +9,7 @@
 
 CHIPS = ("grp", "ring")
 ALL = ("grp", "ring", "core")
+OWNERS = ("core", "grp", "ring")
 S = 16
 B = 1024
 NB = 32
@@ -280,8 +281,12 @@
     return parts[:, :D] + parts[:, D : 2 * D] + parts[:, 2 * D :]
 
 
+def quarter_owners(q, rows, row):
+    return pl.ds(rows * (q % 2 * N + q // 2) + row, NB, stride=2 * rows)
+
+
 def owner_kernel(got_ref, out_ref):
-    own = [got_ref[pl.ds(R1_ROWS * q + OWN, NB, stride=4 * R1_ROWS), :] for q in range(4)]
+    own = [got_ref[quarter_owners(q, R1_ROWS, OWN), :] for q in range(4)]
     total = jnp.concatenate([part[:, : 2 * S] for part in own], axis=1)
     ends = got_ref[pl.ds(OWN, D, stride=R1_ROWS), :][:, 2 * S : 2 * S + ENDS]
     for k in range(ENDS):
@@ -291,27 +296,32 @@
         out_ref[pl.ds(k, D, stride=G2_ROWS), :] = select(end_matches(ends, k), total)
     for q in range(4):
         own = [total[:, 2 * S * q : 2 * S * (q + 1)], jnp.zeros((NB, D - 2 * S), F32)]
-        out_ref[pl.ds(G2_ROWS * q + ENDS, NB, stride=4 * G2_ROWS), :] = jnp.concatenate(own, axis=1)
-
-
-def alpha_kernel(got_ref, mine_ref, other_ref, out_ref, norm_ref):
+        out_ref[quarter_owners(q, G2_ROWS, ENDS), :] = jnp.concatenate(own, axis=1)
+
+
+def norm_kernel(mine_ref, other_ref, out_ref, norm_ref):
     norm_ref[...] = jnp.zeros((S, S), F32)
     for ref in (mine_ref, other_ref):
 
         @pl.loop(0, N, step=4)
         def _(chip):
-            pieces = [ref[chip + i] for i in range(4)]
-            wide = jnp.concatenate(pieces, axis=1)
+            wide = jnp.concatenate([ref[chip + i] for i in range(4)], axis=1)
             norm_ref[...] += gram(wide, wide)
 
+    unit = (iota((S, D), 0) == iota((S, D), 1) % S).astype(F32)
+    out_ref[0] = widen(norm_ref[...])
+    out_ref[1] = gauss_solve(out_ref[0], unit)
+
+
+def alpha_kernel(got_ref, norm_ref, right_ref, out_ref, begun_ref):
     row, rest = [
         jnp.sum(got_ref[pl.ds(at, D, stride=R1_ROWS), :], axis=0, keepdims=True)
         for at in (ENDS, OWN)
     ]
     rest = jnp.concatenate([rest[:, REST:], jnp.zeros((1, REST), F32)], axis=1)
-    out_ref[0] = widen(norm_ref[...])
-    from_symmetric(row, rest, out_ref.at[1])
-    out_ref[2] = gauss_solve(out_ref[1], out_ref[0])
+    from_symmetric(row, rest, out_ref.at[0])
+    out_ref[1] = gauss_solve(out_ref[0], norm_ref[0])
+    begun_ref[...] = mixed(out_ref[1], right_ref[...])
 
 
 def second_kernel(
@@ -319,7 +329,7 @@
     out_ref, keep_ref, high_ref, low_ref, gram_ref, sems,
 ):
     fetch = fetch_parts(high_hbm, low_hbm, high_ref, low_ref, sems)
-    alpha_t = small_t(small_ref[2])[:, :S]
+    alpha_t = small_t(small_ref[1])[:, :S]
 
     def field(k):
         turned = got_ref[pl.ds(k, D, stride=G2_ROWS), :].T
@@ -357,14 +367,8 @@
             out_ref[side, chip, GRAMS:] = flat
 
 
-def inverse_kernel(small_ref, right_ref, inverse_ref, begun_ref):
-    unit = (iota((S, D), 0) == iota((S, D), 1) % S).astype(F32)
-    inverse_ref[...] = gauss_solve(small_ref[0], unit)
-    begun_ref[...] = mixed(small_ref[2], right_ref[...])
-
-
 def last_kernel(
-    got_ref, right_ref, ridge_ref, keep_ref, small_ref, inverse_ref, begun_ref,
+    got_ref, right_ref, ridge_ref, keep_ref, norm_ref, small_ref, begun_ref,
     solution_ref, residual_ref, gram_ref,
 ):
     total = got_ref[0]
@@ -376,10 +380,10 @@
     second = jnp.concatenate([total[:S], total[S : 2 * S]], axis=1) + ridge * residual
     for i in range(3):
         gram_ref[i] = from_rows(total[GRAMS + 2 * i : GRAMS + 2 * i + 2])
-    gram_ref[5] = small_mul(inverse_ref[...], gram_ref[0])
+    gram_ref[5] = small_mul(norm_ref[1], gram_ref[0])
     beta = gram_ref[5]
     gram_ref[3] = small_mul(gram_ref[1], beta)
-    gram_ref[4] = small_mul(small_t(beta), small_mul(small_ref[1], beta))
+    gram_ref[4] = small_mul(small_t(beta), small_mul(small_ref[0], beta))
     bent = gram_ref[2] + gram_ref[3] + small_t(gram_ref[3]) + gram_ref[4]
     last = gauss_solve(bent, gram_ref[0])
     direction = residual + mixed(beta, right)
@@ -410,7 +414,7 @@
 
 
 def exchange_rows(x, rows):
-    return lax.all_to_all(x.reshape(D, 1, rows * D), ALL, 0, 0).reshape(D * rows, D)
+    return lax.all_to_all(x.reshape(D, 1, rows * D), OWNERS, 0, 0).reshape(D * rows, D)
 
 
 def swap(x):
@@ -436,7 +440,17 @@
         [*STAGED, pltpu.VMEM((S, S), F32), pltpu.VMEM((D, D), F32), sems],
         48,
     )
+    later_mine, sent = lax.optimization_barrier((mine, sent))
+    (norm,) = call(
+        norm_kernel,
+        "norm",
+        [(2, S, D)],
+        [HERE] * 2,
+        (later_mine, other),
+        [pltpu.VMEM((S, S), F32)],
+    )
     got = exchange_rows(sent, R1_ROWS)
+    got, norm = lax.optimization_barrier((got, norm))
     (sent,) = call(
         owner_kernel,
         "owner",
@@ -444,13 +458,8 @@
         [HERE],
         (got,),
     )
-    (small,) = call(
-        alpha_kernel,
-        "alpha",
-        [(3, S, D)],
-        [HERE] * 3,
-        (got, mine, other),
-        [pltpu.VMEM((S, S), F32)],
+    small, begun = call(
+        alpha_kernel, "alpha", [(2, S, D), (S, 2 * D)], [HERE] * 3, (got, norm, right)
     )
     got = exchange_rows(sent, G2_ROWS)
     sent, keep = call(
@@ -462,20 +471,14 @@
         [*STAGED, pltpu.VMEM((3, S, S), F32), sems],
         48,
     )
-    sent = sent[0] + swap(sent[1])
-    later, sent = lax.optimization_barrier((small, sent))
-    inverse, begun = call(
-        inverse_kernel, "inverse", [(S, D), (S, 2 * D)], [HERE] * 2, (later, right)
-    )
-    got = lax.all_to_all(sent, CHIPS, 0, 0)
-    got, inverse, begun = lax.optimization_barrier((got, inverse, begun))
+    got = lax.all_to_all(sent[0] + swap(sent[1]), CHIPS, 0, 0)
     return tuple(
         call(
             last_kernel,
             "last",
             [(S, 2 * D)] * 2,
             [HERE] * 7,
-            (got, right, ridge, keep, small, inverse, begun),
+            (got, right, ridge, keep, norm, small, begun),
             [pltpu.VMEM((6, S, D), F32)],
         )
     )

time: 134 us -> 133 us (level)
  blocking collectives: 18.6 us -> 25.2 us
  waiting for transfers between devices: 35.5 us -> 29 us
    all_to_all x1, blocking collectives: 18.6 us -> 25.2 us  [local(): got = lax.all_to_all(sent[0] + swap(sent[1]), CHIPS, 0, 0)]
    all_to_all x2, waiting for transfers between devices: 25.7 us -> 19.4 us  [exchange_rows(): lax.all_to_all(x.reshape(D, 1, rows * D), OWNERS, 0, 0).reshape(D * rows, D)]
where the time goes in v5:
time: 133 us; the launch traced here: 132 us
  Pallas kernels  50.9 us (38%)
  waiting for transfers between devices  29 us (22%)
  blocking collectives  25.2 us (19%)
  starting transfers between devices  23.4 us (18%)
  local copies, waits for them, and re-layouts  2.75 us (2%)
    pallas_call x6, Pallas kernels, call(): pl.pallas_call(kernel, out_shape=[jax.ShapeDtypeStruct(shape, F32) for sh...  38 us
    all_to_all x1, blocking collectives, local(): got = lax.all_to_all(sent[0] + swap(sent[1]), CHIPS, 0, 0)  25.2 us
    all_to_all x2, waiting for transfers between devices, exchange_rows(): lax.all_to_all(x.reshape(D, 1, rows * D), OWNERS, 0, 0).reshape(D * rows, D)  19.4 us
    pallas_call x1, Pallas kernels, stage(): pl.pallas_call(stage_kernel, out_shape=[pltpu.HBM((4, B, B), BF16)] * 2,...  12.9 us
    all_to_all x1, starting transfers between devices, local(): mine = lax.all_to_all(packed, CHIPS, 0, 0)  12.1 us
    all_to_all x2, starting transfers between devices, exchange_rows(): lax.all_to_all(x.reshape(D, 1, rows * D), OWNERS, 0, 0).reshape(D * rows, D)  8.18 us
    ppermute x2, waiting for transfers between devices, swap(): return lax.ppermute(x, 'core', [(0, 1), (1, 0)])  4.95 us
    all_to_all x1, waiting for transfers between devices, local(): mine = lax.all_to_all(packed, CHIPS, 0, 0)  4.7 us
  transfers between devices with their start and end apart: 5, of which 5 were waited for; matrix products, arithmetic and copies ran while one was open for 0% of the time, Pallas kernels for 17%

profile of v5, /device:TPU:1, one launch (start us, length us, event | category | flops | bytes accessed | tf_op | source)
XLA Modules:
  0.0 132.1 jit_solution(17609657583153869704)
XLA Ops:
  0.6 1.8 %broadcast_in_dim.3 = f32[64,16,256]{2,1,0:T(8,128)} broadcast(f32[16,256]{1,0:T(8,128)} %right_ref.7), dimensions={1,2} | broadcast | bytes 1064960 | tf_op jit(solution)/shard_map/broadcast_in_dim | solution.py:427
  2.5 0.0 copy-start.2
  2.5 12.1 %all-to-all-start = ((f32[64,16,256]{2,1,0:T(8,128)}), f32[64,16,256]{2,1,0:T(8,128)S(1)}, u32[]{:S(2)}, u32[]{:S(2)}) async-start(f32[64,16,256]{2,1,0:T(8,128)} %broadcast_in_dim.3), calls=%async_computation | async-start | bytes 2097152 | tf_op jit(solution)/shard_map/all_to_all | solution.py:430
  14.6 0.0 copy-done.2
  14.6 0.0 copy-start.1
  14.6 0.0 copy-start.3
  14.6 12.9 %stage.1 = (bf16[4,1024,1024]{2,1,0:T(8,128)(2,1)}, bf16[4,1024,1024]{2,1,0:T(8,128)(2,1)}) custom-call(s32[2,4]{1,0:T(2,128)S(1)} %bitcast.14, f32[4,1024,1024]{2,1,0:T(8,128)} %tiles_ref.1), custom_call_target="tpu_custom_call" | custom-call | tf_op jit(solution)/shard_map/stage/pallas_call | solution.py:167
  27.5 4.7 %all-to-all-done.mine_ref = f32[64,16,256]{2,1,0:T(8,128)S(1)} async-done(((f32[64,16,256]{2,1,0:T(8,128)}), f32[64,16,256]{2,1,0:T(8,128)S(1)}, u32[]{:S(2)}, u32[]{:S(2)}) %all-to-all-start) | async-done | bytes 1048608 | tf_op jit(solution)/shard_map/all_to_all | solution.py:430
  32.2 2.2 %collective-permute-start = (f32[64,16,256]{2,1,0:T(8,128)S(1)}, f32[64,16,256]{2,1,0:T(8,128)S(1)}, u32[]{:S(2)}, u32[]{:S(2)}) collective-permute-start(f32[64,16,256]{2,1,0:T(8,128)S(1)} %all-to-all-done.mine_ref), channel_id=1, source_target_pairs={{0,1},{1,0},{2,3},{3,2},{4,5},{5,4},{6,7},{7,6},{8,9},{9,8},{10,11... | collective-permute-start | bytes 3145736 | tf_op jit(solution)/shard_map/ppermute | solution.py:421
  34.4 2.3 %collective-permute-done.other_ref = f32[64,16,256]{2,1,0:T(8,128)S(1)} collective-permute-done((f32[64,16,256]{2,1,0:T(8,128)S(1)}, f32[64,16,256]{2,1,0:T(8,128)S(1)}, u32[]{:S(2)}, u32[]{:S(2)}) %collective-permute-start) | collective-permute-done | bytes 1048608 | tf_op jit(solution)/shard_map/ppermute | solution.py:421
  36.7 0.0 copy-done.1
  36.7 0.0 copy-done.3
  36.7 12.6 %first.1 = f32[1280,128]{1,0:T(8,128)} custom-call(s32[2,4]{1,0:T(2,128)S(1)} %bitcast.15, f32[64,16,256]{2,1,0:T(8,128)S(1)} %all-to-all-done.mine_ref, f32[64,16,256]{2,1,0:T(8,128)S(1)} %collective-permute-done.other_ref, f32[16,256]{1,0:T(8,128)S(1)} %copy-done.1, f32[2,128]{1,0:T(2,128)S(1)} %bitcast.17, ...), custom_call_target="tpu_custom_call" | custom-call | tf_op jit(solution)/shard_map/first/pallas_call | solution.py:405
  49.3 3.8 %all-to-all-start.1 = ((f32[128,1,1280]{2,1,0:T(1,128)}), f32[128,1,1280]{2,1,0:T(1,128)S(1)}, u32[]{:S(2)}, u32[]{:S(2)}) async-start(f32[128,1,1280]{2,1,0:T(1,128)} %bitcast.2), calls=%async_computation.1 | async-start | bytes 1310720 | tf_op jit(solution)/shard_map/all_to_all | solution.py:417
  53.1 7.7 %norm.1.norm_ref = f32[2,16,128]{2,1,0:T(8,128)S(1)} custom-call(f32[64,16,256]{2,1,0:T(8,128)S(1)} %all-to-all-done.mine_ref, f32[64,16,256]{2,1,0:T(8,128)S(1)} %collective-permute-done.other_ref), custom_call_target="tpu_custom_call" | custom-call | tf_op jit(solution)/shard_map/norm/pallas_call | solution.py:405
  60.8 7.2 %all-to-all-done.1 = f32[128,1,1280]{2,1,0:T(1,128)S(1)} async-done(((f32[128,1,1280]{2,1,0:T(1,128)}), f32[128,1,1280]{2,1,0:T(1,128)S(1)}, u32[]{:S(2)}, u32[]{:S(2)}) %all-to-all-start.1) | async-done | bytes 655392 | tf_op jit(solution)/shard_map/all_to_all | solution.py:417
  68.1 0.9 owner.1
  69.0 0.0 copy-start
  69.0 0.8 copy-done
  69.8 4.4 %all-to-all-start.2 = ((f32[128,1,1152]{2,1,0:T(1,128)}), f32[128,1,1152]{2,1,0:T(1,128)S(1)}, u32[]{:S(2)}, u32[]{:S(2)}) async-start(f32[128,1,1152]{2,1,0:T(1,128)} %bitcast.13), calls=%async_computation.2 | async-start | bytes 1179648 | tf_op jit(solution)/shard_map/all_to_all | solution.py:417
  74.2 2.1 %alpha.1 = (f32[2,16,128]{2,1,0:T(8,128)S(1)}, f32[16,256]{1,0:T(8,128)S(1)}) custom-call(f32[1280,128]{1,0:T(8,128)S(1)} %bitcast.11, f32[2,16,128]{2,1,0:T(8,128)S(1)} %norm.1.norm_ref, f32[16,256]{1,0:T(8,128)S(1)} %copy-done.1), custom_call_target="tpu_custom_call" | custom-call | tf_op jit(solution)/shard_map/alpha/pallas_call | solution.py:405
  76.2 12.1 %all-to-all-done.2 = f32[128,1,1152]{2,1,0:T(1,128)S(1)} async-done(((f32[128,1,1152]{2,1,0:T(1,128)}), f32[128,1,1152]{2,1,0:T(1,128)S(1)}, u32[]{:S(2)}, u32[]{:S(2)}) %all-to-all-start.2) | async-done | bytes 589856 | tf_op jit(solution)/shard_map/all_to_all | solution.py:417
  88.4 11.5 %second.1 = (f32[2,64,40,128]{3,2,1,0:T(8,128)S(1)}, f32[2,16,256]{2,1,0:T(8,128)S(1)}) custom-call(s32[2,4]{1,0:T(2,128)S(1)} %bitcast.16, f32[64,16,256]{2,1,0:T(8,128)S(1)} %all-to-all-done.mine_ref, f32[64,16,256]{2,1,0:T(8,128)S(1)} %collective-permute-done.other_ref, f32[16,256]{1,0:T(8,128)S(1)} %copy-done.1, f32[2,128]{1,0:T(2,128)S(1)} %bitcast.18, ...), custom_call_target="tpu_custom_call" | custom-call | tf_op jit(solution)/shard_map/second/pallas_call | solution.py:405
  99.9 0.1 slice_bitcast_fusion
  99.9 0.9 collective-permute-start.1
  100.8 2.7 %collective-permute-done.1 = f32[64,40,128]{2,1,0:T(8,128)S(1)} collective-permute-done((f32[64,40,128]{2,1,0:T(8,128)S(1)}, f32[64,40,128]{2,1,0:T(8,128)S(1)}, u32[]{:S(2)}, u32[]{:S(2)}) %collective-permute-start.1) | collective-permute-done | bytes 1310752 | tf_op jit(solution)/shard_map/ppermute | solution.py:421
  103.5 0.1 bitcast_add_fusion
  103.6 25.2 %all_to_all.20.got_ref = f32[64,40,128]{2,1,0:T(8,128)S(1)} all-to-all(f32[64,40,128]{2,1,0:T(8,128)S(1)} %bitcast_add_fusion), channel_id=1, replica_groups=mesh['grp'=4,'ring'=16,'core'=2] {'grp','ring'}, dimensions={0} | all-to-all | bytes 2621440 | tf_op jit(solution)/shard_map/all_to_all | solution.py:474
  128.8 3.3 %last.1 = (f32[16,256]{1,0:T(8,128)}, f32[16,256]{1,0:T(8,128)}) custom-call(f32[64,40,128]{2,1,0:T(8,128)S(1)} %all_to_all.20.got_ref, f32[16,256]{1,0:T(8,128)S(1)} %copy-done.1, f32[2,128]{1,0:T(2,128)S(1)} %bitcast.19, f32[2,16,256]{2,1,0:T(8,128)S(1)} %get-tuple-element.30.keep_ref, f32[2,16,128]{2,1,0:T(8,128)S(1)} %norm.1.norm_ref, ...), custom_call_target="tpu_custom_call" | custom-call | tf_op jit(solution)/shard_map/last/pallas_call | solution.py:405
Async XLA Ops:
  2.5 12.1 %copy-start.2 = (s32[4,2]{0,1:T(2,128)S(1)}, s32[4,2]{0,1:T(2,128)}, u32[]{:S(2)}) copy-start(s32[4,2]{0,1:T(2,128)} %param.7) | copy-start | bytes 100
  2.5 29.8 %all-to-all-start = ((f32[64,16,256]{2,1,0:T(8,128)}), f32[64,16,256]{2,1,0:T(8,128)S(1)}, u32[]{:S(2)}, u32[]{:S(2)}) async-start(f32[64,16,256]{2,1,0:T(8,128)} %broadcast_in_dim.3), calls=%async_computation | async-start | bytes 2097152 | tf_op jit(solution)/shard_map/all_to_all | solution.py:430
  14.6 22.1 %copy-start.1 = (f32[16,256]{1,0:T(8,128)S(1)}, f32[16,256]{1,0:T(8,128)}, u32[]{:S(2)}) copy-start(f32[16,256]{1,0:T(8,128)} %right_ref.7) | copy-start | bytes 49156
  14.6 22.1 %copy-start.3 = (f32[256]{0:T(256)S(1)}, f32[256]{0:T(256)}, u32[]{:S(2)}) copy-start(f32[256]{0:T(256)} %param.5) | copy-start | bytes 3076
  32.2 4.5 %collective-permute-start = (f32[64,16,256]{2,1,0:T(8,128)S(1)}, f32[64,16,256]{2,1,0:T(8,128)S(1)}, u32[]{:S(2)}, u32[]{:S(2)}) collective-permute-start(f32[64,16,256]{2,1,0:T(8,128)S(1)} %all-to-all-done.mine_ref), channel_id=1, source_target_pairs={{0,1},{1,0},{2,3},{3,2},{4,5},{5,4},{6,7},{7,6},{8,9},{9,8},{10,11... | collective-permute-start | bytes 3145736 | tf_op jit(solution)/shard_map/ppermute | solution.py:421
  49.3 18.8 %all-to-all-start.1 = ((f32[128,1,1280]{2,1,0:T(1,128)}), f32[128,1,1280]{2,1,0:T(1,128)S(1)}, u32[]{:S(2)}, u32[]{:S(2)}) async-start(f32[128,1,1280]{2,1,0:T(1,128)} %bitcast.2), calls=%async_computation.1 | async-start | bytes 1310720 | tf_op jit(solution)/shard_map/all_to_all | solution.py:417
  69.0 0.8 copy-start
  69.8 18.6 %all-to-all-start.2 = ((f32[128,1,1152]{2,1,0:T(1,128)}), f32[128,1,1152]{2,1,0:T(1,128)S(1)}, u32[]{:S(2)}, u32[]{:S(2)}) async-start(f32[128,1,1152]{2,1,0:T(1,128)} %bitcast.13), calls=%async_computation.2 | async-start | bytes 1179648 | tf_op jit(solution)/shard_map/all_to_all | solution.py:417
  99.9 3.5 %collective-permute-start.1 = (f32[64,40,128]{2,1,0:T(8,128)S(1)}, f32[64,40,128]{2,1,0:T(8,128)S(1)}, u32[]{:S(2)}, u32[]{:S(2)}) collective-permute-start(f32[64,40,128]{2,1,0:T(8,128)S(1)} %slice_bitcast_fusion), channel_id=1, source_target_pairs={{0,1},{1,0},{2,3},{3,2},{4,5},{5,4},{6,7},{7,6},{8,9},{9,8},{10,11... | collective-permute-start | bytes 3932168 | tf_op jit(solution)/shard_map/ppermute | solution.py:421

commit v6 on v5

--- a/solution.py
+++ b/solution.py
@@ -19,7 +19,7 @@
 ENDS = 8
 REST = 64
 OWN = 9
-SLOT = 40
+SLOT = 36
 GRAMS = 32
 R1_ROWS = 10
 G2_ROWS = 9
@@ -300,16 +300,22 @@
 
 
 def norm_kernel(mine_ref, other_ref, out_ref, norm_ref):
-    norm_ref[...] = jnp.zeros((S, S), F32)
+    norm_ref[...] = jnp.zeros((3 * S, 3 * S), F32)
     for ref in (mine_ref, other_ref):
 
-        @pl.loop(0, N, step=4)
+        @pl.loop(0, N, step=8)
         def _(chip):
-            wide = jnp.concatenate([ref[chip + i] for i in range(4)], axis=1)
-            norm_ref[...] += gram(wide, wide)
-
+            wide = jnp.concatenate([ref[chip + i] for i in range(8)], axis=1)
+            high, rest = split(wide)
+            low = (wide - high.astype(F32) - rest.astype(F32)).astype(BF16)
+            parts = jnp.concatenate([high, rest, low], axis=0)
+            norm_ref[...] += lax.dot_general(parts, parts, NT, preferred_element_type=F32)
+
+    norm = norm_ref[...]
+    norm = norm[:S] + norm[S : 2 * S] + norm[2 * S :]
+    norm = norm[:, :S] + norm[:, S : 2 * S] + norm[:, 2 * S :]
     unit = (iota((S, D), 0) == iota((S, D), 1) % S).astype(F32)
-    out_ref[0] = widen(norm_ref[...])
+    out_ref[0] = widen(norm)
     out_ref[1] = gauss_solve(out_ref[0], unit)
 
 
@@ -344,9 +350,9 @@
         for q in range(4):
             chip, side = 2 * block + q // 2, (q % 2 + core) % 2
             for j in range(2):
-                rows = slice(j * S, (j + 1) * S)
+                rows = pl.ds(chip * SLOT + j * S, S)
                 lanes = slice((2 * q + j) * D, (2 * q + j + 1) * D)
-                out_ref[side, chip, rows] = out_ref[side, chip, rows] + value[:, lanes]
+                out_ref[side, rows, :] = out_ref[side, rows, :] + value[:, lanes]
 
     right = right_ref[...]
     ridge = jnp.concatenate([ridge_ref[0:1], ridge_ref[1:2]], axis=1)
@@ -356,36 +362,32 @@
     keep_ref[0] = residual
     keep_ref[1] = image
     gram_ref[0] = gram(residual, residual)
-    gram_ref[1] = gram(residual, image)
-    gram_ref[2] = gram(residual, ridge * residual)
-    gram_ref[2] += multiply(fetch, high_ref, low_ref, field, put)
-    flat = jnp.concatenate(
-        [flat_rows(widen(gram_ref[i])) for i in range(3)] + [jnp.zeros((2, D), F32)], axis=0
-    )
+    gram_ref[1] = gram(residual, ridge * residual)
+    gram_ref[1] += multiply(fetch, high_ref, low_ref, field, put)
+    flat = jnp.concatenate([flat_rows(widen(gram_ref[i])) for i in range(2)], axis=0)
     for side in range(2):
         for chip in range(N):
-            out_ref[side, chip, GRAMS:] = flat
+            out_ref[side, chip * SLOT + GRAMS : (chip + 1) * SLOT, :] = flat
 
 
 def last_kernel(
     got_ref, right_ref, ridge_ref, keep_ref, norm_ref, small_ref, begun_ref,
     solution_ref, residual_ref, gram_ref,
 ):
-    total = got_ref[0]
-    for chip in range(1, N):
-        total = total + got_ref[chip]
+    total = got_ref[: 2 * SLOT]
+    for chip in range(2, N, 2):
+        total = total + got_ref[chip * SLOT : (chip + 2) * SLOT]
+    total = total[:SLOT] + total[SLOT:]
     right = right_ref[...]
     residual, image = keep_ref[0], keep_ref[1]
     ridge = jnp.concatenate([ridge_ref[0:1], ridge_ref[1:2]], axis=1)
     second = jnp.concatenate([total[:S], total[S : 2 * S]], axis=1) + ridge * residual
-    for i in range(3):
+    for i in range(2):
         gram_ref[i] = from_rows(total[GRAMS + 2 * i : GRAMS + 2 * i + 2])
-    gram_ref[5] = small_mul(norm_ref[1], gram_ref[0])
-    beta = gram_ref[5]
-    gram_ref[3] = small_mul(gram_ref[1], beta)
-    gram_ref[4] = small_mul(small_t(beta), small_mul(small_ref[0], beta))
-    bent = gram_ref[2] + gram_ref[3] + small_t(gram_ref[3]) + gram_ref[4]
-    last = gauss_solve(bent, gram_ref[0])
+    gram_ref[2] = small_mul(norm_ref[1], gram_ref[0])
+    beta = gram_ref[2]
+    gram_ref[3] = small_mul(small_t(beta), small_mul(small_ref[0], beta))
+    last = gauss_solve(gram_ref[1] - gram_ref[3], gram_ref[0])
     direction = residual + mixed(beta, right)
     image_next = second + mixed(beta, image)
     solution_ref[...] = begun_ref[...] + mixed(last, direction)
@@ -440,6 +442,14 @@
         [*STAGED, pltpu.VMEM((S, S), F32), pltpu.VMEM((D, D), F32), sems],
         48,
     )
+    got = exchange_rows(sent, R1_ROWS)
+    (sent,) = call(
+        owner_kernel,
+        "owner",
+        [(D * G2_ROWS, D)],
+        [HERE],
+        (got,),
+    )
     later_mine, sent = lax.optimization_barrier((mine, sent))
     (norm,) = call(
         norm_kernel,
@@ -447,16 +457,7 @@
         [(2, S, D)],
         [HERE] * 2,
         (later_mine, other),
-        [pltpu.VMEM((S, S), F32)],
-    )
-    got = exchange_rows(sent, R1_ROWS)
-    got, norm = lax.optimization_barrier((got, norm))
-    (sent,) = call(
-        owner_kernel,
-        "owner",
-        [(D * G2_ROWS, D)],
-        [HERE],
-        (got,),
+        [pltpu.VMEM((3 * S, 3 * S), F32)],
     )
     small, begun = call(
         alpha_kernel, "alpha", [(2, S, D), (S, 2 * D)], [HERE] * 3, (got, norm, right)
@@ -465,13 +466,14 @@
     sent, keep = call(
         second_kernel,
         "second",
-        [(2, N, SLOT, D), (2, S, 2 * D)],
+        [(2, N * SLOT, D), (2, S, 2 * D)],
         [SCALARS] + [HERE] * 6 + [THERE] * 2,
         (tile_list, mine, other, right, ridge, got, small, *staged),
-        [*STAGED, pltpu.VMEM((3, S, S), F32), sems],
+        [*STAGED, pltpu.VMEM((2, S, S), F32), sems],
         48,
     )
-    got = lax.all_to_all(sent[0] + swap(sent[1]), CHIPS, 0, 0)
+    sent = (sent[0] + swap(sent[1])).reshape(N, 1, SLOT * D)
+    got = lax.all_to_all(sent, CHIPS, 0, 0).reshape(N * SLOT, D)
     return tuple(
         call(
             last_kernel,
@@ -479,7 +481,7 @@
             [(S, 2 * D)] * 2,
             [HERE] * 7,
             (got, right, ridge, keep, norm, small, begun),
-            [pltpu.VMEM((6, S, D), F32)],
+            [pltpu.VMEM((4, S, D), F32)],
         )
     )
 

time: 133 us -> 130 us (0.977)
  blocking collectives: 25.2 us -> 42.1 us
  waiting for transfers between devices: 29 us -> 16.8 us
  starting transfers between devices: 23.4 us -> 19.5 us
  Pallas kernels: 50.9 us -> 47.1 us
    all_to_all x1 -> x2, blocking collectives: 25.2 us -> 42.1 us  [the longest x1 23.8 us: local(): got = lax.all_to_all(sent, CHIPS, 0, 0).reshape(N * SLOT, D)]
    all_to_all x2 -> x1, waiting for transfers between devices: 19.4 us -> 7.38 us  [exchange_rows(): lax.all_to_all(x.reshape(D, 1, rows * D), OWNERS, 0, 0).reshape(D * rows, D)]
    pallas_call x6, Pallas kernels: 38 us -> 34.2 us  [call(): pl.pallas_call(kernel, out_shape=[jax.ShapeDtypeStruct(shape, F32) for sh...]
    all_to_all x2 -> x1, starting transfers between devices: 8.18 us -> 4.35 us  [exchange_rows(): lax.all_to_all(x.reshape(D, 1, rows * D), OWNERS, 0, 0).reshape(D * rows, D)]
  transfers between devices with their start and end apart: 5 -> 4, of which waited for: 5 -> 4; matrix products, arithmetic and copies ran while one was open for 0% -> 0% of each run, Pallas kernels for 17% -> 15%
where the time goes in v6:
time: 130 us; the launch traced here: 129 us
  Pallas kernels  47.1 us (36%)
  blocking collectives  42.1 us (32%)
  starting transfers between devices  19.5 us (15%)
  waiting for transfers between devices  16.8 us (13%)
  local copies, waits for them, and re-layouts  2.74 us (2%)
    pallas_call x6, Pallas kernels, call(): pl.pallas_call(kernel, out_shape=[jax.ShapeDtypeStruct(shape, F32) for sh...  34.2 us
    all_to_all x1, blocking collectives, local(): got = lax.all_to_all(sent, CHIPS, 0, 0).reshape(N * SLOT, D)  23.8 us
    all_to_all x1, blocking collectives, exchange_rows(): lax.all_to_all(x.reshape(D, 1, rows * D), OWNERS, 0, 0).reshape(D * rows, D)  18.3 us
    pallas_call x1, Pallas kernels, stage(): pl.pallas_call(stage_kernel, out_shape=[pltpu.HBM((4, B, B), BF16)] * 2,...  13 us
    all_to_all x1, starting transfers between devices, local(): mine = lax.all_to_all(packed, CHIPS, 0, 0)  12.1 us
    all_to_all x1, waiting for transfers between devices, exchange_rows(): lax.all_to_all(x.reshape(D, 1, rows * D), OWNERS, 0, 0).reshape(D * rows, D)  7.38 us
    ppermute x2, waiting for transfers between devices, swap(): return lax.ppermute(x, 'core', [(0, 1), (1, 0)])  4.76 us
    all_to_all x1, waiting for transfers between devices, local(): mine = lax.all_to_all(packed, CHIPS, 0, 0)  4.65 us
  transfers between devices with their start and end apart: 4, of which 4 were waited for; matrix products, arithmetic and copies ran while one was open for 0% of the time, Pallas kernels for 15%

profile of v6, /device:TPU:1, one launch (start us, length us, event | category | flops | bytes accessed | tf_op | source)
XLA Modules:
  0.0 129.1 jit_solution(8288808171409431194)
XLA Ops:
  0.6 1.8 %broadcast_in_dim.3 = f32[64,16,256]{2,1,0:T(8,128)} broadcast(f32[16,256]{1,0:T(8,128)} %right_ref.7), dimensions={1,2} | broadcast | bytes 1064960 | tf_op jit(solution)/shard_map/broadcast_in_dim | solution.py:429
  2.5 0.0 copy-start.2
  2.5 12.1 %all-to-all-start = ((f32[64,16,256]{2,1,0:T(8,128)}), f32[64,16,256]{2,1,0:T(8,128)S(1)}, u32[]{:S(2)}, u32[]{:S(2)}) async-start(f32[64,16,256]{2,1,0:T(8,128)} %broadcast_in_dim.3), calls=%async_computation | async-start | bytes 2097152 | tf_op jit(solution)/shard_map/all_to_all | solution.py:432
  14.6 0.0 copy-done.2
  14.6 0.0 copy-start.1
  14.6 0.0 copy-start.3
  14.6 13.0 %stage.1 = (bf16[4,1024,1024]{2,1,0:T(8,128)(2,1)}, bf16[4,1024,1024]{2,1,0:T(8,128)(2,1)}) custom-call(s32[2,4]{1,0:T(2,128)S(1)} %bitcast.18, f32[4,1024,1024]{2,1,0:T(8,128)} %tiles_ref.1), custom_call_target="tpu_custom_call" | custom-call | tf_op jit(solution)/shard_map/stage/pallas_call | solution.py:167
  27.6 4.6 %all-to-all-done.mine_ref = f32[64,16,256]{2,1,0:T(8,128)S(1)} async-done(((f32[64,16,256]{2,1,0:T(8,128)}), f32[64,16,256]{2,1,0:T(8,128)S(1)}, u32[]{:S(2)}, u32[]{:S(2)}) %all-to-all-start) | async-done | bytes 1048608 | tf_op jit(solution)/shard_map/all_to_all | solution.py:432
  32.2 2.2 %collective-permute-start = (f32[64,16,256]{2,1,0:T(8,128)S(1)}, f32[64,16,256]{2,1,0:T(8,128)S(1)}, u32[]{:S(2)}, u32[]{:S(2)}) collective-permute-start(f32[64,16,256]{2,1,0:T(8,128)S(1)} %all-to-all-done.mine_ref), channel_id=1, source_target_pairs={{0,1},{1,0},{2,3},{3,2},{4,5},{5,4},{6,7},{7,6},{8,9},{9,8},{10,11... | collective-permute-start | bytes 3145736 | tf_op jit(solution)/shard_map/ppermute | solution.py:423
  34.4 2.3 %collective-permute-done.other_ref = f32[64,16,256]{2,1,0:T(8,128)S(1)} collective-permute-done((f32[64,16,256]{2,1,0:T(8,128)S(1)}, f32[64,16,256]{2,1,0:T(8,128)S(1)}, u32[]{:S(2)}, u32[]{:S(2)}) %collective-permute-start) | collective-permute-done | bytes 1048608 | tf_op jit(solution)/shard_map/ppermute | solution.py:423
  36.7 0.0 copy-done.1
  36.7 0.0 copy-done.3
  36.7 11.8 %first.1 = f32[1280,128]{1,0:T(8,128)S(1)} custom-call(s32[2,4]{1,0:T(2,128)S(1)} %bitcast.19, f32[64,16,256]{2,1,0:T(8,128)S(1)} %all-to-all-done.mine_ref, f32[64,16,256]{2,1,0:T(8,128)S(1)} %collective-permute-done.other_ref, f32[16,256]{1,0:T(8,128)S(1)} %copy-done.1, f32[2,128]{1,0:T(2,128)S(1)} %bitcast.21, ...), custom_call_target="tpu_custom_call" | custom-call | tf_op jit(solution)/shard_map/first/pallas_call | solution.py:407
  48.5 18.3 %all_to_all.20 = f32[128,1,1280]{2,1,0:T(1,128)S(1)} all-to-all(f32[128,1,1280]{2,1,0:T(1,128)S(1)} %bitcast.15), channel_id=1, replica_groups=mesh['grp'=4,'ring'=16,'core'=2] {'core','grp','ring'}, dimensions={0} | all-to-all | bytes 1310720 | tf_op jit(solution)/shard_map/all_to_all | solution.py:419
  66.7 0.9 owner.1
  67.6 0.0 copy-start
  67.6 0.8 copy-done
  68.5 4.4 %all-to-all-start.2 = ((f32[128,1,1152]{2,1,0:T(1,128)}), f32[128,1,1152]{2,1,0:T(1,128)S(1)}, u32[]{:S(2)}, u32[]{:S(2)}) async-start(f32[128,1,1152]{2,1,0:T(1,128)} %bitcast.17), calls=%async_computation.2 | async-start | bytes 1179648 | tf_op jit(solution)/shard_map/all_to_all | solution.py:419
  72.8 4.8 %norm.1.norm_ref = f32[2,16,128]{2,1,0:T(8,128)S(1)} custom-call(f32[64,16,256]{2,1,0:T(8,128)S(1)} %all-to-all-done.mine_ref, f32[64,16,256]{2,1,0:T(8,128)S(1)} %collective-permute-done.other_ref), custom_call_target="tpu_custom_call" | custom-call | tf_op jit(solution)/shard_map/norm/pallas_call | solution.py:407
  77.6 2.1 %alpha.1 = (f32[2,16,128]{2,1,0:T(8,128)S(1)}, f32[16,256]{1,0:T(8,128)S(1)}) custom-call(f32[1280,128]{1,0:T(8,128)S(1)} %bitcast.13, f32[2,16,128]{2,1,0:T(8,128)S(1)} %norm.1.norm_ref, f32[16,256]{1,0:T(8,128)S(1)} %copy-done.1), custom_call_target="tpu_custom_call" | custom-call | tf_op jit(solution)/shard_map/alpha/pallas_call | solution.py:407
  79.7 7.4 %all-to-all-done.2 = f32[128,1,1152]{2,1,0:T(1,128)S(1)} async-done(((f32[128,1,1152]{2,1,0:T(1,128)}), f32[128,1,1152]{2,1,0:T(1,128)S(1)}, u32[]{:S(2)}, u32[]{:S(2)}) %all-to-all-start.2) | async-done | bytes 589856 | tf_op jit(solution)/shard_map/all_to_all | solution.py:419
  87.0 11.5 %second.1 = (f32[2,2304,128]{2,1,0:T(8,128)S(1)}, f32[2,16,256]{2,1,0:T(8,128)S(1)}) custom-call(s32[2,4]{1,0:T(2,128)S(1)} %bitcast.20, f32[64,16,256]{2,1,0:T(8,128)S(1)} %all-to-all-done.mine_ref, f32[64,16,256]{2,1,0:T(8,128)S(1)} %collective-permute-done.other_ref, f32[16,256]{1,0:T(8,128)S(1)} %copy-done.1, f32[2,128]{1,0:T(2,128)S(1)} %bitcast.22, ...), custom_call_target="tpu_custom_call" | custom-call | tf_op jit(solution)/shard_map/second/pallas_call | solution.py:407
  98.5 0.1 slice_bitcast_fusion
  98.6 0.9 collective-permute-start.1
  99.5 2.5 %collective-permute-done.1 = f32[2304,128]{1,0:T(8,128)S(1)} collective-permute-done((f32[2304,128]{1,0:T(8,128)S(1)}, f32[2304,128]{1,0:T(8,128)S(1)}, u32[]{:S(2)}, u32[]{:S(2)}) %collective-permute-start.1) | collective-permute-done | bytes 1179680 | tf_op jit(solution)/shard_map/ppermute | solution.py:423
  102.0 0.1 bitcast_add_fusion
  102.1 23.8 %all_to_all.21 = f32[64,1,4608]{2,1,0:T(1,128)S(1)} all-to-all(f32[64,1,4608]{2,1,0:T(1,128)S(1)} %bitcast.24), channel_id=1, replica_groups=mesh['grp'=4,'ring'=16,'core'=2] {'grp','ring'}, dimensions={0} | all-to-all | bytes 2359296 | tf_op jit(solution)/shard_map/all_to_all | solution.py:476
  125.9 3.2 %last.1 = (f32[16,256]{1,0:T(8,128)}, f32[16,256]{1,0:T(8,128)}) custom-call(f32[2304,128]{1,0:T(8,128)S(1)} %bitcast.14, f32[16,256]{1,0:T(8,128)S(1)} %copy-done.1, f32[2,128]{1,0:T(2,128)S(1)} %bitcast.23, f32[2,16,256]{2,1,0:T(8,128)S(1)} %get-tuple-element.26.keep_ref, f32[2,16,128]{2,1,0:T(8,128)S(1)} %norm.1.norm_ref, ...), custom_call_target="tpu_custom_call" | custom-call | tf_op jit(solution)/shard_map/last/pallas_call | solution.py:407
Async XLA Ops:
  2.5 12.1 %copy-start.2 = (s32[4,2]{0,1:T(2,128)S(1)}, s32[4,2]{0,1:T(2,128)}, u32[]{:S(2)}) copy-start(s32[4,2]{0,1:T(2,128)} %param.7) | copy-start | bytes 100
  2.5 29.8 %all-to-all-start = ((f32[64,16,256]{2,1,0:T(8,128)}), f32[64,16,256]{2,1,0:T(8,128)S(1)}, u32[]{:S(2)}, u32[]{:S(2)}) async-start(f32[64,16,256]{2,1,0:T(8,128)} %broadcast_in_dim.3), calls=%async_computation | async-start | bytes 2097152 | tf_op jit(solution)/shard_map/all_to_all | solution.py:432
  14.6 22.1 %copy-start.1 = (f32[16,256]{1,0:T(8,128)S(1)}, f32[16,256]{1,0:T(8,128)}, u32[]{:S(2)}) copy-start(f32[16,256]{1,0:T(8,128)} %right_ref.7) | copy-start | bytes 49156
  14.6 22.1 %copy-start.3 = (f32[256]{0:T(256)S(1)}, f32[256]{0:T(256)}, u32[]{:S(2)}) copy-start(f32[256]{0:T(256)} %param.5) | copy-start | bytes 3076
  32.2 4.5 %collective-permute-start = (f32[64,16,256]{2,1,0:T(8,128)S(1)}, f32[64,16,256]{2,1,0:T(8,128)S(1)}, u32[]{:S(2)}, u32[]{:S(2)}) collective-permute-start(f32[64,16,256]{2,1,0:T(8,128)S(1)} %all-to-all-done.mine_ref), channel_id=1, source_target_pairs={{0,1},{1,0},{2,3},{3,2},{4,5},{5,4},{6,7},{7,6},{8,9},{9,8},{10,11... | collective-permute-start | bytes 3145736 | tf_op jit(solution)/shard_map/ppermute | solution.py:423
  67.6 0.8 copy-start
  68.5 18.6 %all-to-all-start.2 = ((f32[128,1,1152]{2,1,0:T(1,128)}), f32[128,1,1152]{2,1,0:T(1,128)S(1)}, u32[]{:S(2)}, u32[]{:S(2)}) async-start(f32[128,1,1152]{2,1,0:T(1,128)} %bitcast.17), calls=%async_computation.2 | async-start | bytes 1179648 | tf_op jit(solution)/shard_map/all_to_all | solution.py:419
  98.6 3.4 %collective-permute-start.1 = (f32[2304,128]{1,0:T(8,128)S(1)}, f32[2304,128]{1,0:T(8,128)S(1)}, u32[]{:S(2)}, u32[]{:S(2)}) collective-permute-start(f32[2304,128]{1,0:T(8,128)S(1)} %slice_bitcast_fusion), channel_id=1, source_target_pairs={{0,1},{1,0},{2,3},{3,2},{4,5},{5,4},{6,7},{7,6},{8,9},{9,8},{10,11... | collective-permute-start | bytes 3538952 | tf_op jit(solution)/shard_map/ppermute | solution.py:423

commit v7 on v6

--- a/solution.py
+++ b/solution.py
@@ -27,8 +27,8 @@
 BF16 = jnp.bfloat16
 PIECE = 256
 PIECES = B // PIECE
-PARTS = [(0, 0, 256), (0, 256, 256), (0, 512, 512)]
-PARTS += [(tile, first, 512) for tile in range(1, 4) for first in (0, 512)]
+PARTS = [(0, 0, 256), (0, 256, 256), (0, 512, 512), (1, 0, B), (2, 0, B), (3, 0, B)]
+AHEAD = 4
 NT = (((1,), (1,)), ((), ()))
 NN = (((1,), (0,)), ((), ()))
 
@@ -142,10 +142,12 @@
             for which, (here, there) in enumerate(((high, high_ref), (low, low_ref)))
         ]
 
-    for i in range(4 * PIECES):
+    for i in range(AHEAD):
         fetch(i).start()
     for i in range(4 * PIECES):
         fetch(i).wait()
+        if i + AHEAD < 4 * PIECES:
+            fetch(i + AHEAD).start()
         tile, first = i // PIECES, i % PIECES * PIECE
         high[i], low[i] = split(held[i])
 

time: 130 us -> 130 us (level)
  transfers between devices with their start and end apart: 4 -> 4, of which waited for: 4 -> 4; matrix products, arithmetic and copies ran while one was open for 0% -> 0% of each run, Pallas kernels for 15% -> 16%
where the time goes in v7:
time: 130 us; the launch traced here: 129 us
  Pallas kernels  47.2 us (36%)
  blocking collectives  42.6 us (33%)
  starting transfers between devices  19.5 us (15%)
  waiting for transfers between devices  16.3 us (13%)
  local copies, waits for them, and re-layouts  2.74 us (2%)
    pallas_call x6, Pallas kernels, call(): pl.pallas_call(kernel, out_shape=[jax.ShapeDtypeStruct(shape, F32) for sh...  33.7 us
    all_to_all x1, blocking collectives, local(): got = lax.all_to_all(sent, CHIPS, 0, 0).reshape(N * SLOT, D)  23.8 us
    all_to_all x1, blocking collectives, exchange_rows(): lax.all_to_all(x.reshape(D, 1, rows * D), OWNERS, 0, 0).reshape(D * rows, D)  18.8 us
    pallas_call x1, Pallas kernels, stage(): pl.pallas_call(stage_kernel, out_shape=[pltpu.HBM((4, B, B), BF16)] * 2,...  13.5 us
    all_to_all x1, starting transfers between devices, local(): mine = lax.all_to_all(packed, CHIPS, 0, 0)  12.1 us
    all_to_all x1, waiting for transfers between devices, exchange_rows(): lax.all_to_all(x.reshape(D, 1, rows * D), OWNERS, 0, 0).reshape(D * rows, D)  7.38 us
    ppermute x2, waiting for transfers between devices, swap(): return lax.ppermute(x, 'core', [(0, 1), (1, 0)])  4.76 us
    all_to_all x1, starting transfers between devices, exchange_rows(): lax.all_to_all(x.reshape(D, 1, rows * D), OWNERS, 0, 0).reshape(D * rows, D)  4.35 us
  transfers between devices with their start and end apart: 4, of which 4 were waited for; matrix products, arithmetic and copies ran while one was open for 0% of the time, Pallas kernels for 16%

profile of v7, /device:TPU:1, one launch (start us, length us, event | category | flops | bytes accessed | tf_op | source)
XLA Modules:
  0.0 129.2 jit_solution(11517762402680013403)
XLA Ops:
  0.6 1.8 %broadcast_in_dim.3 = f32[64,16,256]{2,1,0:T(8,128)} broadcast(f32[16,256]{1,0:T(8,128)} %right_ref.7), dimensions={1,2} | broadcast | bytes 1064960 | tf_op jit(solution)/shard_map/broadcast_in_dim | solution.py:431
  2.5 0.0 copy-start.2
  2.5 12.1 %all-to-all-start = ((f32[64,16,256]{2,1,0:T(8,128)}), f32[64,16,256]{2,1,0:T(8,128)S(1)}, u32[]{:S(2)}, u32[]{:S(2)}) async-start(f32[64,16,256]{2,1,0:T(8,128)} %broadcast_in_dim.3), calls=%async_computation | async-start | bytes 2097152 | tf_op jit(solution)/shard_map/all_to_all | solution.py:434
  14.6 0.0 copy-done.2
  14.6 0.0 copy-start.1
  14.6 0.0 copy-start.3
  14.6 13.5 %stage.1 = (bf16[4,1024,1024]{2,1,0:T(8,128)(2,1)}, bf16[4,1024,1024]{2,1,0:T(8,128)(2,1)}) custom-call(s32[2,4]{1,0:T(2,128)S(1)} %bitcast.18, f32[4,1024,1024]{2,1,0:T(8,128)} %tiles_ref.1), custom_call_target="tpu_custom_call" | custom-call | tf_op jit(solution)/shard_map/stage/pallas_call | solution.py:169
  28.1 4.2 %all-to-all-done.mine_ref = f32[64,16,256]{2,1,0:T(8,128)S(1)} async-done(((f32[64,16,256]{2,1,0:T(8,128)}), f32[64,16,256]{2,1,0:T(8,128)S(1)}, u32[]{:S(2)}, u32[]{:S(2)}) %all-to-all-start) | async-done | bytes 1048608 | tf_op jit(solution)/shard_map/all_to_all | solution.py:434
  32.2 2.2 %collective-permute-start = (f32[64,16,256]{2,1,0:T(8,128)S(1)}, f32[64,16,256]{2,1,0:T(8,128)S(1)}, u32[]{:S(2)}, u32[]{:S(2)}) collective-permute-start(f32[64,16,256]{2,1,0:T(8,128)S(1)} %all-to-all-done.mine_ref), channel_id=1, source_target_pairs={{0,1},{1,0},{2,3},{3,2},{4,5},{5,4},{6,7},{7,6},{8,9},{9,8},{10,11... | collective-permute-start | bytes 3145736 | tf_op jit(solution)/shard_map/ppermute | solution.py:425
  34.4 2.3 %collective-permute-done.other_ref = f32[64,16,256]{2,1,0:T(8,128)S(1)} collective-permute-done((f32[64,16,256]{2,1,0:T(8,128)S(1)}, f32[64,16,256]{2,1,0:T(8,128)S(1)}, u32[]{:S(2)}, u32[]{:S(2)}) %collective-permute-start) | collective-permute-done | bytes 1048608 | tf_op jit(solution)/shard_map/ppermute | solution.py:425
  36.7 0.0 copy-done.1
  36.7 0.0 copy-done.3
  36.7 11.3 %first.1 = f32[1280,128]{1,0:T(8,128)S(1)} custom-call(s32[2,4]{1,0:T(2,128)S(1)} %bitcast.19, f32[64,16,256]{2,1,0:T(8,128)S(1)} %all-to-all-done.mine_ref, f32[64,16,256]{2,1,0:T(8,128)S(1)} %collective-permute-done.other_ref, f32[16,256]{1,0:T(8,128)S(1)} %copy-done.1, f32[2,128]{1,0:T(2,128)S(1)} %bitcast.21, ...), custom_call_target="tpu_custom_call" | custom-call | tf_op jit(solution)/shard_map/first/pallas_call | solution.py:409
  48.0 18.8 %all_to_all.20 = f32[128,1,1280]{2,1,0:T(1,128)S(1)} all-to-all(f32[128,1,1280]{2,1,0:T(1,128)S(1)} %bitcast.15), channel_id=1, replica_groups=mesh['grp'=4,'ring'=16,'core'=2] {'core','grp','ring'}, dimensions={0} | all-to-all | bytes 1310720 | tf_op jit(solution)/shard_map/all_to_all | solution.py:421
  66.8 0.9 owner.1
  67.7 0.0 copy-start
  67.7 0.8 copy-done
  68.5 4.4 %all-to-all-start.2 = ((f32[128,1,1152]{2,1,0:T(1,128)}), f32[128,1,1152]{2,1,0:T(1,128)S(1)}, u32[]{:S(2)}, u32[]{:S(2)}) async-start(f32[128,1,1152]{2,1,0:T(1,128)} %bitcast.17), calls=%async_computation.2 | async-start | bytes 1179648 | tf_op jit(solution)/shard_map/all_to_all | solution.py:421
  72.9 4.8 %norm.1.norm_ref = f32[2,16,128]{2,1,0:T(8,128)S(1)} custom-call(f32[64,16,256]{2,1,0:T(8,128)S(1)} %all-to-all-done.mine_ref, f32[64,16,256]{2,1,0:T(8,128)S(1)} %collective-permute-done.other_ref), custom_call_target="tpu_custom_call" | custom-call | tf_op jit(solution)/shard_map/norm/pallas_call | solution.py:409
  77.6 2.1 %alpha.1 = (f32[2,16,128]{2,1,0:T(8,128)S(1)}, f32[16,256]{1,0:T(8,128)S(1)}) custom-call(f32[1280,128]{1,0:T(8,128)S(1)} %bitcast.13, f32[2,16,128]{2,1,0:T(8,128)S(1)} %norm.1.norm_ref, f32[16,256]{1,0:T(8,128)S(1)} %copy-done.1), custom_call_target="tpu_custom_call" | custom-call | tf_op jit(solution)/shard_map/alpha/pallas_call | solution.py:409
  79.7 7.4 %all-to-all-done.2 = f32[128,1,1152]{2,1,0:T(1,128)S(1)} async-done(((f32[128,1,1152]{2,1,0:T(1,128)}), f32[128,1,1152]{2,1,0:T(1,128)S(1)}, u32[]{:S(2)}, u32[]{:S(2)}) %all-to-all-start.2) | async-done | bytes 589856 | tf_op jit(solution)/shard_map/all_to_all | solution.py:421
  87.1 11.4 %second.1 = (f32[2,2304,128]{2,1,0:T(8,128)S(1)}, f32[2,16,256]{2,1,0:T(8,128)S(1)}) custom-call(s32[2,4]{1,0:T(2,128)S(1)} %bitcast.20, f32[64,16,256]{2,1,0:T(8,128)S(1)} %all-to-all-done.mine_ref, f32[64,16,256]{2,1,0:T(8,128)S(1)} %collective-permute-done.other_ref, f32[16,256]{1,0:T(8,128)S(1)} %copy-done.1, f32[2,128]{1,0:T(2,128)S(1)} %bitcast.22, ...), custom_call_target="tpu_custom_call" | custom-call | tf_op jit(solution)/shard_map/second/pallas_call | solution.py:409
  98.5 0.1 slice_bitcast_fusion
  98.6 0.9 collective-permute-start.1
  99.5 2.5 %collective-permute-done.1 = f32[2304,128]{1,0:T(8,128)S(1)} collective-permute-done((f32[2304,128]{1,0:T(8,128)S(1)}, f32[2304,128]{1,0:T(8,128)S(1)}, u32[]{:S(2)}, u32[]{:S(2)}) %collective-permute-start.1) | collective-permute-done | bytes 1179680 | tf_op jit(solution)/shard_map/ppermute | solution.py:425
  102.0 0.1 bitcast_add_fusion
  102.1 23.8 %all_to_all.21 = f32[64,1,4608]{2,1,0:T(1,128)S(1)} all-to-all(f32[64,1,4608]{2,1,0:T(1,128)S(1)} %bitcast.24), channel_id=1, replica_groups=mesh['grp'=4,'ring'=16,'core'=2] {'grp','ring'}, dimensions={0} | all-to-all | bytes 2359296 | tf_op jit(solution)/shard_map/all_to_all | solution.py:478
  125.9 3.2 %last.1 = (f32[16,256]{1,0:T(8,128)}, f32[16,256]{1,0:T(8,128)}) custom-call(f32[2304,128]{1,0:T(8,128)S(1)} %bitcast.14, f32[16,256]{1,0:T(8,128)S(1)} %copy-done.1, f32[2,128]{1,0:T(2,128)S(1)} %bitcast.23, f32[2,16,256]{2,1,0:T(8,128)S(1)} %get-tuple-element.26.keep_ref, f32[2,16,128]{2,1,0:T(8,128)S(1)} %norm.1.norm_ref, ...), custom_call_target="tpu_custom_call" | custom-call | tf_op jit(solution)/shard_map/last/pallas_call | solution.py:409
Async XLA Ops:
  2.5 12.1 %copy-start.2 = (s32[4,2]{0,1:T(2,128)S(1)}, s32[4,2]{0,1:T(2,128)}, u32[]{:S(2)}) copy-start(s32[4,2]{0,1:T(2,128)} %param.7) | copy-start | bytes 100
  2.5 29.8 %all-to-all-start = ((f32[64,16,256]{2,1,0:T(8,128)}), f32[64,16,256]{2,1,0:T(8,128)S(1)}, u32[]{:S(2)}, u32[]{:S(2)}) async-start(f32[64,16,256]{2,1,0:T(8,128)} %broadcast_in_dim.3), calls=%async_computation | async-start | bytes 2097152 | tf_op jit(solution)/shard_map/all_to_all | solution.py:434
  14.6 22.1 %copy-start.1 = (f32[16,256]{1,0:T(8,128)S(1)}, f32[16,256]{1,0:T(8,128)}, u32[]{:S(2)}) copy-start(f32[16,256]{1,0:T(8,128)} %right_ref.7) | copy-start | bytes 49156
  14.6 22.1 %copy-start.3 = (f32[256]{0:T(256)S(1)}, f32[256]{0:T(256)}, u32[]{:S(2)}) copy-start(f32[256]{0:T(256)} %param.5) | copy-start | bytes 3076
  32.2 4.5 %collective-permute-start = (f32[64,16,256]{2,1,0:T(8,128)S(1)}, f32[64,16,256]{2,1,0:T(8,128)S(1)}, u32[]{:S(2)}, u32[]{:S(2)}) collective-permute-start(f32[64,16,256]{2,1,0:T(8,128)S(1)} %all-to-all-done.mine_ref), channel_id=1, source_target_pairs={{0,1},{1,0},{2,3},{3,2},{4,5},{5,4},{6,7},{7,6},{8,9},{9,8},{10,11... | collective-permute-start | bytes 3145736 | tf_op jit(solution)/shard_map/ppermute | solution.py:425
  67.7 0.8 copy-start
  68.5 18.6 %all-to-all-start.2 = ((f32[128,1,1152]{2,1,0:T(1,128)}), f32[128,1,1152]{2,1,0:T(1,128)S(1)}, u32[]{:S(2)}, u32[]{:S(2)}) async-start(f32[128,1,1152]{2,1,0:T(1,128)} %bitcast.17), calls=%async_computation.2 | async-start | bytes 1179648 | tf_op jit(solution)/shard_map/all_to_all | solution.py:421
  98.6 3.4 %collective-permute-start.1 = (f32[2304,128]{1,0:T(8,128)S(1)}, f32[2304,128]{1,0:T(8,128)S(1)}, u32[]{:S(2)}, u32[]{:S(2)}) collective-permute-start(f32[2304,128]{1,0:T(8,128)S(1)} %slice_bitcast_fusion), channel_id=1, source_target_pairs={{0,1},{1,0},{2,3},{3,2},{4,5},{5,4},{6,7},{7,6},{8,9},{9,8},{10,11... | collective-permute-start | bytes 3538952 | tf_op jit(solution)/shard_map/ppermute | solution.py:425

commit v8 on v6

--- a/solution.py
+++ b/solution.py
@@ -27,8 +27,7 @@
 BF16 = jnp.bfloat16
 PIECE = 256
 PIECES = B // PIECE
-PARTS = [(0, 0, 256), (0, 256, 256), (0, 512, 512)]
-PARTS += [(tile, first, 512) for tile in range(1, 4) for first in (0, 512)]
+PARTS = [(0, 0, 256), (0, 256, 256), (0, 512, 512), (1, 0, B), (2, 0, B), (3, 0, B)]
 NT = (((1,), (1,)), ((), ()))
 NN = (((1,), (0,)), ((), ()))
 
@@ -204,18 +203,41 @@
             for which, (there, here) in enumerate(((high_hbm, high_ref), (low_hbm, low_ref)))
         ]
 
-    for i in range(len(PARTS)):
+    for i in range(1, len(PARTS)):
         for copy in fetch(i):
             copy.start()
     return fetch
 
 
-def multiply(fetch, high_ref, low_ref, field, put):
-    def product(vec, tile, part, dims):
+def head_kernel(high_hbm, low_hbm, high_ref, low_ref, sems):
+    part = (0, pl.ds(0, PARTS[0][2]))
+    copies = [
+        pltpu.make_async_copy(there.at[part], here, sems.at[which])
+        for which, (there, here) in enumerate(((high_hbm, high_ref), (low_hbm, low_ref)))
+    ]
+    for copy in copies:
+        copy.start()
+    for copy in copies:
+        copy.wait()
+
+
+def head(staged):
+    return pl.pallas_call(
+        head_kernel,
+        out_shape=[pltpu.VMEM((PARTS[0][2], B), BF16)] * 2,
+        in_specs=[pl.BlockSpec(memory_space=pltpu.HBM)] * 2,
+        out_specs=[pl.BlockSpec(memory_space=pltpu.VMEM)] * 2,
+        scratch_shapes=[pltpu.SemaphoreType.DMA((2,))],
+        name="head",
+    )(*staged)
+
+
+def multiply(fetch, high_ref, low_ref, heads, field, put):
+    def product(vec, high, low, dims):
         vec_high, vec_low = split(vec)
         both = jnp.concatenate([vec_high, vec_low], axis=0)
-        main = lax.dot_general(both, high_ref[tile, part], dims, preferred_element_type=F32)
-        rest = lax.dot_general(vec_high, low_ref[tile, part], dims, preferred_element_type=F32)
+        main = lax.dot_general(both, high[...], dims, preferred_element_type=F32)
+        rest = lax.dot_general(vec_high, low[...], dims, preferred_element_type=F32)
         return main[:S] + (main[S:] + rest)
 
     half = jnp.zeros((S, S), F32)
@@ -225,11 +247,13 @@
         for i, (owner, first, rows) in enumerate(PARTS):
             if owner != tile:
                 continue
-            for copy in fetch(i):
-                copy.wait()
+            if i > 0:
+                for copy in fetch(i):
+                    copy.wait()
             at = slice(first, first + rows)
-            into_row.append(product(from_col, tile, at, NT))
-            into_col.append(product(from_row[:, at], tile, at, NN))
+            parts = (high_ref.at[tile, at], low_ref.at[tile, at]) if i > 0 else heads
+            into_row.append(product(from_col, *parts, NT))
+            into_col.append(product(from_row[:, at], *parts, NN))
         into_row = jnp.concatenate(into_row, axis=1)
         put(2 * tile, into_row)
         put(2 * tile + 1, sum(into_col[1:], into_col[0]))
@@ -238,8 +262,8 @@
 
 
 def first_kernel(
-    list_ref, mine_ref, other_ref, right_ref, ridge_ref, high_hbm, low_hbm, out_ref,
-    high_ref, low_ref, gram_ref, own_ref, sems,
+    list_ref, mine_ref, other_ref, right_ref, ridge_ref, head_high, head_low, high_hbm, low_hbm,
+    out_ref, high_ref, low_ref, gram_ref, own_ref, sems,
 ):
     fetch = fetch_parts(high_hbm, low_hbm, high_ref, low_ref, sems)
 
@@ -259,7 +283,7 @@
         ends = jnp.where(slot == k, list_ref[k % 2, k // 2].astype(F32), ends)
     own = [scaled[:, :D], scaled[:, D:], ends, jnp.zeros((D - 2 * S - ENDS, D), F32)]
     own_ref[...] = jnp.concatenate(own, axis=0).T
-    curvature = multiply(fetch, high_ref, low_ref, field, put)
+    curvature = multiply(fetch, high_ref, low_ref, (head_high, head_low), field, put)
     row, rest = pack_symmetric(widen(gram_ref[...] + curvature))
     out_ref[pl.ds(ENDS, D, stride=R1_ROWS), :] = jnp.broadcast_to(row, (D, D))
     rest = jnp.concatenate([jnp.zeros((1, REST), F32), rest[:, : D - REST]], axis=1)
@@ -331,8 +355,8 @@
 
 
 def second_kernel(
-    list_ref, mine_ref, other_ref, right_ref, ridge_ref, got_ref, small_ref, high_hbm, low_hbm,
-    out_ref, keep_ref, high_ref, low_ref, gram_ref, sems,
+    list_ref, mine_ref, other_ref, right_ref, ridge_ref, got_ref, small_ref, head_high, head_low,
+    high_hbm, low_hbm, out_ref, keep_ref, high_ref, low_ref, gram_ref, sems,
 ):
     fetch = fetch_parts(high_hbm, low_hbm, high_ref, low_ref, sems)
     alpha_t = small_t(small_ref[1])[:, :S]
@@ -363,7 +387,7 @@
     keep_ref[1] = image
     gram_ref[0] = gram(residual, residual)
     gram_ref[1] = gram(residual, ridge * residual)
-    gram_ref[1] += multiply(fetch, high_ref, low_ref, field, put)
+    gram_ref[1] += multiply(fetch, high_ref, low_ref, (head_high, head_low), field, put)
     flat = jnp.concatenate([flat_rows(widen(gram_ref[i])) for i in range(2)], axis=0)
     for side in range(2):
         for chip in range(N):
@@ -431,14 +455,16 @@
     staged = stage(tiles, later_list)
     mine = lax.all_to_all(packed, CHIPS, 0, 0)
     mine, *staged = lax.optimization_barrier((mine, *staged))
+    heads = head(staged)
     other = swap(mine)
+    other, *heads = lax.optimization_barrier((other, *heads))
     sems = pltpu.SemaphoreType.DMA((2, len(PARTS)))
     (sent,) = call(
         first_kernel,
         "first",
         [(D * R1_ROWS, D)],
-        [SCALARS] + [HERE] * 4 + [THERE] * 2,
-        (tile_list, mine, other, right, ridge, *staged),
+        [SCALARS] + [HERE] * 6 + [THERE] * 2,
+        (tile_list, mine, other, right, ridge, *heads, *staged),
         [*STAGED, pltpu.VMEM((S, S), F32), pltpu.VMEM((D, D), F32), sems],
         48,
     )
@@ -462,13 +488,16 @@
     small, begun = call(
         alpha_kernel, "alpha", [(2, S, D), (S, 2 * D)], [HERE] * 3, (got, norm, right)
     )
+    later_high, small = lax.optimization_barrier((staged[0], small))
+    heads = head((later_high, staged[1]))
     got = exchange_rows(sent, G2_ROWS)
+    got, *heads = lax.optimization_barrier((got, *heads))
     sent, keep = call(
         second_kernel,
         "second",
         [(2, N * SLOT, D), (2, S, 2 * D)],
-        [SCALARS] + [HERE] * 6 + [THERE] * 2,
-        (tile_list, mine, other, right, ridge, got, small, *staged),
+        [SCALARS] + [HERE] * 8 + [THERE] * 2,
+        (tile_list, mine, other, right, ridge, got, small, *heads, *staged),
         [*STAGED, pltpu.VMEM((2, S, S), F32), sems],
         48,
     )

time: 130 us -> 130 us (level)
  Pallas kernels: 47.1 us -> 49.9 us
  waiting for transfers between devices: 16.8 us -> 14.2 us
    pallas_call x0 -> x2, Pallas kernels: none -> 2.46 us  [head(): pl.pallas_call(head_kernel, out_shape=[pltpu.VMEM((PARTS[0][2], B), BF16)...]
    all_to_all x1, waiting for transfers between devices: 7.38 us -> 5.92 us  [exchange_rows(): lax.all_to_all(x.reshape(D, 1, rows * D), OWNERS, 0, 0).reshape(D * rows, D)]
  transfers between devices with their start and end apart: 4 -> 4, of which waited for: 4 -> 4; matrix products, arithmetic and copies ran while one was open for 0% -> 0% of each run, Pallas kernels for 15% -> 17%
where the time goes in v8:
time: 130 us; the launch traced here: 129 us
  Pallas kernels  49.9 us (38%)
  blocking collectives  42.1 us (32%)
  starting transfers between devices  20.5 us (16%)
  waiting for transfers between devices  14.2 us (11%)
  local copies, waits for them, and re-layouts  1.91 us (1%)
    pallas_call x6, Pallas kernels, call(): pl.pallas_call(kernel, out_shape=[jax.ShapeDtypeStruct(shape, F32) for sh...  34.6 us
    all_to_all x1, blocking collectives, local(): got = lax.all_to_all(sent, CHIPS, 0, 0).reshape(N * SLOT, D)  23.8 us
    all_to_all x1, blocking collectives, exchange_rows(): lax.all_to_all(x.reshape(D, 1, rows * D), OWNERS, 0, 0).reshape(D * rows, D)  18.3 us
    pallas_call x1, Pallas kernels, stage(): pl.pallas_call(stage_kernel, out_shape=[pltpu.HBM((4, B, B), BF16)] * 2,...  12.9 us
    all_to_all x1, starting transfers between devices, local(): mine = lax.all_to_all(packed, CHIPS, 0, 0)  12.1 us
    all_to_all x1, waiting for transfers between devices, exchange_rows(): lax.all_to_all(x.reshape(D, 1, rows * D), OWNERS, 0, 0).reshape(D * rows, D)  5.92 us
    all_to_all x1, starting transfers between devices, exchange_rows(): lax.all_to_all(x.reshape(D, 1, rows * D), OWNERS, 0, 0).reshape(D * rows, D)  5.27 us
    all_to_all x1, waiting for transfers between devices, local(): mine = lax.all_to_all(packed, CHIPS, 0, 0)  4.72 us
  transfers between devices with their start and end apart: 4, of which 4 were waited for; matrix products, arithmetic and copies ran while one was open for 0% of the time, Pallas kernels for 17%

profile of v8, /device:TPU:1, one launch (start us, length us, event | category | flops | bytes accessed | tf_op | source)
XLA Modules:
  0.0 129.4 jit_solution(10118097790339501914)
XLA Ops:
  0.6 1.8 %broadcast_in_dim.3 = f32[64,16,256]{2,1,0:T(8,128)} broadcast(f32[16,256]{1,0:T(8,128)} %right_ref.7), dimensions={1,2} | broadcast | bytes 1064960 | tf_op jit(solution)/shard_map/broadcast_in_dim | solution.py:453
  2.4 0.0 copy-start.1
  2.5 12.1 %all-to-all-start = ((f32[64,16,256]{2,1,0:T(8,128)}), f32[64,16,256]{2,1,0:T(8,128)S(1)}, u32[]{:S(2)}, u32[]{:S(2)}) async-start(f32[64,16,256]{2,1,0:T(8,128)} %broadcast_in_dim.3), calls=%async_computation | async-start | bytes 2097152 | tf_op jit(solution)/shard_map/all_to_all | solution.py:456
  14.6 0.0 copy-done.1
  14.6 12.9 %stage.1 = (bf16[4,1024,1024]{2,1,0:T(8,128)(2,1)}, bf16[4,1024,1024]{2,1,0:T(8,128)(2,1)}) custom-call(s32[2,4]{1,0:T(2,128)S(1)} %bitcast.16, f32[4,1024,1024]{2,1,0:T(8,128)} %tiles_ref.1), custom_call_target="tpu_custom_call" | custom-call | tf_op jit(solution)/shard_map/stage/pallas_call | solution.py:166
  27.5 4.7 %all-to-all-done.mine_ref = f32[64,16,256]{2,1,0:T(8,128)S(1)} async-done(((f32[64,16,256]{2,1,0:T(8,128)}), f32[64,16,256]{2,1,0:T(8,128)S(1)}, u32[]{:S(2)}, u32[]{:S(2)}) %all-to-all-start) | async-done | bytes 1048608 | tf_op jit(solution)/shard_map/all_to_all | solution.py:456
  32.2 0.0 copy-start
  32.2 0.0 copy-start.2
  32.2 2.2 %collective-permute-start = (f32[64,16,256]{2,1,0:T(8,128)S(1)}, f32[64,16,256]{2,1,0:T(8,128)S(1)}, u32[]{:S(2)}, u32[]{:S(2)}) collective-permute-start(f32[64,16,256]{2,1,0:T(8,128)S(1)} %all-to-all-done.mine_ref), channel_id=1, source_target_pairs={{0,1},{1,0},{2,3},{3,2},{4,5},{5,4},{6,7},{7,6},{8,9},{9,8},{10,11... | collective-permute-start | bytes 3145736 | tf_op jit(solution)/shard_map/ppermute | solution.py:447
  34.4 1.2 head.2
  35.6 1.1 collective-permute-done.other_ref
  36.7 0.0 copy-done
  36.7 0.0 copy-done.2
  36.7 11.2 %first.1 = f32[1280,128]{1,0:T(8,128)S(1)} custom-call(s32[2,4]{1,0:T(2,128)S(1)} %bitcast.17, f32[64,16,256]{2,1,0:T(8,128)S(1)} %all-to-all-done.mine_ref, f32[64,16,256]{2,1,0:T(8,128)S(1)} %collective-permute-done.other_ref, f32[16,256]{1,0:T(8,128)S(1)} %copy-done, f32[2,128]{1,0:T(2,128)S(1)} %bitcast.19, ...), custom_call_target="tpu_custom_call" | custom-call | tf_op jit(solution)/shard_map/first/pallas_call | solution.py:431
  47.9 18.3 %all_to_all.20 = f32[128,1,1280]{2,1,0:T(1,128)S(1)} all-to-all(f32[128,1,1280]{2,1,0:T(1,128)S(1)} %bitcast.15), channel_id=1, replica_groups=mesh['grp'=4,'ring'=16,'core'=2] {'core','grp','ring'}, dimensions={0} | all-to-all | bytes 1310720 | tf_op jit(solution)/shard_map/all_to_all | solution.py:443
  66.2 1.7 %owner.1 = f32[1152,128]{1,0:T(8,128)} custom-call(f32[1280,128]{1,0:T(8,128)S(1)} %bitcast.12), custom_call_target="tpu_custom_call" | custom-call | tf_op jit(solution)/shard_map/owner/pallas_call | solution.py:431
  67.9 5.3 %all-to-all-start.2 = ((f32[128,1,1152]{2,1,0:T(1,128)}), f32[128,1,1152]{2,1,0:T(1,128)}, u32[]{:S(2)}, u32[]{:S(2)}) async-start(f32[128,1,1152]{2,1,0:T(1,128)} %bitcast.4), calls=%async_computation.2 | async-start | bytes 1179648 | tf_op jit(solution)/shard_map/all_to_all | solution.py:443
  73.1 4.8 %norm.1.norm_ref = f32[2,16,128]{2,1,0:T(8,128)S(1)} custom-call(f32[64,16,256]{2,1,0:T(8,128)S(1)} %all-to-all-done.mine_ref, f32[64,16,256]{2,1,0:T(8,128)S(1)} %collective-permute-done.other_ref), custom_call_target="tpu_custom_call" | custom-call | tf_op jit(solution)/shard_map/norm/pallas_call | solution.py:431
  77.9 2.1 %alpha.1 = (f32[2,16,128]{2,1,0:T(8,128)S(1)}, f32[16,256]{1,0:T(8,128)S(1)}) custom-call(f32[1280,128]{1,0:T(8,128)S(1)} %bitcast.13, f32[2,16,128]{2,1,0:T(8,128)S(1)} %norm.1.norm_ref, f32[16,256]{1,0:T(8,128)S(1)} %copy-done), custom_call_target="tpu_custom_call" | custom-call | tf_op jit(solution)/shard_map/alpha/pallas_call | solution.py:431
  80.0 1.2 head.3
  81.2 5.9 %all-to-all-done.2 = f32[128,1,1152]{2,1,0:T(1,128)} async-done(((f32[128,1,1152]{2,1,0:T(1,128)}), f32[128,1,1152]{2,1,0:T(1,128)}, u32[]{:S(2)}, u32[]{:S(2)}) %all-to-all-start.2) | async-done | bytes 589856 | tf_op jit(solution)/shard_map/all_to_all | solution.py:443
  87.1 11.6 %second.1 = (f32[2,2304,128]{2,1,0:T(8,128)S(1)}, f32[2,16,256]{2,1,0:T(8,128)S(1)}) custom-call(s32[2,4]{1,0:T(2,128)S(1)} %bitcast.18, f32[64,16,256]{2,1,0:T(8,128)S(1)} %all-to-all-done.mine_ref, f32[64,16,256]{2,1,0:T(8,128)S(1)} %collective-permute-done.other_ref, f32[16,256]{1,0:T(8,128)S(1)} %copy-done, f32[2,128]{1,0:T(2,128)S(1)} %bitcast.20, ...), custom_call_target="tpu_custom_call" | custom-call | tf_op jit(solution)/shard_map/second/pallas_call | solution.py:431
  98.8 0.1 slice_bitcast_fusion
  98.8 0.9 collective-permute-start.1
  99.7 2.5 %collective-permute-done.1 = f32[2304,128]{1,0:T(8,128)S(1)} collective-permute-done((f32[2304,128]{1,0:T(8,128)S(1)}, f32[2304,128]{1,0:T(8,128)S(1)}, u32[]{:S(2)}, u32[]{:S(2)}) %collective-permute-start.1) | collective-permute-done | bytes 1179680 | tf_op jit(solution)/shard_map/ppermute | solution.py:447
  102.2 0.1 bitcast_add_fusion
  102.3 23.8 %all_to_all.21 = f32[64,1,4608]{2,1,0:T(1,128)S(1)} all-to-all(f32[64,1,4608]{2,1,0:T(1,128)S(1)} %bitcast.22), channel_id=1, replica_groups=mesh['grp'=4,'ring'=16,'core'=2] {'grp','ring'}, dimensions={0} | all-to-all | bytes 2359296 | tf_op jit(solution)/shard_map/all_to_all | solution.py:505
  126.1 3.2 %last.1 = (f32[16,256]{1,0:T(8,128)}, f32[16,256]{1,0:T(8,128)}) custom-call(f32[2304,128]{1,0:T(8,128)S(1)} %bitcast.14, f32[16,256]{1,0:T(8,128)S(1)} %copy-done, f32[2,128]{1,0:T(2,128)S(1)} %bitcast.21, f32[2,16,256]{2,1,0:T(8,128)S(1)} %get-tuple-element.50.keep_ref, f32[2,16,128]{2,1,0:T(8,128)S(1)} %norm.1.norm_ref, ...), custom_call_target="tpu_custom_call" | custom-call | tf_op jit(solution)/shard_map/last/pallas_call | solution.py:431
Async XLA Ops:
  2.4 12.1 %copy-start.1 = (s32[4,2]{0,1:T(2,128)S(1)}, s32[4,2]{0,1:T(2,128)}, u32[]{:S(2)}) copy-start(s32[4,2]{0,1:T(2,128)} %param.7) | copy-start | bytes 100
  2.5 29.8 %all-to-all-start = ((f32[64,16,256]{2,1,0:T(8,128)}), f32[64,16,256]{2,1,0:T(8,128)S(1)}, u32[]{:S(2)}, u32[]{:S(2)}) async-start(f32[64,16,256]{2,1,0:T(8,128)} %broadcast_in_dim.3), calls=%async_computation | async-start | bytes 2097152 | tf_op jit(solution)/shard_map/all_to_all | solution.py:456
  32.2 4.5 %copy-start = (f32[16,256]{1,0:T(8,128)S(1)}, f32[16,256]{1,0:T(8,128)}, u32[]{:S(2)}) copy-start(f32[16,256]{1,0:T(8,128)} %right_ref.7) | copy-start | bytes 49156
  32.2 4.5 %copy-start.2 = (f32[256]{0:T(256)S(1)}, f32[256]{0:T(256)}, u32[]{:S(2)}) copy-start(f32[256]{0:T(256)} %param.5) | copy-start | bytes 3076
  32.2 4.5 %collective-permute-start = (f32[64,16,256]{2,1,0:T(8,128)S(1)}, f32[64,16,256]{2,1,0:T(8,128)S(1)}, u32[]{:S(2)}, u32[]{:S(2)}) collective-permute-start(f32[64,16,256]{2,1,0:T(8,128)S(1)} %all-to-all-done.mine_ref), channel_id=1, source_target_pairs={{0,1},{1,0},{2,3},{3,2},{4,5},{5,4},{6,7},{7,6},{8,9},{9,8},{10,11... | collective-permute-start | bytes 3145736 | tf_op jit(solution)/shard_map/ppermute | solution.py:447
  67.9 19.3 %all-to-all-start.2 = ((f32[128,1,1152]{2,1,0:T(1,128)}), f32[128,1,1152]{2,1,0:T(1,128)}, u32[]{:S(2)}, u32[]{:S(2)}) async-start(f32[128,1,1152]{2,1,0:T(1,128)} %bitcast.4), calls=%async_computation.2 | async-start | bytes 1179648 | tf_op jit(solution)/shard_map/all_to_all | solution.py:443
  98.8 3.4 %collective-permute-start.1 = (f32[2304,128]{1,0:T(8,128)S(1)}, f32[2304,128]{1,0:T(8,128)S(1)}, u32[]{:S(2)}, u32[]{:S(2)}) collective-permute-start(f32[2304,128]{1,0:T(8,128)S(1)} %slice_bitcast_fusion), channel_id=1, source_target_pairs={{0,1},{1,0},{2,3},{3,2},{4,5},{5,4},{6,7},{7,6},{8,9},{9,8},{10,11... | collective-permute-start | bytes 3538952 | tf_op jit(solution)/shard_map/ppermute | solution.py:447

commit v9 on v6

--- a/solution.py
+++ b/solution.py
@@ -27,8 +27,7 @@
 BF16 = jnp.bfloat16
 PIECE = 256
 PIECES = B // PIECE
-PARTS = [(0, 0, 256), (0, 256, 256), (0, 512, 512)]
-PARTS += [(tile, first, 512) for tile in range(1, 4) for first in (0, 512)]
+PARTS = [(0, 0, 256), (0, 256, 256), (0, 512, 512), (1, 0, B), (2, 0, B), (3, 0, B)]
 NT = (((1,), (1,)), ((), ()))
 NN = (((1,), (0,)), ((), ()))
 

time: 130 us -> 130 us (level)
  no operation moved by 1% of the time
where the time goes in v9:
time: 130 us; the launch traced here: 129 us
  Pallas kernels  46.6 us (36%)
  blocking collectives  42.1 us (32%)
  starting transfers between devices  19.5 us (15%)
  waiting for transfers between devices  16.8 us (13%)
  local copies, waits for them, and re-layouts  2.74 us (2%)
    pallas_call x6, Pallas kernels, call(): pl.pallas_call(kernel, out_shape=[jax.ShapeDtypeStruct(shape, F32) for sh...  33.7 us
    all_to_all x1, blocking collectives, local(): got = lax.all_to_all(sent, CHIPS, 0, 0).reshape(N * SLOT, D)  23.8 us
    all_to_all x1, blocking collectives, exchange_rows(): lax.all_to_all(x.reshape(D, 1, rows * D), OWNERS, 0, 0).reshape(D * rows, D)  18.3 us
    pallas_call x1, Pallas kernels, stage(): pl.pallas_call(stage_kernel, out_shape=[pltpu.HBM((4, B, B), BF16)] * 2,...  12.9 us
    all_to_all x1, starting transfers between devices, local(): mine = lax.all_to_all(packed, CHIPS, 0, 0)  12.1 us
    all_to_all x1, waiting for transfers between devices, exchange_rows(): lax.all_to_all(x.reshape(D, 1, rows * D), OWNERS, 0, 0).reshape(D * rows, D)  7.38 us
    ppermute x2, waiting for transfers between devices, swap(): return lax.ppermute(x, 'core', [(0, 1), (1, 0)])  4.76 us
    all_to_all x1, waiting for transfers between devices, local(): mine = lax.all_to_all(packed, CHIPS, 0, 0)  4.68 us
  transfers between devices with their start and end apart: 4, of which 4 were waited for; matrix products, arithmetic and copies ran while one was open for 0% of the time, Pallas kernels for 15%

profile of v9, /device:TPU:1, one launch (start us, length us, event | category | flops | bytes accessed | tf_op | source)
XLA Modules:
  0.0 128.7 jit_solution(1002353305599466531)
XLA Ops:
  0.6 1.8 %broadcast_in_dim.3 = f32[64,16,256]{2,1,0:T(8,128)} broadcast(f32[16,256]{1,0:T(8,128)} %right_ref.7), dimensions={1,2} | broadcast | bytes 1064960 | tf_op jit(solution)/shard_map/broadcast_in_dim | solution.py:428
  2.5 0.0 copy-start.2
  2.5 12.1 %all-to-all-start = ((f32[64,16,256]{2,1,0:T(8,128)}), f32[64,16,256]{2,1,0:T(8,128)S(1)}, u32[]{:S(2)}, u32[]{:S(2)}) async-start(f32[64,16,256]{2,1,0:T(8,128)} %broadcast_in_dim.3), calls=%async_computation | async-start | bytes 2097152 | tf_op jit(solution)/shard_map/all_to_all | solution.py:431
  14.6 0.0 copy-done.2
  14.6 0.0 copy-start.1
  14.6 0.0 copy-start.3
  14.6 12.9 %stage.1 = (bf16[4,1024,1024]{2,1,0:T(8,128)(2,1)}, bf16[4,1024,1024]{2,1,0:T(8,128)(2,1)}) custom-call(s32[2,4]{1,0:T(2,128)S(1)} %bitcast.18, f32[4,1024,1024]{2,1,0:T(8,128)} %tiles_ref.1), custom_call_target="tpu_custom_call" | custom-call | tf_op jit(solution)/shard_map/stage/pallas_call | solution.py:166
  27.5 4.7 %all-to-all-done.mine_ref = f32[64,16,256]{2,1,0:T(8,128)S(1)} async-done(((f32[64,16,256]{2,1,0:T(8,128)}), f32[64,16,256]{2,1,0:T(8,128)S(1)}, u32[]{:S(2)}, u32[]{:S(2)}) %all-to-all-start) | async-done | bytes 1048608 | tf_op jit(solution)/shard_map/all_to_all | solution.py:431
  32.2 2.2 %collective-permute-start = (f32[64,16,256]{2,1,0:T(8,128)S(1)}, f32[64,16,256]{2,1,0:T(8,128)S(1)}, u32[]{:S(2)}, u32[]{:S(2)}) collective-permute-start(f32[64,16,256]{2,1,0:T(8,128)S(1)} %all-to-all-done.mine_ref), channel_id=1, source_target_pairs={{0,1},{1,0},{2,3},{3,2},{4,5},{5,4},{6,7},{7,6},{8,9},{9,8},{10,11... | collective-permute-start | bytes 3145736 | tf_op jit(solution)/shard_map/ppermute | solution.py:422
  34.4 2.3 %collective-permute-done.other_ref = f32[64,16,256]{2,1,0:T(8,128)S(1)} collective-permute-done((f32[64,16,256]{2,1,0:T(8,128)S(1)}, f32[64,16,256]{2,1,0:T(8,128)S(1)}, u32[]{:S(2)}, u32[]{:S(2)}) %collective-permute-start) | collective-permute-done | bytes 1048608 | tf_op jit(solution)/shard_map/ppermute | solution.py:422
  36.7 0.0 copy-done.1
  36.7 0.0 copy-done.3
  36.7 11.3 %first.1 = f32[1280,128]{1,0:T(8,128)S(1)} custom-call(s32[2,4]{1,0:T(2,128)S(1)} %bitcast.19, f32[64,16,256]{2,1,0:T(8,128)S(1)} %all-to-all-done.mine_ref, f32[64,16,256]{2,1,0:T(8,128)S(1)} %collective-permute-done.other_ref, f32[16,256]{1,0:T(8,128)S(1)} %copy-done.1, f32[2,128]{1,0:T(2,128)S(1)} %bitcast.21, ...), custom_call_target="tpu_custom_call" | custom-call | tf_op jit(solution)/shard_map/first/pallas_call | solution.py:406
  48.0 18.3 %all_to_all.20 = f32[128,1,1280]{2,1,0:T(1,128)S(1)} all-to-all(f32[128,1,1280]{2,1,0:T(1,128)S(1)} %bitcast.15), channel_id=1, replica_groups=mesh['grp'=4,'ring'=16,'core'=2] {'core','grp','ring'}, dimensions={0} | all-to-all | bytes 1310720 | tf_op jit(solution)/shard_map/all_to_all | solution.py:418
  66.3 0.9 owner.1
  67.2 0.0 copy-start
  67.2 0.8 copy-done
  68.0 4.4 %all-to-all-start.2 = ((f32[128,1,1152]{2,1,0:T(1,128)}), f32[128,1,1152]{2,1,0:T(1,128)S(1)}, u32[]{:S(2)}, u32[]{:S(2)}) async-start(f32[128,1,1152]{2,1,0:T(1,128)} %bitcast.17), calls=%async_computation.2 | async-start | bytes 1179648 | tf_op jit(solution)/shard_map/all_to_all | solution.py:418
  72.4 4.8 %norm.1.norm_ref = f32[2,16,128]{2,1,0:T(8,128)S(1)} custom-call(f32[64,16,256]{2,1,0:T(8,128)S(1)} %all-to-all-done.mine_ref, f32[64,16,256]{2,1,0:T(8,128)S(1)} %collective-permute-done.other_ref), custom_call_target="tpu_custom_call" | custom-call | tf_op jit(solution)/shard_map/norm/pallas_call | solution.py:406
  77.2 2.1 %alpha.1 = (f32[2,16,128]{2,1,0:T(8,128)S(1)}, f32[16,256]{1,0:T(8,128)S(1)}) custom-call(f32[1280,128]{1,0:T(8,128)S(1)} %bitcast.13, f32[2,16,128]{2,1,0:T(8,128)S(1)} %norm.1.norm_ref, f32[16,256]{1,0:T(8,128)S(1)} %copy-done.1), custom_call_target="tpu_custom_call" | custom-call | tf_op jit(solution)/shard_map/alpha/pallas_call | solution.py:406
  79.2 7.4 %all-to-all-done.2 = f32[128,1,1152]{2,1,0:T(1,128)S(1)} async-done(((f32[128,1,1152]{2,1,0:T(1,128)}), f32[128,1,1152]{2,1,0:T(1,128)S(1)}, u32[]{:S(2)}, u32[]{:S(2)}) %all-to-all-start.2) | async-done | bytes 589856 | tf_op jit(solution)/shard_map/all_to_all | solution.py:418
  86.6 11.4 %second.1 = (f32[2,2304,128]{2,1,0:T(8,128)S(1)}, f32[2,16,256]{2,1,0:T(8,128)S(1)}) custom-call(s32[2,4]{1,0:T(2,128)S(1)} %bitcast.20, f32[64,16,256]{2,1,0:T(8,128)S(1)} %all-to-all-done.mine_ref, f32[64,16,256]{2,1,0:T(8,128)S(1)} %collective-permute-done.other_ref, f32[16,256]{1,0:T(8,128)S(1)} %copy-done.1, f32[2,128]{1,0:T(2,128)S(1)} %bitcast.22, ...), custom_call_target="tpu_custom_call" | custom-call | tf_op jit(solution)/shard_map/second/pallas_call | solution.py:406
  98.1 0.1 slice_bitcast_fusion
  98.1 0.9 collective-permute-start.1
  99.0 2.5 %collective-permute-done.1 = f32[2304,128]{1,0:T(8,128)S(1)} collective-permute-done((f32[2304,128]{1,0:T(8,128)S(1)}, f32[2304,128]{1,0:T(8,128)S(1)}, u32[]{:S(2)}, u32[]{:S(2)}) %collective-permute-start.1) | collective-permute-done | bytes 1179680 | tf_op jit(solution)/shard_map/ppermute | solution.py:422
  101.5 0.1 bitcast_add_fusion
  101.6 23.8 %all_to_all.21 = f32[64,1,4608]{2,1,0:T(1,128)S(1)} all-to-all(f32[64,1,4608]{2,1,0:T(1,128)S(1)} %bitcast.24), channel_id=1, replica_groups=mesh['grp'=4,'ring'=16,'core'=2] {'grp','ring'}, dimensions={0} | all-to-all | bytes 2359296 | tf_op jit(solution)/shard_map/all_to_all | solution.py:475
  125.4 3.2 %last.1 = (f32[16,256]{1,0:T(8,128)}, f32[16,256]{1,0:T(8,128)}) custom-call(f32[2304,128]{1,0:T(8,128)S(1)} %bitcast.14, f32[16,256]{1,0:T(8,128)S(1)} %copy-done.1, f32[2,128]{1,0:T(2,128)S(1)} %bitcast.23, f32[2,16,256]{2,1,0:T(8,128)S(1)} %get-tuple-element.26.keep_ref, f32[2,16,128]{2,1,0:T(8,128)S(1)} %norm.1.norm_ref, ...), custom_call_target="tpu_custom_call" | custom-call | tf_op jit(solution)/shard_map/last/pallas_call | solution.py:406
Async XLA Ops:
  2.5 12.1 %copy-start.2 = (s32[4,2]{0,1:T(2,128)S(1)}, s32[4,2]{0,1:T(2,128)}, u32[]{:S(2)}) copy-start(s32[4,2]{0,1:T(2,128)} %param.7) | copy-start | bytes 100
  2.5 29.8 %all-to-all-start = ((f32[64,16,256]{2,1,0:T(8,128)}), f32[64,16,256]{2,1,0:T(8,128)S(1)}, u32[]{:S(2)}, u32[]{:S(2)}) async-start(f32[64,16,256]{2,1,0:T(8,128)} %broadcast_in_dim.3), calls=%async_computation | async-start | bytes 2097152 | tf_op jit(solution)/shard_map/all_to_all | solution.py:431
  14.6 22.1 %copy-start.1 = (f32[16,256]{1,0:T(8,128)S(1)}, f32[16,256]{1,0:T(8,128)}, u32[]{:S(2)}) copy-start(f32[16,256]{1,0:T(8,128)} %right_ref.7) | copy-start | bytes 49156
  14.6 22.1 %copy-start.3 = (f32[256]{0:T(256)S(1)}, f32[256]{0:T(256)}, u32[]{:S(2)}) copy-start(f32[256]{0:T(256)} %param.5) | copy-start | bytes 3076
  32.2 4.5 %collective-permute-start = (f32[64,16,256]{2,1,0:T(8,128)S(1)}, f32[64,16,256]{2,1,0:T(8,128)S(1)}, u32[]{:S(2)}, u32[]{:S(2)}) collective-permute-start(f32[64,16,256]{2,1,0:T(8,128)S(1)} %all-to-all-done.mine_ref), channel_id=1, source_target_pairs={{0,1},{1,0},{2,3},{3,2},{4,5},{5,4},{6,7},{7,6},{8,9},{9,8},{10,11... | collective-permute-start | bytes 3145736 | tf_op jit(solution)/shard_map/ppermute | solution.py:422
  67.2 0.8 copy-start
  68.0 18.6 %all-to-all-start.2 = ((f32[128,1,1152]{2,1,0:T(1,128)}), f32[128,1,1152]{2,1,0:T(1,128)S(1)}, u32[]{:S(2)}, u32[]{:S(2)}) async-start(f32[128,1,1152]{2,1,0:T(1,128)} %bitcast.17), calls=%async_computation.2 | async-start | bytes 1179648 | tf_op jit(solution)/shard_map/all_to_all | solution.py:418
  98.1 3.4 %collective-permute-start.1 = (f32[2304,128]{1,0:T(8,128)S(1)}, f32[2304,128]{1,0:T(8,128)S(1)}, u32[]{:S(2)}, u32[]{:S(2)}) collective-permute-start(f32[2304,128]{1,0:T(8,128)S(1)} %slice_bitcast_fusion), channel_id=1, source_target_pairs={{0,1},{1,0},{2,3},{3,2},{4,5},{5,4},{6,7},{7,6},{8,9},{9,8},{10,11... | collective-permute-start | bytes 3538952 | tf_op jit(solution)/shard_map/ppermute | solution.py:422
